TPU v7x, 32 devices: a whole 2x2x4 slice. The times are simulated.
32 devices in a mesh: sec: 4 (over x, core), col: 8 (over z, y).
Axes of the slice: x: 2, y: 2, z: 4, core: 2. Of those that a mesh axis runs over, the one named last changes fastest.
Arguments:
- column_state: float32 [2048, 128], P('col'), may hold values from -6 to 6
- mixing_rate: float32 [128], replicated, may hold values from 0.05 to 0.2
- neighbours: int32 [512, 4], P('col'), may hold values from 0 to 511, as said below
- assignment: int32 [2048, 1], P('col'), may hold values from 0 to 23; in each aligned block of 256 rows (0 to 255, 256 to 511, ...) at most 21 rows name the same one
- substeps: int32 [2048], P('col'), may hold values from 1 to 4
- cloud_state: bfloat16 [4, 2, 58, 32, 1344], P('sec', None, None, None, 'col'), may hold values from -6 to 6
- level_map: float32 [58, 64], replicated, may hold values from -0.75 to 0.75
- saturation: float32 [58], replicated, may hold values from -0.5 to 0.5
Outputs:
- new_columns: float32 [2048, 128], P('col')
- new_cloud_state: bfloat16 [4, 2, 58, 32, 1344], P('sec', None, None, None, 'col')
Inputs may be any that keep to these rules, and one draw needn't show every extreme that they name: `neighbours`: each neighbour lies within 64 elements of its own element in the order of elements that wraps around, and some lie exactly 64 away. `assignment`: in each aligned block of 256 columns no cloud device is named by more than 21 columns, and in some block one is named by exactly 21.
All inputs are finite; a program needn't handle non-finite values.
Results may differ from a plain program's by a relative error of at most 0.001.
Values sent between devices are 32-bit elements; how exact they have to be, the bound alone decides.
No kernel may reach another device: no remote copies, remote signals or barrier semaphores. Data moves between devices by JAX's collectives and lax.ppermute only.
A program may use at most 64 MiB of HBM per device.

v0:
```python
import jax
import jax.numpy as jnp
from jax import lax
from jax.sharding import PartitionSpec as P

MAX_SUB = 4


RELAX = 0.25
HORIZ = 0.12
VERTIC = 0.1
LATENT = 2.5
VMIX = 0.2
HIGH = lax.Precision.HIGHEST


def extended_2(cells, sides, width):
    for axis, dim in sides:
        count = lax.axis_size(axis)
        head = lax.slice_in_dim(cells, 0, width, axis=dim)
        tail = lax.slice_in_dim(cells, cells.shape[dim] - width, cells.shape[dim], axis=dim)
        cells = jnp.concatenate(
            [
                lax.ppermute(tail, axis, [(i, (i + 1) % count) for i in range(count)]),
                cells,
                lax.ppermute(head, axis, [((i + 1) % count, i) for i in range(count)]),
            ],
            axis=dim,
        )
    return cells


def vertical_term(values, levels):
    shaped = values.reshape(values.shape[0], -1, levels)
    upper = jnp.concatenate([shaped[:, :, 1:], shaped[:, :, -1:]], axis=2)
    lower = jnp.concatenate([shaped[:, :, :1], shaped[:, :, :-1]], axis=2)
    return (upper + lower - 2.0 * shaped).reshape(values.shape)


def advance(columns, mixing_rate, element_means, near_ids, own_means, levels):
    spread = jnp.sum(element_means[near_ids], axis=1) - 4.0 * own_means
    return (
        columns
        + mixing_rate[None, :] * jnp.repeat(spread, 4, axis=0)
        + VMIX * vertical_term(columns, levels)
    )


def slot_ranks(targets, destinations):
    onehot = (targets[:, None] == jnp.arange(destinations, dtype=jnp.int32)[None, :]).astype(
        jnp.int32
    )
    running = jnp.cumsum(onehot, axis=0) - 1
    return jnp.sum(running * onehot, axis=1)


def cloud_substep(fields, target, saturation):
    mean_now = jnp.mean(fields, axis=2)
    fields = fields + RELAX * (target - mean_now)[:, :, None, :]
    across = jnp.roll(fields, 1, axis=2) + jnp.roll(fields, -1, axis=2) - 2.0 * fields
    upper = jnp.concatenate([fields[:, 1:], fields[:, -1:]], axis=1)
    lower = jnp.concatenate([fields[:, :1], fields[:, :-1]], axis=1)
    fields = fields + HORIZ * across + VERTIC * (upper + lower - 2.0 * fields)
    condensed = 0.5 * jnp.maximum(fields[1] - saturation[:, None, None], 0.0)
    return jnp.stack([fields[0] + LATENT * condensed, fields[1] - condensed])


def run_cloud(block, columns, counts, level_map, saturation, levels):
    shaped = columns.reshape(columns.shape[0], -1, levels)
    target = jnp.einsum("zl,sfl->fzs", level_map, shaped, precision=HIGH)
    start = block.astype(jnp.float32)
    fields = start
    for substep_index in range(MAX_SUB):
        stepped = cloud_substep(fields, target, saturation)
        fields = jnp.where((counts > substep_index)[None, None, None, :], stepped, fields)
    change = jnp.mean(fields, axis=2) - jnp.mean(start, axis=2)
    tendency = jnp.einsum("zl,fzs->sfl", level_map, change, precision=HIGH).reshape(
        columns.shape[0], -1
    )
    return (fields.astype(jnp.bfloat16), tendency)


def body(
    column_state, mixing_rate, neighbours, assignment, substeps, cloud_state, level_map, saturation
):
    col_count = lax.axis_size("col")
    section = lax.axis_index("sec")
    position = lax.axis_index("col")
    host_rows = column_state.shape[0]
    width = column_state.shape[1]
    levels = level_map.shape[1]
    elements = host_rows // 4
    own_means = jnp.mean(column_state.reshape(-1, 4, width), axis=1)
    extended = extended_2(column_state, (("col", 0),), host_rows)
    ext_means = jnp.mean(extended.reshape(-1, 4, width), axis=1)
    near_ids = jnp.mod(neighbours - (position - 1) * elements, elements * col_count)
    advanced = advance(column_state, mixing_rate, ext_means, near_ids, own_means, levels)
    per_device = cloud_state.shape[-1]
    capacity = per_device // col_count
    targets = assignment[:, 0]
    ranks = slot_ranks(targets, (lax.axis_size("sec") - 1) * col_count)
    mine = targets // col_count + 1 == section
    slot_index = jnp.where(mine, targets % col_count * capacity + ranks, per_device)
    outgoing = jnp.zeros((per_device, width), jnp.float32).at[slot_index].set(advanced, mode="drop")
    out_counts = jnp.zeros((per_device,), jnp.int32).at[slot_index].set(substeps, mode="drop")
    incoming, in_counts = (
        lax.all_to_all(outgoing, "col", split_axis=0, concat_axis=0, tiled=True),
        lax.all_to_all(out_counts, "col", split_axis=0, concat_axis=0, tiled=True),
    )
    new_block, tendency = run_cloud(
        cloud_state[0], incoming, in_counts, level_map, saturation, levels
    )
    returned = lax.all_to_all(tendency, "col", split_axis=0, concat_axis=0, tiled=True)
    own_tendency = jnp.where(mine[:, None], returned[jnp.minimum(slot_index, per_device - 1)], 0.0)
    contribution = jnp.where(section == 0, advanced, own_tendency)
    is_water = (jnp.arange(width) // levels == 1)[None, :]
    share = lax.psum_scatter(contribution, "sec", scatter_dimension=0, tiled=True)
    share = jnp.where(is_water, jnp.maximum(share, 0.0), share)
    new_columns = lax.all_gather(share, "sec", axis=0, tiled=True)
    return (new_columns, new_block[None])


def solution(mesh):
    in_specs = (
        P("col", None),
        P(),
        P("col", None),
        P("col", None),
        P("col"),
        P("sec", None, None, None, "col"),
        P(),
        P(),
    )
    out_specs = (P("col", None), P("sec", None, None, None, "col"))
    return jax.shard_map(body, mesh=mesh, in_specs=in_specs, out_specs=out_specs, check_vma=False)
```

profile of v0, /device:TPU:0, one launch (start us, length us, event | category | flops | bytes accessed | tf_op | source)
XLA Modules:
  0.0 125.1 jit_solution(10195750836227592127)
XLA Ops:
  7.2 3.0 %collective-permute-start = (f32[256,128]{1,0:T(8,128)}, f32[256,128]{1,0:T(8,128)S(1)}, u32[]{:S(2)}, u32[]{:S(2)}) collective-permute-start(f32[256,128]{1,0:T(8,128)} %param.8), channel_id=1, source_target_pairs={{0,1},{1,2},{2,3},{3,4},{4,5},{5,6},{6,7},{7,0},{8,9},{9,10},{10,1... | collective-permute-start | bytes 393224 | tf_op jit(solution)/shard_map/ppermute | solution.py:24
  10.3 3.1 %collective-permute-start.1 = (f32[256,128]{1,0:T(8,128)}, f32[256,128]{1,0:T(8,128)S(1)}, u32[]{:S(2)}, u32[]{:S(2)}) collective-permute-start(f32[256,128]{1,0:T(8,128)} %param.8), channel_id=1, source_target_pairs={{1,0},{2,1},{3,2},{4,3},{5,4},{6,5},{7,6},{0,7},{9,8},{10,9},{11,1... | collective-permute-start | bytes 393224 | tf_op jit(solution)/shard_map/ppermute | solution.py:26
  13.4 0.7 compare_reduce_fusion.4
  14.1 0.7 fusion.43
  14.8 0.6 reduce-window.6
  15.3 0.2 slice_reduce_fusion
  15.6 0.8 fusion.42
  16.3 0.7 compare_select_fusion
  17.0 1.6 %scatter_custom_fusion = s32[168]{0:T(256)S(1)} fusion(s32[256]{0:T(256)S(1)} %bitcast.83, s32[256]{0:T(256)} %param.12, s32[]{:T(128)} %constant.104.clone.1), kind=kCustom, calls=%fused_computation.122 | custom fusion | bytes 1184 | tf_op jit(solution)/shard_map/scatter | solution.py:105
  18.6 0.7 all_to_all.20
  19.3 3.3 %all-to-all-start = ((s32[8,21,1]{1,2,0:T(1,128)}), s32[8,21,1]{1,2,0:T(1,128)S(1)}, u32[]{:S(2)}, u32[]{:S(2)}) async-start(s32[8,21,1]{1,2,0:T(1,128)} %bitcast.11), calls=%async_computation | async-start | bytes 8192 | tf_op jit(solution)/shard_map/all_to_all | solution.py:108
  22.6 1.0 copy.20
  23.6 0.7 compare_select_fusion.2
  24.7 1.0 reduce_sum.89
  25.7 0.9 pad_maximum_fusion
  26.6 0.2 reduce_sum.87
  26.9 0.7 gather_fusion
  27.8 1.2 scatter_custom_fusion.1
  29.0 0.6 all_to_all.22
  29.6 5.9 %all-to-all-start.1 = ((f32[8,21,128]{2,1,0:T(8,128)}), f32[8,21,128]{2,1,0:T(8,128)S(1)}, u32[]{:S(2)}, u32[]{:S(2)}) async-start(f32[8,21,128]{2,1,0:T(8,128)} %all_to_all.22), calls=%async_computation.1 | async-start | bytes 196608 | tf_op jit(solution)/shard_map/all_to_all | solution.py:107
  35.6 0.7 convert_reduce_fusion
  36.7 6.0 %all-to-all-done.1 = f32[8,21,128]{2,1,0:T(8,128)S(1)} async-done(((f32[8,21,128]{2,1,0:T(8,128)}), f32[8,21,128]{2,1,0:T(8,128)S(1)}, u32[]{:S(2)}, u32[]{:S(2)}) %all-to-all-start.1) | async-done | bytes 86048 | tf_op jit(solution)/shard_map/all_to_all | solution.py:107
  42.9 0.5 subtract_multiply_fusion.3
  43.3 0.6 fusion.1
  44.0 1.6 %fusion.69 = (f32[2,58,31,168]{3,2,1,0:T(8,128)S(1)}, f32[2,58,31,168]{3,2,1,0:T(8,128)S(1)}) fusion(f32[2,58,32,168]{3,2,1,0:T(8,128)S(1)} %fusion.1), kind=kLoop, calls=%fused_computation.141 | loop fusion | bytes 9666048 | tf_op jit(solution)/shard_map/jit(_roll_static)/slice | solution.py:60
  45.5 1.2 fusion.68
  46.7 0.2 fusion.70
  46.9 2.8 %fusion.9 = f32[2,58,32,168]{3,2,1,0:T(8,128)S(1)} fusion(f32[2,58,31,168]{3,2,1,0:T(8,128)S(1)} %get-tuple-element.51, f32[2,58,1,168]{3,2,1,0:T(1,128)S(1)} %get-tuple-element.53, f32[2,58,1,168]{3,2,1,0:T(1,128)S(1)} %get-tuple-element.52, f32[2,58,31,168]{3,2,1,0:T(8,128)S(1)} %get-tuple-element.50, f32[2,1,32,168]{3,2,1,0:T(8,128)S(1)} %get-tuple-element.47, ...), kind=kLoop, calls=%fused_computation.17 | loop fusion | flops 9354240 | bytes 13797504 | tf_op jit(solution)/shard_map/add | solution.py:63
  49.8 0.5 slice_add_fusion.3
  50.3 1.1 fusion.35
  51.4 1.0 broadcast_add_fusion.2
  52.4 1.6 %fusion.65 = (f32[2,58,31,168]{3,2,1,0:T(8,128)S(1)}, f32[2,58,31,168]{3,2,1,0:T(8,128)S(1)}) fusion(f32[2,58,32,168]{3,2,1,0:T(8,128)S(1)} %broadcast_add_fusion.2), kind=kLoop, calls=%fused_computation.137 | loop fusion | bytes 9666048 | tf_op jit(solution)/shard_map/jit(_roll_static)/slice | solution.py:60
  54.0 1.2 fusion.64
  55.2 0.2 fusion.66
  55.4 3.7 %fusion.15 = f32[2,58,32,168]{3,2,1,0:T(8,128)S(1)} fusion(f32[2,58,31,168]{3,2,1,0:T(8,128)S(1)} %get-tuple-element.43, f32[2,58,1,168]{3,2,1,0:T(1,128)S(1)} %get-tuple-element.45, f32[2,58,1,168]{3,2,1,0:T(1,128)S(1)} %get-tuple-element.44, f32[2,58,31,168]{3,2,1,0:T(8,128)S(1)} %get-tuple-element.42, f32[2,1,32,168]{3,2,1,0:T(8,128)S(1)} %get-tuple-element.39, ...), kind=kLoop, calls=%fused_computation.25 | loop fusion | flops 10601472 | bytes 16292136 | tf_op jit(solution)/shard_map/add | solution.py:63
  59.1 0.5 slice_add_fusion.2
  59.6 1.6 %fusion.54 = (f32[2,58,168]{2,1,0:T(8,128)S(1)}, f32[2,58,32,168]{3,2,1,0:T(8,128)S(1)}) fusion(bf16[1,2,58,32,168]{4,3,2,1,0:T(8,128)(2,1)S(1)} %copy-done.1, f32[1,58,32,168]{3,2,1,0:T(8,128)S(1)} %get-tuple-element.21, f32[1,58,32,168]{3,2,1,0:T(8,128)S(1)} %get-tuple-element.20, pred[168]{0:T(512)(128)(4,1)S(1)} %gt.59, ...), kind=kLoop, calls=%fused_computation.126 | loop fusion | flops 3722208 | bytes 8808912 | tf_op jit(solution)/shard_map/reduce_sum | solution.py:58
  61.3 0.5 copy-done.5
  61.8 0.9 broadcast_add_fusion.1
  62.7 1.6 %fusion.61 = (f32[2,58,31,168]{3,2,1,0:T(8,128)S(1)}, f32[2,58,31,168]{3,2,1,0:T(8,128)S(1)}) fusion(f32[2,58,32,168]{3,2,1,0:T(8,128)S(1)} %broadcast_add_fusion.1), kind=kLoop, calls=%fused_computation.133 | loop fusion | bytes 9666048 | tf_op jit(solution)/shard_map/jit(_roll_static)/slice | solution.py:60
  64.3 1.2 fusion.60
  65.5 0.2 fusion.62
  65.7 3.1 %fusion.21 = f32[2,58,32,168]{3,2,1,0:T(8,128)S(1)} fusion(f32[2,58,31,168]{3,2,1,0:T(8,128)S(1)} %get-tuple-element.35, f32[2,58,1,168]{3,2,1,0:T(1,128)S(1)} %get-tuple-element.37, f32[2,58,1,168]{3,2,1,0:T(1,128)S(1)} %get-tuple-element.36, f32[2,58,31,168]{3,2,1,0:T(8,128)S(1)} %get-tuple-element.34, f32[2,1,32,168]{3,2,1,0:T(8,128)S(1)} %get-tuple-element.31, ...), kind=kLoop, calls=%fused_computation.34 | loop fusion | flops 8730624 | bytes 15044736 | tf_op jit(solution)/shard_map/add | solution.py:63
  68.8 0.5 slice_add_fusion.1
  69.3 1.3 %fusion.53 = (f32[2,58,168]{2,1,0:T(8,128)S(1)}, f32[2,58,32,168]{3,2,1,0:T(8,128)S(1)}) fusion(f32[2,58,32,168]{3,2,1,0:T(8,128)S(1)} %get-tuple-element.13, f32[1,58,32,168]{3,2,1,0:T(8,128)S(1)} %get-tuple-element.17, f32[1,58,32,168]{3,2,1,0:T(8,128)S(1)} %get-tuple-element.16, pred[168]{0:T(512)(128)(4,1)S(1)} %gt.54), kind=kLoop, calls=%fused_computation.125 | loop fusion | flops 1851360 | bytes 7561512 | tf_op jit(solution)/shard_map/reduce_sum | solution.py:58
  70.7 0.5 copy-done.7
  71.2 0.9 broadcast_add_fusion
  72.1 1.6 %fusion.57 = (f32[2,58,31,168]{3,2,1,0:T(8,128)S(1)}, f32[2,58,31,168]{3,2,1,0:T(8,128)S(1)}) fusion(f32[2,58,32,168]{3,2,1,0:T(8,128)S(1)} %broadcast_add_fusion), kind=kLoop, calls=%fused_computation.129 | loop fusion | bytes 9666048 | tf_op jit(solution)/shard_map/jit(_roll_static)/slice | solution.py:60
  73.7 1.2 fusion.56
  75.1 3.3 %fusion.27 = f32[2,58,32,168]{3,2,1,0:T(8,128)S(1)} fusion(f32[2,58,31,168]{3,2,1,0:T(8,128)S(1)} %get-tuple-element.27, f32[2,58,1,168]{3,2,1,0:T(1,128)S(1)} %get-tuple-element.29, f32[2,58,1,168]{3,2,1,0:T(1,128)S(1)} %get-tuple-element.28, f32[2,58,31,168]{3,2,1,0:T(8,128)S(1)} %get-tuple-element.26, f32[2,1,32,168]{3,2,1,0:T(8,128)S(1)} %get-tuple-element.23, ...), kind=kLoop, calls=%fused_computation.43 | loop fusion | flops 8730624 | bytes 15044736 | tf_op jit(solution)/shard_map/add | solution.py:63
  78.4 0.5 slice_add_fusion
  78.9 1.3 %fusion.30 = f32[2,58,168]{2,1,0:T(8,128)S(1)} fusion(f32[2,58,32,168]{3,2,1,0:T(8,128)S(1)} %get-tuple-element.11, f32[1,58,32,168]{3,2,1,0:T(8,128)S(1)} %get-tuple-element.15, f32[1,58,32,168]{3,2,1,0:T(8,128)S(1)} %get-tuple-element.14, pred[168]{0:T(512)(128)(4,1)S(1)} %gt.51), kind=kLoop, calls=%fused_computation.48 | loop fusion | flops 1851360 | bytes 5067048 | tf_op jit(solution)/shard_map/reduce_sum | solution.py:76
  80.2 0.5 copy-done.9
  80.7 0.3 convolution_bitcast_fusion
  81.2 0.8 all_to_all.24
  82.0 3.4 %all-to-all-start.2 = ((f32[8,21,128]{2,1,0:T(8,128)}), f32[8,21,128]{2,1,0:T(8,128)S(1)}, u32[]{:S(2)}, u32[]{:S(2)}) async-start(f32[8,21,128]{2,1,0:T(8,128)} %all_to_all.24), calls=%async_computation.2 | async-start | bytes 196608 | tf_op jit(solution)/shard_map/all_to_all | solution.py:113
  85.4 7.0 %all-to-all-done.2 = f32[8,21,128]{2,1,0:T(8,128)S(1)} async-done(((f32[8,21,128]{2,1,0:T(8,128)}), f32[8,21,128]{2,1,0:T(8,128)S(1)}, u32[]{:S(2)}, u32[]{:S(2)}) %all-to-all-start.2) | async-done | bytes 86048 | tf_op jit(solution)/shard_map/all_to_all | solution.py:113
  92.4 0.7 gather_fusion.1
  93.1 0.8 select_select_fusion
  93.9 7.6 %fusion.5 = bf16[1,2,58,32,168]{4,3,2,1,0:T(8,128)(2,1)} fusion(bf16[1,2,58,32,168]{4,3,2,1,0:T(8,128)(2,1)S(1)} %copy-done.1, f32[1,1,58,32,168]{4,3,2,1,0:T(8,128)} %bitcast.71, f32[1,1,58,32,168]{4,3,2,1,0:T(8,128)} %bitcast.70, f32[1,1,58,32,168]{4,3,2,1,0:T(8,128)} %bitcast.69, f32[1,1,58,32,168]{4,3,2,1,0:T(8,128)} %bitcast.68, ...), kind=kLoop, calls=%fused_computation.12 | loop fusion | flops 13095936 | bytes 12472992 | tf_op jit(solution)/shard_map/convert_element_type | solution.py:80
  101.6 9.8 %reduce-scatter.2.cloned.1.call-done = f32[64,128]{1,0:T(8,128)} async-done(((f32[256,128]{1,0:T(8,128)}), f32[64,128]{1,0:T(8,128)}) %reduce-scatter.2.cloned.1.call-update) | async-done | bytes 32784 | tf_op jit(solution)/shard_map/reduce_scatter | solution.py:117
  111.4 0.8 maximum_select_fusion.3
  112.2 5.4 %all_gather.3 = f32[256,128]{1,0:T(8,128)S(1)} all-gather(f32[64,128]{1,0:T(8,128)S(1)} %maximum_select_fusion.3), channel_id=1, replica_groups=mesh['sec'=4,'col'=8] {'sec'}, dimensions={0}, use_global_device_ids=true | all-gather | bytes 163840 | tf_op jit(solution)/shard_map/all_gather | solution.py:119
  117.6 0.7 copy.36
  (61 shorter events, 1.9 us)
Async XLA Ops:
  7.2 35.7 %copy-start = (f32[58,64]{1,0:T(8,128)S(1)}, f32[58,64]{1,0:T(8,128)}, u32[]{:S(2)}) copy-start(f32[58,64]{1,0:T(8,128)} %param.14) | copy-start | bytes 44548
  7.2 20.6 %copy-start.10 = (f32[256,128]{1,0:T(8,128)S(1)}, f32[256,128]{1,0:T(8,128)}, u32[]{:S(2)}) copy-start(f32[256,128]{1,0:T(8,128)} %param.8) | copy-start | bytes 393220
  7.2 20.6 %copy-start.12 = (f32[128]{0:T(128)S(1)}, f32[128]{0:T(128)}, u32[]{:S(2)}) copy-start(f32[128]{0:T(128)} %param.9) | copy-start | bytes 1540
  7.2 28.4 %copy-start.1 = (bf16[1,2,58,32,168]{4,3,2,1,0:T(8,128)(2,1)S(1)}, bf16[1,2,58,32,168]{4,3,2,1,0:T(8,128)(2,1)}, u32[]{:S(2)}) copy-start(bf16[1,2,58,32,168]{4,3,2,1,0:T(8,128)(2,1)} %param.13) | copy-start | bytes 3741700
  7.2 18.5 %collective-permute-start = (f32[256,128]{1,0:T(8,128)}, f32[256,128]{1,0:T(8,128)S(1)}, u32[]{:S(2)}, u32[]{:S(2)}) collective-permute-start(f32[256,128]{1,0:T(8,128)} %param.8), channel_id=1, source_target_pairs={{0,1},{1,2},{2,3},{3,4},{4,5},{5,6},{6,7},{7,0},{8,9},{9,10},{10,1... | collective-permute-start | bytes 393224 | tf_op jit(solution)/shard_map/ppermute | solution.py:24
  10.3 15.4 %collective-permute-start.1 = (f32[256,128]{1,0:T(8,128)}, f32[256,128]{1,0:T(8,128)S(1)}, u32[]{:S(2)}, u32[]{:S(2)}) collective-permute-start(f32[256,128]{1,0:T(8,128)} %param.8), channel_id=1, source_target_pairs={{1,0},{2,1},{3,2},{4,3},{5,4},{6,5},{7,6},{0,7},{9,8},{10,9},{11,1... | collective-permute-start | bytes 393224 | tf_op jit(solution)/shard_map/ppermute | solution.py:26
  19.3 10.4 %all-to-all-start = ((s32[8,21,1]{1,2,0:T(1,128)}), s32[8,21,1]{1,2,0:T(1,128)S(1)}, u32[]{:S(2)}, u32[]{:S(2)}) async-start(s32[8,21,1]{1,2,0:T(1,128)} %bitcast.11), calls=%async_computation | async-start | bytes 8192 | tf_op jit(solution)/shard_map/all_to_all | solution.py:108
  29.6 13.1 %all-to-all-start.1 = ((f32[8,21,128]{2,1,0:T(8,128)}), f32[8,21,128]{2,1,0:T(8,128)S(1)}, u32[]{:S(2)}, u32[]{:S(2)}) async-start(f32[8,21,128]{2,1,0:T(8,128)} %all_to_all.22), calls=%async_computation.1 | async-start | bytes 196608 | tf_op jit(solution)/shard_map/all_to_all | solution.py:107
  46.9 2.9 %copy-start.11 = (f32[58]{0:T(128)S(1)}, f32[58]{0:T(128)}, u32[]{:S(2)}) copy-start(f32[58]{0:T(128)} %param.15) | copy-start | bytes 700
  50.3 9.3 %copy-start.2 = (f32[1,58,32,168]{3,2,1,0:T(8,128)}, f32[1,58,32,168]{3,2,1,0:T(8,128)S(1)}, u32[]{:S(2)}) copy-start(f32[1,58,32,168]{3,2,1,0:T(8,128)S(1)} %get-tuple-element.20) | copy-start | bytes 3741700
  50.3 9.3 %copy-start.3 = (f32[1,58,32,168]{3,2,1,0:T(8,128)}, f32[1,58,32,168]{3,2,1,0:T(8,128)S(1)}, u32[]{:S(2)}) copy-start(f32[1,58,32,168]{3,2,1,0:T(8,128)S(1)} %get-tuple-element.21) | copy-start | bytes 3741700
  59.5 1.7 %copy-start.4 = (f32[1,58,32,168]{3,2,1,0:T(8,128)}, f32[1,58,32,168]{3,2,1,0:T(8,128)S(1)}, u32[]{:S(2)}) copy-start(f32[1,58,32,168]{3,2,1,0:T(8,128)S(1)} %get-tuple-element.18) | copy-start | bytes 3741700
  59.6 2.2 %copy-start.5 = (f32[1,58,32,168]{3,2,1,0:T(8,128)}, f32[1,58,32,168]{3,2,1,0:T(8,128)S(1)}, u32[]{:S(2)}) copy-start(f32[1,58,32,168]{3,2,1,0:T(8,128)S(1)} %get-tuple-element.19) | copy-start | bytes 3741700
  69.2 1.5 %copy-start.6 = (f32[1,58,32,168]{3,2,1,0:T(8,128)}, f32[1,58,32,168]{3,2,1,0:T(8,128)S(1)}, u32[]{:S(2)}) copy-start(f32[1,58,32,168]{3,2,1,0:T(8,128)S(1)} %get-tuple-element.16) | copy-start | bytes 3741700
  69.2 1.9 %copy-start.7 = (f32[1,58,32,168]{3,2,1,0:T(8,128)}, f32[1,58,32,168]{3,2,1,0:T(8,128)S(1)}, u32[]{:S(2)}) copy-start(f32[1,58,32,168]{3,2,1,0:T(8,128)S(1)} %get-tuple-element.17) | copy-start | bytes 3741700
  78.9 1.3 %copy-start.8 = (f32[1,58,32,168]{3,2,1,0:T(8,128)}, f32[1,58,32,168]{3,2,1,0:T(8,128)S(1)}, u32[]{:S(2)}) copy-start(f32[1,58,32,168]{3,2,1,0:T(8,128)S(1)} %get-tuple-element.14) | copy-start | bytes 3741700
  78.9 1.8 %copy-start.9 = (f32[1,58,32,168]{3,2,1,0:T(8,128)}, f32[1,58,32,168]{3,2,1,0:T(8,128)S(1)}, u32[]{:S(2)}) copy-start(f32[1,58,32,168]{3,2,1,0:T(8,128)S(1)} %get-tuple-element.15) | copy-start | bytes 3741700
  82.0 10.4 %all-to-all-start.2 = ((f32[8,21,128]{2,1,0:T(8,128)}), f32[8,21,128]{2,1,0:T(8,128)S(1)}, u32[]{:S(2)}, u32[]{:S(2)}) async-start(f32[8,21,128]{2,1,0:T(8,128)} %all_to_all.24), calls=%async_computation.2 | async-start | bytes 196608 | tf_op jit(solution)/shard_map/all_to_all | solution.py:113
  85.3 26.1 %reduce-scatter.2.cloned.1.call-start = ((), (), s32[]{:S(2)}) async-start(), calls=%async_computation.4 | async-start | bytes 163840 | tf_op jit(solution)/shard_map/reduce_scatter | solution.py:117
Sparse Core Ops, SparseCore 0:
  94.1 17.3 reduce-scatter.1
where the time goes:
time: 126 us; the launch traced here: 125 us
  other arithmetic  40 us (32%)
  waiting for transfers between devices  22.9 us (18%)
  local copies, waits for them, and re-layouts  22.6 us (18%)
  starting transfers between devices  18.8 us (15%)
  between operations  14.7 us (12%)
  blocking collectives  5.4 us (4%)
    add x4, other arithmetic, cloud_substep(): fields = fields + HORIZ * across + VERTIC * (upper + lower - 2.0 * fields)  13 us
    reduce_scatter x1, waiting for transfers between devices, body(): lax.psum_scatter(contribution, 'sec', scatter_dimension=0, tiled=True)  9.85 us
    convert_element_type x1, other arithmetic, run_cloud(): return (fields.astype(jnp.bfloat16), tendency)  7.63 us
    all_to_all x1, waiting for transfers between devices, body(): lax.all_to_all(tendency, 'col', split_axis=0, concat_axis=0, tiled=True)  6.98 us
    slice x8, local copies, waits for them, and re-layouts, cloud_substep(): jnp.roll(fields, -1, axis=2)  6.97 us
    all_to_all x1, waiting for transfers between devices, body(): lax.all_to_all(outgoing, 'col', split_axis=0, concat_axis=0, tiled=True)  6 us
    all_to_all x1, starting transfers between devices, body(): lax.all_to_all(outgoing, 'col', split_axis=0, concat_axis=0, tiled=True)  5.93 us
    all_gather x1, blocking collectives, body(): new_columns = lax.all_gather(share, 'sec', axis=0, tiled=True)  5.4 us
  transfers between devices with their start and end apart: 6, of which 3 were waited for; matrix products, arithmetic and copies ran while one was open for 16% of the time, Pallas kernels for 0%

commit v1 on v0

v1 whole, which is shorter than its diff:
```python
import functools

import jax
import jax.numpy as jnp
from jax import lax
from jax.experimental import pallas as pl
from jax.experimental.pallas import tpu as pltpu
from jax.sharding import PartitionSpec as P

MAX_SUB = 4
RELAX = 0.25
HORIZ = 0.12
VERTIC = 0.1
LATENT = 2.5
VMIX = 0.2
HIGH = lax.Precision.HIGHEST
LANES = 128
F32 = jnp.float32
I32 = jnp.int32


def iota(shape, dim):
    return lax.broadcasted_iota(I32, shape, dim)


def mm(a, b, contract, precision=HIGH):
    return lax.dot_general(
        a, b, (contract, ((), ())), precision=precision, preferred_element_type=F32
    )


NN = ((1,), (0,))
NT = ((1,), (1,))
TN = ((0,), (0,))


def divided(value, by):
    return jnp.floor((value.astype(F32) + 0.5) * (1.0 / by)).astype(I32)


def vertical_mix(values, levels):
    upper = jnp.concatenate([values[1:levels], values[levels - 1 : levels]], axis=0)
    lower = jnp.concatenate([values[0:1], values[0 : levels - 1]], axis=0)
    inner = values[0:levels]
    return inner + VERTIC * (upper + lower - 2.0 * inner)


def means_kernel(columns_ref, means_ref):
    elements = means_ref.shape[0]
    total = columns_ref[pl.ds(0, elements, stride=4), :]
    for k in range(1, 4):
        total = total + columns_ref[pl.ds(k, elements, stride=4), :]
    means_ref[...] = 0.25 * total


def host_kernel(
    where_ref,
    columns_ref,
    means_ref,
    mixing_ref,
    neighbours_ref,
    targets_ref,
    substeps_ref,
    map_ref,
    base_ref,
    sides_ref,
    pack_ref,
    counts_ref,
    slots_ref,
    fold_ref,
    unfold_ref,
    *,
    col_count,
    capacity,
    padded,
    clouds,
):
    section = where_ref[0]
    position = where_ref[1]
    rows, width = columns_ref.shape
    levels = map_ref.shape[1]
    cloud_levels = map_ref.shape[0]
    elements = rows // 4
    block = col_count * padded
    near = neighbours_ref[...] - (position - 1) * elements
    near = jnp.where(near < 0, near + elements * col_count, near)
    near = jnp.where(near >= elements * col_count, near - elements * col_count, near)
    window = iota((3 * elements, elements), 0)
    picks = jnp.where(window == iota((3 * elements, elements), 1) + elements, -4.0, 0.0)
    for k in range(near.shape[0]):
        picks = picks + jnp.where(window == near[k : k + 1, :], 1.0, 0.0)
    row_element = divided(iota((rows, elements), 0), 4)
    spread_rows = jnp.where(row_element == iota((rows, elements), 1), 1.0, 0.0)
    weights = mm(spread_rows, picks, NT)
    sides_ref[:, :elements] = weights[:, :elements]
    sides_ref[:, elements:] = weights[:, 2 * elements :]
    own = mm(weights[:, elements : 2 * elements], means_ref[...], NN)
    values = columns_ref[...]
    lane = iota((rows, width), 1)
    level = lane - levels * divided(lane, levels)
    upper = jnp.where(level == levels - 1, values, pltpu.roll(values, width - 1, 1))
    lower = jnp.where(level == 0, values, pltpu.roll(values, 1, 1))
    base_ref[...] = values + mixing_ref[...] * own + VMIX * (upper + lower - 2.0 * values)
    targets = targets_ref[...]
    onehot = jnp.where(iota((clouds, rows), 0) == targets, 1.0, 0.0)
    before = jnp.where(iota((rows, rows), 0) < iota((rows, rows), 1), 1.0, 0.0)
    running = mm(onehot, before, NN)
    ranks = jnp.sum(running * onehot, axis=0, keepdims=True).astype(I32)
    owner = divided(targets, col_count)
    slot = (targets - owner * col_count) * padded + ranks
    mine = jnp.where(owner + 1 == section, slot, -1)
    pack = jnp.where(iota((block, rows), 0) == mine, 1.0, 0.0)
    pack_ref[...] = pack
    count_rows = jnp.where(
        iota((width, rows), 0) == levels - 1, substeps_ref[...].astype(F32), 0.0
    )
    counts_ref[...] = mm(pack, count_rows, NT)
    everywhere = (owner * block + slot).astype(F32)
    identity = jnp.where(iota((rows, rows), 0) == iota((rows, rows), 1), 1.0, 0.0)
    slots_ref[...] = mm(identity, jnp.broadcast_to(everywhere, (LANES, rows)), NT)
    plain = map_ref[...]
    folded = RELAX * vertical_mix(plain, cloud_levels)
    for ref, value in ((fold_ref, folded), (unfold_ref, plain)):
        ref[...] = jnp.zeros_like(ref)
        for f in range(width // levels):
            ref[f * levels : f * levels + cloud_levels, f * levels : (f + 1) * levels] = value


def pack_kernel(
    base_ref, sides_ref, left_ref, right_ref, mixing_ref, pack_ref, counts_ref, fold_ref,
    advanced_ref, out_ref,
):
    halo = jnp.concatenate([left_ref[...], right_ref[...]], axis=0)
    spread = mm(sides_ref[...], halo, NN)
    advanced = base_ref[...] + mixing_ref[...] * spread
    advanced_ref[...] = advanced
    packed = mm(pack_ref[...], advanced, NN)
    out_ref[...] = mm(packed, fold_ref[...], NT) + counts_ref[...]


def linear(below, here, above):
    east = [pltpu.roll(here[3], 1, 0), here[0], here[1], here[2]]
    west = [here[1], here[2], here[3], pltpu.roll(here[0], 7, 0)]
    keep = 1.0 - 2.0 * HORIZ - 2.0 * VERTIC
    return [
        keep * here[j] + HORIZ * (east[j] + west[j]) + VERTIC * (below[j] + above[j])
        for j in range(4)
    ]


def groups(ref, index):
    return [ref[index + (pl.ds(8 * j, 8),)] for j in range(4)]


def prepare_kernel(state_ref, moved_ref, means_ref, natural_ref, sums_ref):
    fields, levels, columns, slots = state_ref.shape
    tiles = moved_ref.shape[0]
    for tile in range(tiles):
        width = min(LANES, slots - tile * LANES)
        for f in range(fields):

            def widen(z, carry):
                value = state_ref[f, z, :, tile * LANES : tile * LANES + width].astype(F32)
                natural_ref[z, :, :width] = value
                return carry

            lax.fori_loop(0, levels, widen, 0, unroll=2)

            def strided(z):
                return [natural_ref[z, pl.ds(j, 8, stride=4), :] for j in range(4)]

            def level(z, carry):
                below, here = carry
                above = strided(jnp.minimum(z + 1, levels - 1))
                out = linear(below, here, above)
                for j in range(4):
                    moved_ref[tile, f, z, pl.ds(8 * j, 8), :] = out[j]
                sums_ref[pl.ds(pl.multiple_of(z * 8, 8), 8), :] = (here[0] + here[1]) + (here[2] + here[3])
                return here, above

            first = strided(0)
            lax.fori_loop(0, levels, level, (first, first), unroll=2)
            means_ref[tile, f] = folded_sums(sums_ref, columns)


def folded_sums(sums_ref, columns):
    rows = sums_ref.shape[0] // 8
    total = sums_ref[pl.ds(0, rows, stride=8), :]
    for k in range(1, 8):
        total = total + sums_ref[pl.ds(k, rows, stride=8), :]
    return total * (1.0 / columns)


def slot_map(block, slots, capacity, padded):
    slot = iota((block, slots), 1)
    row = slot + (padded - capacity) * divided(slot, capacity)
    return jnp.where(iota((block, slots), 0) == row, 1.0, 0.0)


def water_kernel(
    received_ref,
    moved_ref,
    means_ref,
    saturation_ref,
    unfold_ref,
    water_ref,
    excess_ref,
    offsets_ref,
    counts_ref,
    back_ref,
    target_ref,
    sums_ref,
    change_ref,
    *,
    capacity,
    padded,
    slots,
    stride,
):
    tiles, _, levels, columns, _ = moved_ref.shape
    block = received_ref.shape[0]
    places = slot_map(block, slots, capacity, padded)
    arrived = mm(received_ref[...], places, TN)
    change_ref[...] = jnp.zeros_like(change_ref)
    for tile in range(tiles):
        width = min(LANES, slots - tile * LANES)
        target_ref[...] = jnp.zeros_like(target_ref)
        target_ref[:, :width] = arrived[:, tile * LANES : tile * LANES + width]
        count = target_ref[stride - 1 : stride, :]
        counts_ref[tile] = jnp.broadcast_to(count, (8, LANES))
        goal = [target_ref[f * stride : f * stride + levels, :] for f in range(2)]
        start = [means_ref[tile, f, :levels, :] for f in range(2)]
        mean = list(start)
        for n in range(MAX_SUB):
            mixed = [vertical_mix(mean[f], levels) for f in range(2)]
            offset = [goal[f] - RELAX * mixed[f] for f in range(2)]
            for f in range(2):
                offsets_ref[n, tile, f, :levels, :] = offset[f]
            active = jnp.broadcast_to(count, (8, LANES)) > float(n)

            def finish(z, lin, old):
                shift = jnp.broadcast_to(offsets_ref[n, tile, 1, pl.ds(z, 1), :], (8, LANES))
                limit = jnp.broadcast_to(saturation_ref[pl.ds(z, 1), :], (8, LANES))
                total = None
                for j in range(4):
                    v = lin[j] + shift
                    h = jnp.maximum(v - limit, 0.0)
                    u = v - 0.5 * h
                    if old is not None:
                        u = jnp.where(active, u, old[j])
                    excess_ref[n, tile, z, pl.ds(8 * j, 8), :] = h
                    water_ref[tile, z, pl.ds(8 * j, 8), :] = u
                    total = h if total is None else total + h
                sums_ref[pl.ds(pl.multiple_of(z * 8, 8), 8), :] = total

            if n == 0:

                def level(z, carry):
                    finish(z, groups(moved_ref, (tile, 1, z)), None)
                    return carry

                lax.fori_loop(0, levels, level, 0, unroll=2)
            else:

                def level(z, carry):
                    below, here = carry
                    above = groups(water_ref, (tile, jnp.minimum(z + 1, levels - 1)))
                    finish(z, linear(below, here, above), here)
                    return here, above

                first = groups(water_ref, (tile, 0))
                lax.fori_loop(0, levels, level, (first, first), unroll=2)
            spilled = folded_sums(sums_ref, columns)[:levels]
            step = [
                mixed[0] + offset[0] + (0.5 * LATENT) * spilled,
                mixed[1] + offset[1] - 0.5 * spilled,
            ]
            keep = count > float(n)
            mean = [jnp.where(keep, step[f], mean[f]) for f in range(2)]
        for f in range(2):
            change_ref[f * stride : f * stride + levels, tile * LANES : tile * LANES + width] = (
                mean[f] - start[f]
            )[:, :width]
    spread = mm(places, change_ref[...], NT)
    back_ref[...] = mm(spread, unfold_ref[...], NN)


def energy_kernel(
    state_ref, moved_ref, water_ref, excess_ref, offsets_ref, counts_ref, out_ref, energy_ref,
    natural_ref,
):
    tiles, _, levels, columns, _ = moved_ref.shape
    slots = state_ref.shape[3]
    for tile in range(tiles):
        width = min(LANES, slots - tile * LANES)
        count = counts_ref[tile]
        for n in range(MAX_SUB):
            active = count > float(n)

            def finish(z, lin, old):
                shift = jnp.broadcast_to(offsets_ref[n, tile, 0, pl.ds(z, 1), :], (8, LANES))
                h = groups(excess_ref, (n, tile, z))
                for j in range(4):
                    u = lin[j] + shift + (0.5 * LATENT) * h[j]
                    if old is not None:
                        u = jnp.where(active, u, old[j])
                    energy_ref[z, pl.ds(8 * j, 8), :] = u

            if n == 0:

                def level(z, carry):
                    finish(z, groups(moved_ref, (tile, 0, z)), None)
                    return carry

                lax.fori_loop(0, levels, level, 0, unroll=2)
            else:

                def level(z, carry):
                    below, here = carry
                    above = groups(energy_ref, (jnp.minimum(z + 1, levels - 1),))
                    finish(z, linear(below, here, above), here)
                    return here, above

                first = groups(energy_ref, (0,))
                lax.fori_loop(0, levels, level, (first, first), unroll=2)
        for f in range(2):

            def permute(z, carry):
                source = groups(energy_ref, (z,)) if f == 0 else groups(water_ref, (tile, z))
                for j in range(4):
                    natural_ref[z, pl.ds(j, 8, stride=4), :] = source[j]
                return carry

            lax.fori_loop(0, levels, permute, 0, unroll=2)
            held = jnp.broadcast_to(count[0:1, :width], (columns, width)) > 0.0

            def narrow(z, carry):
                at = slice(tile * LANES, tile * LANES + width)
                old = state_ref[f, z, :, at].astype(F32)
                value = jnp.where(held, natural_ref[z, :, :width], old)
                out_ref[f, z, :, at] = value.astype(jnp.bfloat16)
                return carry

            lax.fori_loop(0, levels, narrow, 0, unroll=2)


def final_kernel(advanced_ref, slots_ref, gathered_ref, out_ref, *, levels):
    rows, width = advanced_ref.shape
    sections, block, _ = gathered_ref.shape
    summed = advanced_ref[...]
    place = slots_ref[:, :1].astype(I32)
    for s in range(1, sections):
        picks = jnp.where(iota((rows, block), 1) + (s - 1) * block == place, 1.0, 0.0)
        summed = summed + mm(picks, gathered_ref[s], NN)
    water = divided(iota((rows, width), 1), levels) == 1
    out_ref[...] = jnp.where(water, jnp.maximum(summed, 0.0), summed)


def shape(*dims, dtype=F32):
    return jax.ShapeDtypeStruct(dims, dtype)


VMEM = pl.BlockSpec(memory_space=pltpu.VMEM)
SMEM = pl.BlockSpec(memory_space=pltpu.SMEM)
PARAMS = pltpu.CompilerParams(vmem_limit_bytes=60 << 20)


def call(kernel, inputs, out_shape, name, scratch=(), first=VMEM):
    many = isinstance(out_shape, (list, tuple))
    return pl.pallas_call(
        kernel,
        out_shape=out_shape,
        in_specs=[first] + [VMEM] * (len(inputs) - 1),
        out_specs=[VMEM] * len(out_shape) if many else VMEM,
        scratch_shapes=list(scratch),
        compiler_params=PARAMS,
        name=name,
    )(*inputs)


def body(
    column_state, mixing_rate, neighbours, assignment, substeps, cloud_state, level_map, saturation
):
    col_count = lax.axis_size("col")
    sec_count = lax.axis_size("sec")
    section = lax.axis_index("sec")
    position = lax.axis_index("col")
    rows, width = column_state.shape
    cloud_levels, levels = level_map.shape
    _, fields, _, columns, slots = cloud_state.shape
    elements = rows // 4
    capacity = slots // col_count
    padded = -(-capacity // 8) * 8
    block = col_count * padded
    clouds = (sec_count - 1) * col_count
    tiles = -(-slots // LANES)
    level_rows = -(-cloud_levels // 8) * 8
    mixing = mixing_rate.reshape(1, width)
    state = cloud_state[0]

    means = call(means_kernel, (column_state,), shape(elements, width), "means")
    ring = [(i, (i + 1) % col_count) for i in range(col_count)]
    left = lax.ppermute(means, "col", ring)
    right = lax.ppermute(means, "col", [(j, i) for i, j in ring])

    where = jnp.stack([section, position]).astype(I32)
    base, sides, pack, counts, places, fold, unfold = call(
        functools.partial(
            host_kernel, col_count=col_count, capacity=capacity, padded=padded, clouds=clouds
        ),
        (
            where,
            column_state,
            means,
            mixing,
            neighbours.T,
            assignment.reshape(1, rows),
            substeps.reshape(1, rows),
            level_map,
        ),
        [
            shape(rows, width),
            shape(rows, 2 * elements),
            shape(block, rows),
            shape(block, width),
            shape(rows, LANES),
            shape(width, width),
            shape(width, width),
        ],
        "host",
        first=SMEM,
    )
    moved, cloud_means = call(
        prepare_kernel,
        (state,),
        [
            shape(tiles, fields, cloud_levels, columns, LANES),
            shape(tiles, fields, level_rows, LANES),
        ],
        "prepare",
        scratch=[
            pltpu.VMEM((cloud_levels, columns, LANES), F32),
            pltpu.VMEM((level_rows * 8, LANES), F32),
        ],
    )
    advanced, outgoing = call(
        pack_kernel,
        (base, sides, left, right, mixing, pack, counts, fold),
        [shape(rows, width), shape(block, width)],
        "pack",
    )
    received = lax.all_to_all(outgoing, "col", split_axis=0, concat_axis=0, tiled=True)
    water, excess, offsets, slot_counts, back = call(
        functools.partial(
            water_kernel, capacity=capacity, padded=padded, slots=slots, stride=levels
        ),
        (
            received,
            moved,
            cloud_means,
            jnp.broadcast_to(saturation[:, None], (cloud_levels, LANES)),
            unfold,
        ),
        [
            shape(tiles, cloud_levels, columns, LANES),
            shape(MAX_SUB, tiles, cloud_levels, columns, LANES),
            shape(MAX_SUB, tiles, fields, level_rows, LANES),
            shape(tiles, 8, LANES),
            shape(block, width),
        ],
        "water",
        scratch=[
            pltpu.VMEM((width, LANES), F32),
            pltpu.VMEM((level_rows * 8, LANES), F32),
            pltpu.VMEM((width, slots), F32),
        ],
    )
    returned = lax.all_to_all(back, "col", split_axis=0, concat_axis=0, tiled=True)
    new_block = call(
        energy_kernel,
        (state, moved, water, excess, offsets, slot_counts),
        shape(fields, cloud_levels, columns, slots, dtype=jnp.bfloat16),
        "energy",
        scratch=[
            pltpu.VMEM((cloud_levels, columns, LANES), F32),
            pltpu.VMEM((cloud_levels, columns, LANES), F32),
        ],
    )
    gathered = lax.all_gather(returned, "sec", axis=0, tiled=False)
    new_columns = call(
        functools.partial(final_kernel, levels=levels),
        (advanced, places, gathered),
        shape(rows, width),
        "final",
    )
    return new_columns, new_block[None]


def solution(mesh):
    in_specs = (
        P("col", None),
        P(),
        P("col", None),
        P("col", None),
        P("col"),
        P("sec", None, None, None, "col"),
        P(),
        P(),
    )
    out_specs = (P("col", None), P("sec", None, None, None, "col"))
    return jax.shard_map(body, mesh=mesh, in_specs=in_specs, out_specs=out_specs, check_vma=False)
```

time: 126 us -> 66.7 us (0.53)
  Pallas kernels: 0 us -> 40.5 us
  other arithmetic: 40 us -> 0.58 us
  waiting for transfers between devices: 22.9 us -> 1.25 us
  local copies, waits for them, and re-layouts: 22.6 us -> 1.28 us
  between operations: 14.7 us -> 0.67 us
  starting transfers between devices: 18.8 us -> 15 us
  blocking collectives: 5.4 us -> 7.06 us
    pallas_call x0 -> x7, Pallas kernels: none -> 40.5 us  [call(): pl.pallas_call(kernel, out_shape=out_shape, in_specs=[first] + [VMEM] * (...]
    add x14 -> x0, other arithmetic: 18.3 us -> none  [the longest x4 13 us: cloud_substep(): fields = fields + HORIZ * across + VERTIC * (upper + lower - 2.0 * fields)]
    slice x18 -> x0, local copies, waits for them, and re-layouts: 11.7 us -> none  [the longest x8 6.97 us: cloud_substep(): jnp.roll(fields, -1, axis=2)]
    reduce_scatter x1 -> x0, waiting for transfers between devices: 9.85 us -> none  [body(): lax.psum_scatter(contribution, 'sec', scatter_dimension=0, tiled=True)]
    convert_element_type x2 -> x0, other arithmetic: 8.32 us -> none  [the longest x1 7.63 us: run_cloud(): return (fields.astype(jnp.bfloat16), tendency)]
    reduce_sum x9 -> x0, other arithmetic: 7.98 us -> none  [the longest x4 4.62 us: cloud_substep(): mean_now = jnp.mean(fields, axis=2)]
    all_to_all x2 -> x1, waiting for transfers between devices: 6.98 us -> 0.01 us  [body(): lax.all_to_all(back, 'col', split_axis=0, concat_axis=0, tiled=True)]
    all_to_all x1, waiting for transfers between devices: 6 us -> 1.24 us  [body(): lax.all_to_all(outgoing, 'col', split_axis=0, concat_axis=0, tiled=True)]
  transfers between devices with their start and end apart: 6 -> 4, of which waited for: 3 -> 1; matrix products, arithmetic and copies ran while one was open for 16% -> 1% of each run, Pallas kernels for 0% -> 32%
where the time goes in v1:
time: 66.7 us; the launch traced here: 66.3 us
  Pallas kernels  40.5 us (61%)
  starting transfers between devices  15 us (22%)
  blocking collectives  7.06 us (11%)
  local copies, waits for them, and re-layouts  1.28 us (2%)
  waiting for transfers between devices  1.25 us (2%)
  between operations  0.67 us (1%)
    pallas_call x7, Pallas kernels, call(): pl.pallas_call(kernel, out_shape=out_shape, in_specs=[first] + [VMEM] * (...  40.5 us
    all_gather x1, blocking collectives, body(): gathered = lax.all_gather(returned, 'sec', axis=0, tiled=False)  7.06 us
    all_to_all x1, starting transfers between devices, body(): lax.all_to_all(back, 'col', split_axis=0, concat_axis=0, tiled=True)  4.76 us
    all_to_all x1, starting transfers between devices, body(): lax.all_to_all(outgoing, 'col', split_axis=0, concat_axis=0, tiled=True)  4.16 us
    ppermute x1, starting transfers between devices, body(): right = lax.ppermute(means, 'col', [(j, i) for i, j in ring])  3.04 us
    ppermute x1, starting transfers between devices, body(): left = lax.ppermute(means, 'col', ring)  3 us
  transfers between devices with their start and end apart: 4, of which 1 were waited for; matrix products, arithmetic and copies ran while one was open for 1% of the time, Pallas kernels for 32%

profile of v1, /device:TPU:0, one launch (start us, length us, event | category | flops | bytes accessed | tf_op | source)
XLA Modules:
  0.0 66.3 jit_solution(3333494196270088410)
XLA Ops:
  0.6 0.0 copy-start.3
  0.6 1.5 %means.1.means_ref = f32[64,128]{1,0:T(8,128)} custom-call(f32[256,128]{1,0:T(8,128)} %columns_ref.3), custom_call_target="tpu_custom_call" | custom-call | tf_op jit(solution)/shard_map/means/pallas_call | solution.py:370
  2.2 3.0 %collective-permute-start = (f32[64,128]{1,0:T(8,128)}, f32[64,128]{1,0:T(8,128)S(1)}, u32[]{:S(2)}, u32[]{:S(2)}) collective-permute-start(f32[64,128]{1,0:T(8,128)} %means.1.means_ref), channel_id=1, source_target_pairs={{0,1},{1,2},{2,3},{3,4},{4,5},{5,6},{6,7},{7,0},{8,9},{9,10},{10,1... | collective-permute-start | bytes 98312 | tf_op jit(solution)/shard_map/ppermute | solution.py:403
  5.2 3.0 %collective-permute-start.1 = (f32[64,128]{1,0:T(8,128)}, f32[64,128]{1,0:T(8,128)S(1)}, u32[]{:S(2)}, u32[]{:S(2)}) collective-permute-start(f32[64,128]{1,0:T(8,128)} %means.1.means_ref), channel_id=1, source_target_pairs={{1,0},{2,1},{3,2},{4,3},{5,4},{6,5},{7,6},{0,7},{9,8},{10,9},{11,1... | collective-permute-start | bytes 98312 | tf_op jit(solution)/shard_map/ppermute | solution.py:404
  8.2 0.6 pad_add_fusion.where_ref
  8.8 3.3 %host.1 = (f32[256,128]{1,0:T(8,128)}, f32[256,128]{1,0:T(8,128)}, f32[192,256]{1,0:T(8,128)}, f32[192,128]{1,0:T(8,128)}, f32[256,128]{1,0:T(8,128)}, /*index=5*/f32[128,128]{1,0:T(8,128)}, f32[128,128]{1,0:T(8,128)}) custom-call(s32[2]{0:T(128)} %pad_add_fusion.where_ref, f32[256,128]{1,0:T(8,128)} %columns_ref.3, f32[64,128]{1,0:T(8,128)} %means.1.means_ref, ...), custom_call_target="tpu_custom_call" | custom-call | tf_op jit(solution)/shard_map/host/pallas_call | solution.py:370
  12.1 0.0 collective-permute-done.left_ref
  12.1 0.0 copy-start.1
  12.1 0.0 collective-permute-done.1.right_ref
  12.1 0.0 copy-start.2
  12.1 0.6 copy-done.1
  12.7 0.0 copy-done.2
  12.7 2.8 %pack.1 = (f32[256,128]{1,0:T(8,128)}, f32[192,128]{1,0:T(8,128)}) custom-call(f32[256,128]{1,0:T(8,128)} %get-tuple-element.18.base_ref, f32[256,128]{1,0:T(8,128)} %get-tuple-element.19.sides_ref, f32[64,128]{1,0:T(8,128)} %copy-done.1, f32[64,128]{1,0:T(8,128)} %copy-done.2, f32[1,128]{1,0:T(1,128)} %bitcast.21, f32[192,256]{1,0:T(8,128)} %get-tuple-element.20.pack_ref, ...), custom_call_target="tpu_custom_call" | custom-call | tf_op jit(solution)/shard_map/pack/pallas_call | solution.py:370
  15.6 4.2 %all-to-all-start = ((f32[8,24,128]{2,1,0:T(8,128)}), f32[8,24,128]{2,1,0:T(8,128)S(1)}, u32[]{:S(2)}, u32[]{:S(2)}) async-start(f32[8,24,128]{2,1,0:T(8,128)} %bitcast.17), calls=%async_computation | async-start | bytes 196608 | tf_op jit(solution)/shard_map/all_to_all | solution.py:452
  19.7 5.9 %prepare.1 = (f32[2,2,58,32,128]{4,3,2,1,0:T(8,128)}, f32[2,2,64,128]{3,2,1,0:T(8,128)}) custom-call(bf16[2,58,32,168]{3,2,1,0:T(8,128)(2,1)} %bitcast.12), custom_call_target="tpu_custom_call" | custom-call | tf_op jit(solution)/shard_map/prepare/pallas_call | solution.py:370
  25.6 1.2 %all-to-all-done = f32[8,24,128]{2,1,0:T(8,128)S(1)} async-done(((f32[8,24,128]{2,1,0:T(8,128)}), f32[8,24,128]{2,1,0:T(8,128)S(1)}, u32[]{:S(2)}, u32[]{:S(2)}) %all-to-all-start) | async-done | bytes 98336 | tf_op jit(solution)/shard_map/all_to_all | solution.py:452
  26.8 0.0 copy-start
  26.8 0.0 copy-done.3
  26.8 0.7 %broadcast_in_dim.4.saturation_ref = f32[58,128]{1,0:T(8,128)} broadcast(f32[58]{0:T(128)S(1)} %copy-done.3), dimensions={0} | broadcast | bytes 29928 | tf_op jit(solution)/shard_map/broadcast_in_dim | solution.py:461
  27.5 0.0 copy-done
  27.5 12.3 %water.1 = (f32[2,58,32,128]{3,2,1,0:T(8,128)}, f32[4,2,58,32,128]{4,3,2,1,0:T(8,128)}, f32[4,2,2,64,128]{4,3,2,1,0:T(8,128)}, f32[2,8,128]{2,1,0:T(8,128)}, f32[192,128]{1,0:T(8,128)}) custom-call(f32[192,128]{1,0:T(8,128)} %bitcast.16, f32[2,2,58,32,128]{4,3,2,1,0:T(8,128)} %get-tuple-element.26.moved_ref, f32[2,2,64,128]{3,2,1,0:T(8,128)} %get-tuple-element.27.means_ref, ...), custom_call_target="tpu_custom_call" | custom-call | tf_op jit(solution)/shard_map/water/pallas_call | solution.py:370
  39.8 4.8 %all-to-all-start.1 = ((f32[8,24,128]{2,1,0:T(8,128)}), f32[8,24,128]{2,1,0:T(8,128)S(1)}, u32[]{:S(2)}, u32[]{:S(2)}) async-start(f32[8,24,128]{2,1,0:T(8,128)} %bitcast.18), calls=%async_computation.1 | async-start | bytes 196608 | tf_op jit(solution)/shard_map/all_to_all | solution.py:478
  44.6 12.0 %energy.1 = bf16[2,58,32,168]{3,2,1,0:T(8,128)(2,1)} custom-call(bf16[2,58,32,168]{3,2,1,0:T(8,128)(2,1)} %bitcast.13, f32[2,2,58,32,128]{4,3,2,1,0:T(8,128)} %get-tuple-element.26.moved_ref, f32[2,58,32,128]{3,2,1,0:T(8,128)} %get-tuple-element.30.water_ref, f32[4,2,58,32,128]{4,3,2,1,0:T(8,128)} %get-tuple-element.31.excess_ref, ...), custom_call_target="tpu_custom_call" | custom-call | tf_op jit(solution)/shard_map/energy/pallas_call | solution.py:370
  56.6 0.0 all-to-all-done.1
  56.6 7.1 %all_gather.7.gathered_ref = f32[4,192,128]{2,1,0:T(8,128)} all-gather(f32[1,192,128]{2,1,0:T(8,128)S(1)} %bitcast.15), channel_id=1, replica_groups=mesh['sec'=4,'col'=8] {'sec'}, dimensions={0}, use_global_device_ids=true | all-gather | bytes 491520 | tf_op jit(solution)/shard_map/all_gather | solution.py:489
  63.7 2.7 %final.1 = f32[256,128]{1,0:T(8,128)} custom-call(f32[256,128]{1,0:T(8,128)} %get-tuple-element.23.advanced_ref, f32[256,128]{1,0:T(8,128)} %get-tuple-element.24.slots_ref, f32[4,192,128]{2,1,0:T(8,128)} %all_gather.7.gathered_ref), custom_call_target="tpu_custom_call" | custom-call | tf_op jit(solution)/shard_map/final/pallas_call | solution.py:370
Async XLA Ops:
  0.6 26.2 %copy-start.3 = (f32[58]{0:T(128)S(1)}, f32[58]{0:T(128)}, u32[]{:S(2)}) copy-start(f32[58]{0:T(128)} %param.15) | copy-start | bytes 700
  2.2 9.9 %collective-permute-start = (f32[64,128]{1,0:T(8,128)}, f32[64,128]{1,0:T(8,128)S(1)}, u32[]{:S(2)}, u32[]{:S(2)}) collective-permute-start(f32[64,128]{1,0:T(8,128)} %means.1.means_ref), channel_id=1, source_target_pairs={{0,1},{1,2},{2,3},{3,4},{4,5},{5,6},{6,7},{7,0},{8,9},{9,10},{10,1... | collective-permute-start | bytes 98312 | tf_op jit(solution)/shard_map/ppermute | solution.py:403
  5.2 7.0 %collective-permute-start.1 = (f32[64,128]{1,0:T(8,128)}, f32[64,128]{1,0:T(8,128)S(1)}, u32[]{:S(2)}, u32[]{:S(2)}) collective-permute-start(f32[64,128]{1,0:T(8,128)} %means.1.means_ref), channel_id=1, source_target_pairs={{1,0},{2,1},{3,2},{4,3},{5,4},{6,5},{7,6},{0,7},{9,8},{10,9},{11,1... | collective-permute-start | bytes 98312 | tf_op jit(solution)/shard_map/ppermute | solution.py:404
  12.1 0.6 copy-start.1
  12.1 0.6 copy-start.2
  15.6 11.3 %all-to-all-start = ((f32[8,24,128]{2,1,0:T(8,128)}), f32[8,24,128]{2,1,0:T(8,128)S(1)}, u32[]{:S(2)}, u32[]{:S(2)}) async-start(f32[8,24,128]{2,1,0:T(8,128)} %bitcast.17), calls=%async_computation | async-start | bytes 196608 | tf_op jit(solution)/shard_map/all_to_all | solution.py:452
  26.8 0.7 %copy-start = (f32[8,24,128]{2,1,0:T(8,128)}, f32[8,24,128]{2,1,0:T(8,128)S(1)}, u32[]{:S(2)}) copy-start(f32[8,24,128]{2,1,0:T(8,128)S(1)} %all-to-all-done) | copy-start | bytes 294916
  39.8 16.8 %all-to-all-start.1 = ((f32[8,24,128]{2,1,0:T(8,128)}), f32[8,24,128]{2,1,0:T(8,128)S(1)}, u32[]{:S(2)}, u32[]{:S(2)}) async-start(f32[8,24,128]{2,1,0:T(8,128)} %bitcast.18), calls=%async_computation.1 | async-start | bytes 196608 | tf_op jit(solution)/shard_map/all_to_all | solution.py:478

commit v2 on v1

v2 whole, which is shorter than its diff:
```python
import functools

import jax
import jax.numpy as jnp
from jax import lax
from jax.experimental import pallas as pl
from jax.experimental.pallas import tpu as pltpu
from jax.sharding import PartitionSpec as P

MAX_SUB = 4
RELAX = 0.25
HORIZ = 0.12
VERTIC = 0.1
LATENT = 2.5
VMIX = 0.2
HIGH = lax.Precision.HIGHEST
LANES = 128
F32 = jnp.float32
BF16 = jnp.bfloat16
STEP = 10
SHRINK = 1.0 / LATENT
I32 = jnp.int32


def iota(shape, dim):
    return lax.broadcasted_iota(I32, shape, dim)


def mm(a, b, contract, precision=HIGH):
    return lax.dot_general(
        a, b, (contract, ((), ())), precision=precision, preferred_element_type=F32
    )


NN = ((1,), (0,))
NT = ((1,), (1,))
TN = ((0,), (0,))


def divided(value, by):
    return jnp.floor((value.astype(F32) + 0.5) * (1.0 / by)).astype(I32)


def split(values):
    high = values.astype(BF16)
    rest = values - high.astype(F32)
    middle = rest.astype(BF16)
    low = (rest - middle.astype(F32)).astype(BF16)
    return low, middle, high


def select(picks, values, contract, swap=False):
    total = None
    for part in split(values):
        a, b = (part, picks) if swap else (picks, part)
        term = lax.dot_general(a, b, (contract, ((), ())), preferred_element_type=F32)
        total = term if total is None else total + term
    return total


def vertical_mix(values, levels):
    upper = jnp.concatenate([values[1:levels], values[levels - 1 : levels]], axis=0)
    lower = jnp.concatenate([values[0:1], values[0 : levels - 1]], axis=0)
    inner = values[0:levels]
    return inner + VERTIC * (upper + lower - 2.0 * inner)


def means_kernel(columns_ref, means_ref):
    elements = means_ref.shape[0]
    total = columns_ref[pl.ds(0, elements, stride=4), :]
    for k in range(1, 4):
        total = total + columns_ref[pl.ds(k, elements, stride=4), :]
    means_ref[...] = 0.25 * total


def host_kernel(
    columns_ref,
    means_ref,
    mixing_ref,
    neighbours_ref,
    targets_ref,
    substeps_ref,
    map_ref,
    base_ref,
    sides_ref,
    wanted_ref,
    constant_ref,
    slots_ref,
    fold_ref,
    unfold_ref,
    *,
    col_count,
    padded,
    clouds,
):
    section = lax.axis_index("sec")
    position = lax.axis_index("col")
    rows, width = columns_ref.shape
    levels = map_ref.shape[1]
    cloud_levels = map_ref.shape[0]
    elements = rows // 4
    block = col_count * padded
    near = neighbours_ref[...] - (position - 1) * elements
    near = jnp.where(near < 0, near + elements * col_count, near)
    near = jnp.where(near >= elements * col_count, near - elements * col_count, near)
    window = iota((3 * elements, elements), 0)
    picks = jnp.where(window == iota((3 * elements, elements), 1) + elements, -4.0, 0.0)
    for k in range(near.shape[0]):
        picks = picks + jnp.where(window == near[k : k + 1, :], 1.0, 0.0)
    row_element = divided(iota((rows, elements), 0), 4)
    spread_rows = jnp.where(row_element == iota((rows, elements), 1), 1.0, 0.0)
    weights = mm(spread_rows.astype(BF16), picks.astype(BF16), NT, None)
    sides = jnp.concatenate([weights[:, :elements], weights[:, 2 * elements :]], axis=1)
    sides = sides.astype(BF16)
    sides_ref[...] = sides
    own = select(weights[:, elements : 2 * elements].astype(BF16), means_ref[...], NN)
    values = columns_ref[...]
    lane = iota((rows, width), 1)
    level = lane - levels * divided(lane, levels)
    upper = jnp.where(level == levels - 1, values, pltpu.roll(values, width - 1, 1))
    lower = jnp.where(level == 0, values, pltpu.roll(values, 1, 1))
    base = values + mixing_ref[...] * own + VMIX * (upper + lower - 2.0 * values)
    base_ref[...] = base
    targets = targets_ref[...]
    onehot = jnp.where(iota((clouds, rows), 0) == targets, 1.0, 0.0)
    before = jnp.where(iota((rows, rows), 0) < iota((rows, rows), 1), 1.0, 0.0)
    running = mm(onehot.astype(BF16), before.astype(BF16), NN, None)
    ranks = jnp.sum(running * onehot, axis=0, keepdims=True).astype(I32)
    owner = divided(targets, col_count)
    slot = (targets - owner * col_count) * padded + ranks
    mine = jnp.where(owner + 1 == section, slot, -1)
    pack = jnp.where(iota((block, rows), 0) == mine, 1.0, 0.0).astype(BF16)
    wanted_ref[...] = mm(pack, sides, NN, None).astype(BF16)
    plain = map_ref[...]
    folded = RELAX * vertical_mix(plain, cloud_levels)
    for ref, value in ((fold_ref, folded), (unfold_ref, plain)):
        ref[...] = jnp.zeros_like(ref)
        for f in range(width // levels):
            ref[f * levels : f * levels + cloud_levels, f * levels : (f + 1) * levels] = value
    count_rows = jnp.where(
        iota((width, rows), 0) == levels - 1, substeps_ref[...].astype(F32), 0.0
    )
    counts = mm(pack, count_rows.astype(BF16), NT, None)
    constant_ref[...] = mm(select(pack, base, NN), fold_ref[...], NT) + counts
    everywhere = jnp.broadcast_to((owner * block + slot).astype(F32), (LANES, rows))
    identity = jnp.where(iota((rows, rows), 0) == iota((rows, rows), 1), 1.0, 0.0)
    slots_ref[...] = select(identity.astype(BF16), everywhere, NT)


def pack_kernel(wanted_ref, left_ref, right_ref, mixing_ref, constant_ref, fold_ref, out_ref):
    halo = jnp.concatenate([left_ref[...], right_ref[...]], axis=0)
    spread = mixing_ref[...] * select(wanted_ref[...], halo, NN)
    out_ref[...] = constant_ref[...] + mm(spread, fold_ref[...], NT)


class Segment:
    def __init__(self, lane0, width, levels, begin):
        self.lane0, self.width, self.begin, self.levels = lane0, width, begin, levels
        self.steps = -(-levels // (LANES // width))
        self.groups = -(-levels // self.steps)
        self.missing = self.groups * self.steps - levels
        self.blocks = -(-self.steps // STEP)
        self.rows = (begin + 1, begin + 1 + self.steps)

    def group_steps(self, g):
        return self.steps - (self.missing if g == self.groups - 1 else 0)


def segments_of(slots, levels):
    segments, begin = [], 0
    for lane0 in range(0, slots, LANES):
        segments.append(Segment(lane0, min(LANES, slots - lane0), levels, begin))
        begin += segments[-1].steps + 2
    rows = max([begin] + [s.begin + 2 + s.blocks * STEP for s in segments])
    return segments, -(-rows // 8) * 8


def fill_spare(segments, load, store):
    def turned(value, shift):
        tall = jnp.broadcast_to(value, (8, LANES)) if value.shape[0] == 1 else value
        return pltpu.roll(tall, shift % LANES, 1)[: value.shape[0]]

    for s in segments:
        if s.missing:
            row = s.rows[1] - s.missing
            value = load(row - 1)
            lane = iota(value.shape, 1)
            store(row, jnp.where(lane >= (s.groups - 1) * s.width, value, load(row)))
        first, last = load(s.rows[0]), load(s.rows[1] - 1)
        before, after = first, last
        if s.groups > 1:
            lane = iota(first.shape, 1)
            before = jnp.where(lane < s.width, first, turned(last, s.width))
            after = jnp.where(lane < (s.groups - 1) * s.width, turned(first, -s.width), last)
        store(s.begin, before)
        store(s.rows[1], after)


def fill_wide(segments, ref):
    def store(row, value):
        ref[row] = value

    fill_spare(segments, lambda row: ref[row], store)


def fill_flat(segments, ref):
    def store(row, value):
        ref[row : row + 1, :] = value

    fill_spare(segments, lambda row: ref[row : row + 1, :], store)


def linear(below, here, above):
    east = [pltpu.roll(here[3], 1, 0), here[0], here[1], here[2]]
    west = [here[1], here[2], here[3], pltpu.roll(here[0], 7, 0)]
    keep = (1.0 - 2.0 * HORIZ - 2.0 * VERTIC) / VERTIC
    return [
        (below[j] + above[j]) + ((HORIZ / VERTIC) * (east[j] + west[j]) + keep * here[j])
        for j in range(4)
    ]


def groups(ref, index):
    return [ref[index + (pl.ds(8 * j, 8),)] for j in range(4)]


def strided(ref, row):
    return [ref[row, pl.ds(j, 8, stride=4), :] for j in range(4)]


def sweep(segment, load, work):
    def block(i, carry):
        row = segment.begin + i * STEP
        held = [load(row), load(row + 1)]
        for k in range(STEP):
            held.append(load(row + k + 2))
            work(row + k + 1, held[k], held[k + 1], held[k + 2])
        return carry

    lax.fori_loop(0, segment.blocks, block, 0)


def folded_sums(sums_ref, columns):
    rows = sums_ref.shape[0] // 8
    total = sums_ref[pl.ds(0, rows, stride=8), :]
    for k in range(1, 8):
        total = total + sums_ref[pl.ds(k, rows, stride=8), :]
    return total * (1.0 / columns)


def slab(row):
    return pl.ds(pl.multiple_of(row * 8, 8), 8)


def spread_row(ref, row):
    return jnp.broadcast_to(ref[pl.ds(row, 1), :], (8, LANES))


def lane_places(segments):
    return [(s, g) for s in segments for g in range(s.groups)]


def prepare_kernel(
    state_ref,
    saturation_ref,
    moved_ref,
    means_ref,
    limits_ref,
    places_ref,
    state_buf,
    moved_buf,
    natural_ref,
    sums_ref,
    in_sems,
    out_sems,
    *,
    segments,
    capacity,
    padded,
):
    fields, levels, columns, slots = state_ref.shape
    order = list(range(fields))[::-1]
    loads = [pltpu.make_async_copy(state_ref.at[f], state_buf.at[f], in_sems.at[f]) for f in range(fields)]
    for f in order:
        loads[f].start()
    for t, (s, g) in enumerate(lane_places(segments)):
        lane = iota((places_ref.shape[0], LANES), 1) - g * s.width
        slot = s.lane0 + lane
        row = slot + (padded - capacity) * divided(jnp.maximum(slot, 0), capacity)
        inside = (lane >= 0) & (lane < s.width)
        hit = jnp.where(inside & (iota(lane.shape, 0) == row), 1.0, 0.0)
        places_ref[:, t * LANES : (t + 1) * LANES] = hit.astype(BF16)
    limits_ref[...] = jnp.zeros_like(limits_ref)
    for s in segments:

        def limit(k, carry):
            lane = iota((1, LANES), 1)
            value = jnp.full((1, LANES), saturation_ref[k])
            for g in range(1, s.groups):
                other = saturation_ref[jnp.minimum(k + g * s.steps, levels - 1)]
                value = jnp.where(lane >= g * s.width, other, value)
            limits_ref[pl.ds(s.begin + 1 + k, 1), :] = 0.5 * value
            return carry

        lax.fori_loop(0, s.steps, limit, 0)
    stores = []
    for f in order:
        scale = SHRINK if f == 0 else 1.0
        loads[f].wait()
        for s in segments:
            at = slice(s.lane0, s.lane0 + s.width)

            def widen(k, carry):
                parts = []
                for g in range(s.groups):
                    level = jnp.minimum(g * s.steps + k, levels - 1)
                    parts.append(state_buf[f, level, :, at].astype(F32))
                spare = LANES - s.groups * s.width
                if spare:
                    parts.append(jnp.zeros((columns, spare), F32))
                value = jnp.concatenate(parts, axis=1) if len(parts) > 1 else parts[0]
                natural_ref[s.begin + 1 + k] = scale * value if scale != 1.0 else value
                return carry

            lax.fori_loop(0, s.steps, widen, 0, unroll=2)
        fill_wide(segments, natural_ref)
        for s in segments:

            def work(row, below, here, above):
                out = linear(below, here, above)
                for j in range(4):
                    moved_buf[f, row, pl.ds(8 * j, 8), :] = out[j]
                sums_ref[slab(row), :] = (here[0] + here[1]) + (here[2] + here[3])

            sweep(s, lambda row: strided(natural_ref, row), work)
        means_ref[f] = folded_sums(sums_ref, columns) * (1.0 / scale)
        stores.append(pltpu.make_async_copy(moved_buf.at[f], moved_ref.at[f], out_sems.at[f]))
        stores[-1].start()
    for copy in stores:
        copy.wait()


def water_kernel(
    received_ref,
    places_ref,
    moved_ref,
    means_ref,
    limits_ref,
    unfold_ref,
    water_ref,
    spill_ref,
    offsets_ref,
    counts_ref,
    back_ref,
    moved_buf,
    even_ref,
    odd_ref,
    spill_buf,
    goal_ref,
    mean_ref,
    shift_ref,
    limit_ref,
    sums_ref,
    change_ref,
    in_sem,
    spill_sems,
    out_sem,
    *,
    segments,
    levels,
    stride,
):
    rows = means_ref.shape[1]
    columns = moved_buf.shape[1]
    load = pltpu.make_async_copy(moved_ref.at[1], moved_buf, in_sem)
    load.start()
    arrived = select(places_ref[...], received_ref[...], TN, swap=True)
    goal_ref[...] = jnp.zeros_like(goal_ref)
    counts_ref[...] = jnp.zeros_like(counts_ref)
    for s in segments:
        count = None
        for t, (owner, g) in enumerate(lane_places(segments)):
            if owner is not s:
                continue
            lanes = slice(t * LANES, (t + 1) * LANES)
            number = s.group_steps(g)
            for f in range(2):
                first = f * stride + g * s.steps
                at = slice(s.rows[0], s.rows[0] + number)
                goal_ref[f, at, :] = goal_ref[f, at, :] + arrived[first : first + number, lanes]
            part = arrived[stride - 1 : stride, lanes]
            count = part if count is None else count + part
        counts_ref[s.rows[0] : s.rows[1], :] = jnp.broadcast_to(count, (s.steps, LANES))
    for f in range(2):
        mean_ref[f] = means_ref[f]
    load.wait()
    spills = []
    source, target = None, even_ref
    for n in range(MAX_SUB):
        scale = 10.0 ** (n + 1)
        expected = []
        for f in range(2):
            fill_flat(segments, mean_ref.at[f])
            mean = mean_ref[f]
            mixed = mean + VERTIC * (
                pltpu.roll(mean, 1, 0) + pltpu.roll(mean, rows - 1, 0) - 2.0 * mean
            )
            offset = goal_ref[f] - RELAX * mixed
            expected.append(mixed + offset)
            if f == 1:
                shift_ref[...] = scale * offset
            else:
                offsets_ref[n] = (scale * SHRINK) * offset
        limit_ref[...] = scale * limits_ref[...]
        for s in segments:
            active = spread_row(counts_ref, s.rows[0]) > float(n)

            def finish(row, lin, old):
                shift = spread_row(shift_ref, row)
                limit = spread_row(limit_ref, row)
                total = None
                for j in range(4):
                    v = lin[j] + shift
                    c = jnp.maximum(0.5 * v - limit, 0.0)
                    u = v - c
                    if old is not None:
                        u = jnp.where(active, u, old[j])
                    spill_buf[n, row, pl.ds(8 * j, 8), :] = c
                    target[row, pl.ds(8 * j, 8), :] = u
                    total = c if total is None else total + c
                sums_ref[slab(row), :] = total

            if n == 0:

                def block(i, carry):
                    for k in range(STEP):
                        row = s.begin + 1 + i * STEP + k
                        finish(row, groups(moved_buf, (row,)), None)
                    return carry

                lax.fori_loop(0, s.blocks, block, 0)
            else:

                def work(row, below, here, above):
                    finish(row, linear(below, here, above), here)

                sweep(s, lambda row: groups(source, (row,)), work)
        spills.append(pltpu.make_async_copy(spill_buf.at[n], spill_ref.at[n], spill_sems.at[n]))
        spills[-1].start()
        spilled = folded_sums(sums_ref, columns) * (1.0 / scale)
        step = [expected[0] + LATENT * spilled, expected[1] - spilled]
        keep = counts_ref[...] > float(n)
        for f in range(2):
            mean_ref[f] = jnp.where(keep, step[f], mean_ref[f])
        if n + 1 < MAX_SUB:
            fill_wide(segments, target)
        source, target = target, (odd_ref if target is even_ref else even_ref)
    leave = pltpu.make_async_copy(source, water_ref, out_sem)
    leave.start()
    change_ref[...] = jnp.zeros_like(change_ref)
    for f in range(2):
        change = mean_ref[f] - means_ref[f]
        for t, (s, g) in enumerate(lane_places(segments)):
            first, number = f * stride + g * s.steps, s.group_steps(g)
            change_ref[first : first + number, t * LANES : (t + 1) * LANES] = change[
                s.rows[0] : s.rows[0] + number
            ]
    spread = select(places_ref[...], change_ref[...], NT)
    back_ref[...] = mm(spread, unfold_ref[...], NN)
    for copy in spills:
        copy.wait()
    leave.wait()


def energy_kernel(
    state_ref,
    moved_ref,
    water_ref,
    spill_ref,
    offsets_ref,
    counts_ref,
    out_ref,
    state_buf,
    moved_buf,
    water_buf,
    spill_buf,
    out_buf,
    even_ref,
    odd_ref,
    natural_ref,
    state_sems,
    moved_sem,
    water_sem,
    spill_sems,
    out_sems,
    *,
    segments,
):
    fields, levels, columns, _ = state_ref.shape
    waters = pltpu.make_async_copy(water_ref, water_buf, water_sem)
    states = [pltpu.make_async_copy(state_ref.at[f], state_buf.at[f], state_sems.at[f]) for f in range(fields)]
    moved = pltpu.make_async_copy(moved_ref.at[0], moved_buf, moved_sem)
    spills = [
        pltpu.make_async_copy(spill_ref.at[n], spill_buf.at[n], spill_sems.at[n])
        for n in range(MAX_SUB)
    ]
    waters.start()
    states[1].start()
    moved.start()
    for n in range(MAX_SUB):
        spills[n].start()
    states[0].start()
    leaves = [pltpu.make_async_copy(out_buf.at[f], out_ref.at[f], out_sems.at[f]) for f in range(fields)]

    def finish_field(f, source):
        for s in segments:
            count = spread_row(counts_ref, s.rows[0])
            back = jnp.zeros((8, LANES), F32)
            for n in range(1, MAX_SUB + 1):
                scale = 10.0**-n * (LATENT if f == 0 else 1.0)
                back = jnp.where(count == float(n), scale, back)

            def permute(row, carry):
                value = groups(source, (row,))
                for j in range(4):
                    natural_ref[row, pl.ds(j, 8, stride=4), :] = value[j] * back
                return carry

            lax.fori_loop(s.rows[0], s.rows[1], permute, 0, unroll=2)
            for g in range(s.groups):
                lanes = slice(g * s.width, (g + 1) * s.width)
                at = slice(s.lane0, s.lane0 + s.width)
                held = jnp.broadcast_to(count[0:1, lanes], (columns, s.width)) > 0.0

                def narrow(k, carry):
                    level = g * s.steps + k
                    old = state_buf[f, level, :, at].astype(F32)
                    value = jnp.where(held, natural_ref[s.begin + 1 + k, :, lanes], old)
                    out_buf[f, level, :, at] = value.astype(BF16)
                    return carry

                lax.fori_loop(0, s.group_steps(g), narrow, 0, unroll=2)
        leaves[f].start()

    waters.wait()
    states[1].wait()
    finish_field(1, water_buf)
    moved.wait()
    source, target = None, even_ref
    for n in range(MAX_SUB):
        spills[n].wait()
        for s in segments:
            active = spread_row(counts_ref, s.rows[0]) > float(n)

            def finish(row, lin, old):
                shift = spread_row(offsets_ref.at[n], row)
                c = groups(spill_buf, (n, row))
                for j in range(4):
                    u = (lin[j] + shift) + c[j]
                    if old is not None:
                        u = jnp.where(active, u, old[j])
                    target[row, pl.ds(8 * j, 8), :] = u

            if n == 0:

                def block(i, carry):
                    for k in range(STEP):
                        row = s.begin + 1 + i * STEP + k
                        finish(row, groups(moved_buf, (row,)), None)
                    return carry

                lax.fori_loop(0, s.blocks, block, 0)
            else:

                def work(row, below, here, above):
                    finish(row, linear(below, here, above), here)

                sweep(s, lambda row: groups(source, (row,)), work)
        if n + 1 < MAX_SUB:
            fill_wide(segments, target)
        source, target = target, (odd_ref if target is even_ref else even_ref)
    states[0].wait()
    finish_field(0, source)
    for f in range(fields):
        leaves[f].wait()


def final_kernel(
    base_ref, sides_ref, left_ref, right_ref, mixing_ref, slots_ref, gathered_ref, out_ref, *, levels
):
    rows, width = base_ref.shape
    sections, block, _ = gathered_ref.shape
    halo = jnp.concatenate([left_ref[...], right_ref[...]], axis=0)
    summed = base_ref[...] + mixing_ref[...] * select(sides_ref[...], halo, NN)
    place = slots_ref[:, :1].astype(I32)
    for s in range(1, sections):
        picks = jnp.where(iota((rows, block), 1) + (s - 1) * block == place, 1.0, 0.0)
        summed = summed + select(picks.astype(BF16), gathered_ref[s], NN)
    water = divided(iota((rows, width), 1), levels) == 1
    out_ref[...] = jnp.where(water, jnp.maximum(summed, 0.0), summed)


SPACES = dict(
    auto=pl.BlockSpec(memory_space=pltpu.VMEM),
    near=pl.BlockSpec(memory_space=pltpu.VMEM),
    far=pl.BlockSpec(memory_space=pl.ANY),
    scalar=pl.BlockSpec(memory_space=pltpu.SMEM),
)


def call(kernel, name, inputs, outputs, scratch=(), limit=8):
    arrays = [
        pltpu.with_memory_space_constraint(x, pltpu.VMEM) if space == "near" else x
        for space, x in inputs
    ]
    shapes = [
        (pltpu.VMEM if space == "near" else jax.ShapeDtypeStruct)(dims, dtype)
        for space, dims, dtype in outputs
    ]
    return pl.pallas_call(
        kernel,
        out_shape=shapes,
        in_specs=[SPACES[space] for space, _ in inputs],
        out_specs=[SPACES[space] for space, _, _ in outputs],
        scratch_shapes=list(scratch),
        compiler_params=pltpu.CompilerParams(vmem_limit_bytes=limit << 20),
        name=name,
    )(*arrays)


def body(
    column_state, mixing_rate, neighbours, assignment, substeps, cloud_state, level_map, saturation
):
    col_count = lax.axis_size("col")
    sec_count = lax.axis_size("sec")
    count, width = column_state.shape
    cloud_levels, levels = level_map.shape
    _, fields, _, columns, slots = cloud_state.shape
    elements = count // 4
    capacity = slots // col_count
    padded = -(-capacity // 8) * 8
    block = col_count * padded
    clouds = (sec_count - 1) * col_count
    segments, rows = segments_of(slots, cloud_levels)
    mapped = LANES * len(lane_places(segments))
    mixing = mixing_rate.reshape(1, width)
    state = cloud_state[0]
    dma = pltpu.SemaphoreType.DMA

    def wide(*lead):
        return pltpu.VMEM((*lead, rows, columns, LANES), F32)

    (means,) = call(
        means_kernel, "means", [("auto", column_state)], [("near", (elements, width), F32)]
    )
    ring = [(i, (i + 1) % col_count) for i in range(col_count)]
    left = lax.ppermute(means, "col", ring)
    right = lax.ppermute(means, "col", [(j, i) for i, j in ring])

    base, sides, wanted, constant, homes, fold, unfold = call(
        functools.partial(host_kernel, col_count=col_count, padded=padded, clouds=clouds),
        "host",
        [
            ("auto", column_state),
            ("near", means),
            ("auto", mixing),
            ("auto", neighbours.T),
            ("auto", assignment.reshape(1, count)),
            ("auto", substeps.reshape(1, count)),
            ("auto", level_map),
        ],
        [
            ("near", (count, width), F32),
            ("near", (count, 2 * elements), BF16),
            ("near", (block, 2 * elements), BF16),
            ("near", (block, width), F32),
            ("near", (count, LANES), F32),
            ("near", (width, width), F32),
            ("near", (width, width), F32),
        ],
    )
    (outgoing,) = call(
        pack_kernel,
        "pack",
        [
            ("near", wanted),
            ("near", left),
            ("near", right),
            ("auto", mixing),
            ("near", constant),
            ("near", fold),
        ],
        [("auto", (block, width), F32)],
    )
    received = lax.all_to_all(outgoing, "col", split_axis=0, concat_axis=0, tiled=True)
    moved, cloud_means, limits, places = call(
        functools.partial(
            prepare_kernel, segments=segments, capacity=capacity, padded=padded
        ),
        "prepare",
        [("far", state), ("scalar", saturation)],
        [
            ("far", (fields, rows, columns, LANES), F32),
            ("near", (fields, rows, LANES), F32),
            ("near", (rows, LANES), F32),
            ("near", (block, mapped), BF16),
        ],
        scratch=[
            pltpu.VMEM(state.shape, BF16),
            wide(fields),
            wide(),
            pltpu.VMEM((rows * 8, LANES), F32),
            dma((fields,)),
            dma((fields,)),
        ],
        limit=16,
    )
    water, spill, offsets, counts, back = call(
        functools.partial(water_kernel, segments=segments, levels=cloud_levels, stride=levels),
        "water",
        [
            ("near", received),
            ("near", places),
            ("far", moved),
            ("near", cloud_means),
            ("near", limits),
            ("near", unfold),
        ],
        [
            ("far", (rows, columns, LANES), F32),
            ("far", (MAX_SUB, rows, columns, LANES), F32),
            ("near", (MAX_SUB, rows, LANES), F32),
            ("near", (rows, LANES), F32),
            ("auto", (block, width), F32),
        ],
        scratch=[
            wide(),
            wide(),
            wide(),
            wide(MAX_SUB),
            pltpu.VMEM((fields, rows, LANES), F32),
            pltpu.VMEM((fields, rows, LANES), F32),
            pltpu.VMEM((rows, LANES), F32),
            pltpu.VMEM((rows, LANES), F32),
            pltpu.VMEM((rows * 8, LANES), F32),
            pltpu.VMEM((width, mapped), F32),
            dma(()),
            dma((MAX_SUB,)),
            dma(()),
        ],
        limit=24,
    )
    returned = lax.all_to_all(back, "col", split_axis=0, concat_axis=0, tiled=True)
    (new_block,) = call(
        functools.partial(energy_kernel, segments=segments),
        "energy",
        [
            ("far", state),
            ("far", moved),
            ("far", water),
            ("far", spill),
            ("near", offsets),
            ("near", counts),
        ],
        [("far", state.shape, BF16)],
        scratch=[
            pltpu.VMEM(state.shape, BF16),
            wide(),
            wide(),
            wide(MAX_SUB),
            pltpu.VMEM(state.shape, BF16),
            wide(),
            wide(),
            wide(),
            dma((fields,)),
            dma(()),
            dma(()),
            dma((MAX_SUB,)),
            dma((fields,)),
        ],
        limit=32,
    )
    gathered = lax.all_gather(returned, "sec", axis=0, tiled=False)
    (new_columns,) = call(
        functools.partial(final_kernel, levels=levels),
        "final",
        [
            ("near", base),
            ("near", sides),
            ("near", left),
            ("near", right),
            ("auto", mixing),
            ("near", homes),
            ("near", gathered),
        ],
        [("auto", (count, width), F32)],
    )
    return new_columns, new_block[None]


def solution(mesh):
    in_specs = (
        P("col", None),
        P(),
        P("col", None),
        P("col", None),
        P("col"),
        P("sec", None, None, None, "col"),
        P(),
        P(),
    )
    out_specs = (P("col", None), P("sec", None, None, None, "col"))
    return jax.shard_map(body, mesh=mesh, in_specs=in_specs, out_specs=out_specs, check_vma=False)
```

time: 66.7 us -> 71.9 us (1.078)
  local copies, waits for them, and re-layouts: 1.28 us -> 22.7 us
  Pallas kernels: 40.5 us -> 25.5 us
  waiting for transfers between devices: 1.25 us -> 0.01 us
    unnamed x8 -> x54, local copies, waits for them, and re-layouts: 0.61 us -> 22.7 us
    pallas_call x7, Pallas kernels: 40.5 us -> 25.5 us  [call(): pl.pallas_call(kernel, out_shape=shapes, in_specs=[SPACES[space] for spac...]
    all_to_all x1, waiting for transfers between devices: 1.24 us -> 0.01 us  [body(): lax.all_to_all(outgoing, 'col', split_axis=0, concat_axis=0, tiled=True)]
    all_to_all x1, starting transfers between devices: 4.76 us -> 5.93 us  [body(): lax.all_to_all(back, 'col', split_axis=0, concat_axis=0, tiled=True)]
    all_to_all x1, starting transfers between devices: 4.16 us -> 3.36 us  [body(): lax.all_to_all(outgoing, 'col', split_axis=0, concat_axis=0, tiled=True)]
  transfers between devices with their start and end apart: 4 -> 4, of which waited for: 1 -> 0; matrix products, arithmetic and copies ran while one was open for 1% -> 0% of each run, Pallas kernels for 32% -> 25%
where the time goes in v2:
time: 71.9 us; the launch traced here: 71.1 us
  Pallas kernels  25.5 us (35%)
  local copies, waits for them, and re-layouts  22.7 us (32%)
  starting transfers between devices  15.4 us (21%)
  blocking collectives  6.77 us (9%)
  between operations  0.76 us (1%)
    pallas_call x7, Pallas kernels, call(): pl.pallas_call(kernel, out_shape=shapes, in_specs=[SPACES[space] for spac...  25.5 us
    unnamed x54, local copies, waits for them, and re-layouts  22.7 us
    all_gather x1, blocking collectives, body(): gathered = lax.all_gather(returned, 'sec', axis=0, tiled=False)  6.77 us
    all_to_all x1, starting transfers between devices, body(): lax.all_to_all(back, 'col', split_axis=0, concat_axis=0, tiled=True)  5.93 us
    all_to_all x1, starting transfers between devices, body(): lax.all_to_all(outgoing, 'col', split_axis=0, concat_axis=0, tiled=True)  3.36 us
    ppermute x1, starting transfers between devices, body(): right = lax.ppermute(means, 'col', [(j, i) for i, j in ring])  3.1 us
    ppermute x1, starting transfers between devices, body(): left = lax.ppermute(means, 'col', ring)  3.05 us
  transfers between devices with their start and end apart: 4, of which 0 were waited for; matrix products, arithmetic and copies ran while one was open for 0% of the time, Pallas kernels for 25%

profile of v2, /device:TPU:0, one launch (start us, length us, event | category | flops | bytes accessed | tf_op | source)
XLA Modules:
  0.0 71.1 jit_solution(6676246882191083466)
XLA Ops:
  0.6 0.0 copy-start.6
  0.6 0.9 %copy-done.6 = f32[256,128]{1,0:T(8,128)S(1)} copy-done((f32[256,128]{1,0:T(8,128)S(1)}, f32[256,128]{1,0:T(8,128)}, u32[]{:S(2)}) %copy-start.6) | copy-done | bytes 131096
  1.5 3.0 %collective-permute-start = (f32[64,128]{1,0:T(8,128)S(1)}, f32[64,128]{1,0:T(8,128)S(1)}, u32[]{:S(2)}, u32[]{:S(2)}) collective-permute-start(f32[64,128]{1,0:T(8,128)S(1)} %means.1.means_ref), channel_id=1, source_target_pairs={{0,1},{1,2},{2,3},{3,4},{4,5},{5,6},{6,7},{7,0},{8,9},{9,10},{10,1... | collective-permute-start | bytes 98312 | tf_op jit(solution)/shard_map/ppermute | solution.py:657
  4.6 3.1 %collective-permute-start.1 = (f32[64,128]{1,0:T(8,128)S(1)}, f32[64,128]{1,0:T(8,128)S(1)}, u32[]{:S(2)}, u32[]{:S(2)}) collective-permute-start(f32[64,128]{1,0:T(8,128)S(1)} %means.1.means_ref), channel_id=1, source_target_pairs={{1,0},{2,1},{3,2},{4,3},{5,4},{6,5},{7,6},{0,7},{9,8},{10,9},{11,1... | collective-permute-start | bytes 98312 | tf_op jit(solution)/shard_map/ppermute | solution.py:658
  7.7 0.0 copy-start.20
  7.7 0.8 %copy-done.20 = f32[58,64]{1,0:T(8,128)S(1)} copy-done((f32[58,64]{1,0:T(8,128)S(1)}, f32[58,64]{1,0:T(8,128)}, u32[]{:S(2)}) %copy-start.20) | copy-done | bytes 14872
  8.5 0.0 copy-start.21
  8.5 0.7 copy-done.21
  9.1 0.0 copy-start.23
  9.1 0.7 copy-done.23
  9.8 0.0 copy-start.24
  9.8 0.7 copy-done.24
  10.5 0.0 copy-start.25
  10.5 0.7 copy-done.25
  11.2 1.1 %host.1 = (f32[256,128]{1,0:T(8,128)S(1)}, bf16[256,128]{1,0:T(8,128)(2,1)S(1)}, bf16[192,128]{1,0:T(8,128)(2,1)S(1)}, f32[192,128]{1,0:T(8,128)S(1)}, f32[256,1...) custom-call(f32[256,128]{1,0:T(8,128)S(1)} %copy-done.6, f32[64,128]{1,0:T(8,128)S(1)} %means.1.means_ref, ...), custom_call_target="tpu_custom_call" | custom-call | tf_op jit(solution)/shard_map/host/pallas_call | solution.py:620
  12.3 0.0 copy-start.7
  12.3 0.6 copy-done.7
  12.9 0.0 copy-start.12
  12.9 0.6 copy-done.12
  13.5 0.0 copy-start.14
  13.5 0.0 collective-permute-done.left_ref
  13.5 0.0 collective-permute-done.1.right_ref
  13.5 1.1 %pack.1 = f32[192,128]{1,0:T(8,128)} custom-call(bf16[192,128]{1,0:T(8,128)(2,1)S(1)} %get-tuple-element.21.wanted_ref, f32[64,128]{1,0:T(8,128)S(1)} %collective-permute-done.left_ref, f32[64,128]{1,0:T(8,128)S(1)} %collective-permute-done.1.right_ref, f32[1,128]{1,0:T(1,128)S(1)} %bitcast.15, f32[192,128]{1,0:T(8,128)S(1)} %get-tuple-element.22.constant_ref, ...), custom_call_target="tpu_custom_call" | custom-call | tf_op jit(solution)/shard_map/pack/pallas_call | solution.py:620
  14.6 0.0 copy-done.14
  14.6 3.4 %all-to-all-start = ((f32[8,24,128]{2,1,0:T(8,128)}), f32[8,24,128]{2,1,0:T(8,128)S(1)}, u32[]{:S(2)}, u32[]{:S(2)}) async-start(f32[8,24,128]{2,1,0:T(8,128)} %bitcast.4), calls=%async_computation | async-start | bytes 196608 | tf_op jit(solution)/shard_map/all_to_all | solution.py:695
  18.0 0.0 copy-start
  18.0 1.5 %copy-done = bf16[1,2,58,32,168]{4,3,2,1,0:T(8,128)(2,1)S(1)} copy-done((bf16[1,2,58,32,168]{4,3,2,1,0:T(8,128)(2,1)S(1)}, bf16[1,2,58,32,168]{4,3,2,1,0:T(8,128)(2,1)}, u32[]{:S(2)}) %copy-start) | copy-done | bytes 1247256
  19.5 0.0 copy-start.26
  19.5 0.7 copy-done.26
  20.2 5.3 %prepare.1 = (f32[2,88,32,128]{3,2,1,0:T(8,128)S(1)}, f32[2,88,128]{2,1,0:T(8,128)S(1)}, f32[88,128]{1,0:T(8,128)S(1)}, bf16[192,512]{1,0:T(8,128)(2,1)S(1)}) custom-call(bf16[2,58,32,168]{3,2,1,0:T(8,128)(2,1)S(1)} %bitcast.10, f32[58]{0:T(128)S(1)} %copy-done.26), custom_call_target="tpu_custom_call" | custom-call | tf_op jit(solution)/shard_map/prepare/pallas_call | solution.py:620
  25.5 0.0 copy-start.10
  25.5 0.6 copy-done.10
  26.1 0.0 copy-start.18
  26.1 0.6 copy-done.18
  26.7 0.0 all-to-all-done
  26.7 0.0 copy-start.11
  26.7 0.9 %copy-done.11 = f32[2,88,128]{2,1,0:T(8,128)S(1)} copy-done((f32[2,88,128]{2,1,0:T(8,128)S(1)}, f32[2,88,128]{2,1,0:T(8,128)}, u32[]{:S(2)}) %copy-start.11) | copy-done | bytes 90136
  27.6 0.0 copy-start.15
  27.6 0.8 %copy-done.15 = f32[128,128]{1,0:T(8,128)S(1)} copy-done((f32[128,128]{1,0:T(8,128)S(1)}, f32[128,128]{1,0:T(8,128)}, u32[]{:S(2)}) %copy-start.15) | copy-done | bytes 65560
  28.5 0.0 copy-start.19
  28.5 0.8 %copy-done.19 = f32[88,128]{1,0:T(8,128)S(1)} copy-done((f32[88,128]{1,0:T(8,128)S(1)}, f32[88,128]{1,0:T(8,128)}, u32[]{:S(2)}) %copy-start.19) | copy-done | bytes 45080
  29.3 5.3 %water.1 = (f32[88,32,128]{2,1,0:T(8,128)S(1)}, f32[4,88,32,128]{3,2,1,0:T(8,128)S(1)}, f32[4,88,128]{2,1,0:T(8,128)S(1)}, f32[88,128]{1,0:T(8,128)S(1)}, f32[192,128]{1,0:T(8,128)S(1)}) custom-call(f32[192,128]{1,0:T(8,128)S(1)} %bitcast.12, bf16[192,512]{1,0:T(8,128)(2,1)S(1)} %get-tuple-element.24.places_ref, ...), custom_call_target="tpu_custom_call" | custom-call | tf_op jit(solution)/shard_map/water/pallas_call | solution.py:620
  34.6 0.0 copy-start.2
  34.6 2.5 %copy-done.2 = f32[4,88,32,128]{3,2,1,0:T(8,128)} copy-done((f32[4,88,32,128]{3,2,1,0:T(8,128)}, f32[4,88,32,128]{3,2,1,0:T(8,128)S(1)}, u32[]{:S(2)}) %copy-start.2) | copy-done | bytes 5767192
  37.1 0.0 copy-start.4
  37.1 1.1 %copy-done.4 = f32[88,32,128]{2,1,0:T(8,128)} copy-done((f32[88,32,128]{2,1,0:T(8,128)}, f32[88,32,128]{2,1,0:T(8,128)S(1)}, u32[]{:S(2)}) %copy-start.4) | copy-done | bytes 1441816
  38.1 0.0 copy-start.9
  38.2 0.6 copy-done.9
  38.8 0.0 copy-start.16
  38.8 0.6 copy-done.16
  39.4 5.9 %all-to-all-start.1 = ((f32[8,24,128]{2,1,0:T(8,128)}), f32[8,24,128]{2,1,0:T(8,128)}, u32[]{:S(2)}, u32[]{:S(2)}) async-start(f32[8,24,128]{2,1,0:T(8,128)} %bitcast.13), calls=%async_computation.1 | async-start | bytes 196608 | tf_op jit(solution)/shard_map/all_to_all | solution.py:753
  45.3 0.0 copy-start.1
  45.3 1.5 %copy-done.1 = bf16[1,2,58,32,168]{4,3,2,1,0:T(8,128)(2,1)S(1)} copy-done((bf16[1,2,58,32,168]{4,3,2,1,0:T(8,128)(2,1)S(1)}, bf16[1,2,58,32,168]{4,3,2,1,0:T(8,128)(2,1)}, u32[]{:S(2)}) %copy-start.1) | copy-done | bytes 1247256
  46.9 0.0 copy-start.3
  46.9 2.6 %copy-done.3 = f32[4,88,32,128]{3,2,1,0:T(8,128)S(1)} copy-done((f32[4,88,32,128]{3,2,1,0:T(8,128)S(1)}, f32[4,88,32,128]{3,2,1,0:T(8,128)}, u32[]{:S(2)}) %copy-start.3) | copy-done | bytes 5767192
  49.5 1.4 %copy-done.5 = f32[88,32,128]{2,1,0:T(8,128)S(1)} copy-done((f32[88,32,128]{2,1,0:T(8,128)S(1)}, f32[88,32,128]{2,1,0:T(8,128)}, u32[]{:S(2)}) %copy-start.5) | copy-done | bytes 1441816
  50.9 0.8 %copy-done.17 = f32[88,128]{1,0:T(8,128)S(1)} copy-done((f32[88,128]{1,0:T(8,128)S(1)}, f32[88,128]{1,0:T(8,128)}, u32[]{:S(2)}) %copy-start.17) | copy-done | bytes 45080
  51.7 11.5 %energy.1 = bf16[2,58,32,168]{3,2,1,0:T(8,128)(2,1)} custom-call(bf16[2,58,32,168]{3,2,1,0:T(8,128)(2,1)S(1)} %bitcast.11, f32[2,88,32,128]{3,2,1,0:T(8,128)S(1)} %get-tuple-element.25.moved_ref, f32[88,32,128]{2,1,0:T(8,128)S(1)} %copy-done.5, f32[4,88,32,128]{3,2,1,0:T(8,128)S(1)} %copy-done.3, f32[4,88,128]{2,1,0:T(8,128)S(1)} %get-tuple-element.32.offsets_ref, ...), custom_call_target="tpu_custom_call" | custom-call | tf_op jit(solution)/shard_map/energy/pallas_call | solution.py:620
  63.1 0.0 all-to-all-done.1
  63.1 6.8 %all_gather.7.gathered_ref = f32[4,192,128]{2,1,0:T(8,128)S(1)} all-gather(f32[1,192,128]{2,1,0:T(8,128)} %bitcast.8), channel_id=1, replica_groups=mesh['sec'=4,'col'=8] {'sec'}, dimensions={0}, use_global_device_ids=true | all-gather | bytes 491520 | tf_op jit(solution)/shard_map/all_gather | solution.py:783
  69.9 0.0 copy-done.8
  69.9 0.0 copy-done.13
  69.9 0.0 copy-done.22
  69.9 1.2 %final.1 = f32[256,128]{1,0:T(8,128)} custom-call(f32[256,128]{1,0:T(8,128)S(1)} %get-tuple-element.18.base_ref, bf16[256,128]{1,0:T(8,128)(2,1)S(1)} %copy-done.13, f32[64,128]{1,0:T(8,128)S(1)} %collective-permute-done.left_ref, f32[64,128]{1,0:T(8,128)S(1)} %collective-permute-done.1.right_ref, f32[1,128]{1,0:T(1,128)S(1)} %bitcast.16, ...), custom_call_target="tpu_custom_call" | custom-call | tf_op jit(solution)/shard_map/final/pallas_call | solution.py:620
  (6 shorter events, 0.0 us)
Async XLA Ops:
  0.6 0.9 %copy-start.6 = (f32[256,128]{1,0:T(8,128)S(1)}, f32[256,128]{1,0:T(8,128)}, u32[]{:S(2)}) copy-start(f32[256,128]{1,0:T(8,128)} %columns_ref.3) | copy-start | bytes 393220
  1.5 12.0 %collective-permute-start = (f32[64,128]{1,0:T(8,128)S(1)}, f32[64,128]{1,0:T(8,128)S(1)}, u32[]{:S(2)}, u32[]{:S(2)}) collective-permute-start(f32[64,128]{1,0:T(8,128)S(1)} %means.1.means_ref), channel_id=1, source_target_pairs={{0,1},{1,2},{2,3},{3,4},{4,5},{5,6},{6,7},{7,0},{8,9},{9,10},{10,1... | collective-permute-start | bytes 98312 | tf_op jit(solution)/shard_map/ppermute | solution.py:657
  4.6 8.9 %collective-permute-start.1 = (f32[64,128]{1,0:T(8,128)S(1)}, f32[64,128]{1,0:T(8,128)S(1)}, u32[]{:S(2)}, u32[]{:S(2)}) collective-permute-start(f32[64,128]{1,0:T(8,128)S(1)} %means.1.means_ref), channel_id=1, source_target_pairs={{1,0},{2,1},{3,2},{4,3},{5,4},{6,5},{7,6},{0,7},{9,8},{10,9},{11,1... | collective-permute-start | bytes 98312 | tf_op jit(solution)/shard_map/ppermute | solution.py:658
  7.7 0.8 %copy-start.20 = (f32[58,64]{1,0:T(8,128)S(1)}, f32[58,64]{1,0:T(8,128)}, u32[]{:S(2)}) copy-start(f32[58,64]{1,0:T(8,128)} %map_ref.1) | copy-start | bytes 44548
  8.5 0.7 copy-start.21
  9.1 0.7 copy-start.23
  9.8 0.7 copy-start.24
  10.5 0.7 copy-start.25
  12.3 0.7 copy-start.7
  12.9 0.6 copy-start.12
  13.5 1.1 %copy-start.14 = (f32[128,128]{1,0:T(8,128)}, f32[128,128]{1,0:T(8,128)S(1)}, u32[]{:S(2)}) copy-start(f32[128,128]{1,0:T(8,128)S(1)} %get-tuple-element.28.unfold_ref) | copy-start | bytes 196612
  14.6 12.1 %all-to-all-start = ((f32[8,24,128]{2,1,0:T(8,128)}), f32[8,24,128]{2,1,0:T(8,128)S(1)}, u32[]{:S(2)}, u32[]{:S(2)}) async-start(f32[8,24,128]{2,1,0:T(8,128)} %bitcast.4), calls=%async_computation | async-start | bytes 196608 | tf_op jit(solution)/shard_map/all_to_all | solution.py:695
  18.0 1.5 %copy-start = (bf16[1,2,58,32,168]{4,3,2,1,0:T(8,128)(2,1)S(1)}, bf16[1,2,58,32,168]{4,3,2,1,0:T(8,128)(2,1)}, u32[]{:S(2)}) copy-start(bf16[1,2,58,32,168]{4,3,2,1,0:T(8,128)(2,1)} %param.13) | copy-start | bytes 3741700
  19.5 0.7 copy-start.26
  25.5 0.6 copy-start.10
  26.1 0.6 copy-start.18
  26.7 0.9 %copy-start.11 = (f32[2,88,128]{2,1,0:T(8,128)S(1)}, f32[2,88,128]{2,1,0:T(8,128)}, u32[]{:S(2)}) copy-start(f32[2,88,128]{2,1,0:T(8,128)} %copy-done.10) | copy-start | bytes 270340
  27.6 0.8 %copy-start.15 = (f32[128,128]{1,0:T(8,128)S(1)}, f32[128,128]{1,0:T(8,128)}, u32[]{:S(2)}) copy-start(f32[128,128]{1,0:T(8,128)} %copy-done.14) | copy-start | bytes 196612
  28.5 0.8 %copy-start.19 = (f32[88,128]{1,0:T(8,128)S(1)}, f32[88,128]{1,0:T(8,128)}, u32[]{:S(2)}) copy-start(f32[88,128]{1,0:T(8,128)} %copy-done.18) | copy-start | bytes 135172
  34.6 2.5 %copy-start.2 = (f32[4,88,32,128]{3,2,1,0:T(8,128)}, f32[4,88,32,128]{3,2,1,0:T(8,128)S(1)}, u32[]{:S(2)}) copy-start(f32[4,88,32,128]{3,2,1,0:T(8,128)S(1)} %get-tuple-element.31.spill_ref) | copy-start | bytes 17301508
  37.1 1.1 %copy-start.4 = (f32[88,32,128]{2,1,0:T(8,128)}, f32[88,32,128]{2,1,0:T(8,128)S(1)}, u32[]{:S(2)}) copy-start(f32[88,32,128]{2,1,0:T(8,128)S(1)} %get-tuple-element.30.water_ref) | copy-start | bytes 4325380
  38.1 0.6 copy-start.9
  38.8 0.6 copy-start.16
  39.4 23.7 %all-to-all-start.1 = ((f32[8,24,128]{2,1,0:T(8,128)}), f32[8,24,128]{2,1,0:T(8,128)}, u32[]{:S(2)}, u32[]{:S(2)}) async-start(f32[8,24,128]{2,1,0:T(8,128)} %bitcast.13), calls=%async_computation.1 | async-start | bytes 196608 | tf_op jit(solution)/shard_map/all_to_all | solution.py:753
  45.3 1.5 %copy-start.1 = (bf16[1,2,58,32,168]{4,3,2,1,0:T(8,128)(2,1)S(1)}, bf16[1,2,58,32,168]{4,3,2,1,0:T(8,128)(2,1)}, u32[]{:S(2)}) copy-start(bf16[1,2,58,32,168]{4,3,2,1,0:T(8,128)(2,1)} %param.13) | copy-start | bytes 3741700
  46.9 2.6 %copy-start.3 = (f32[4,88,32,128]{3,2,1,0:T(8,128)S(1)}, f32[4,88,32,128]{3,2,1,0:T(8,128)}, u32[]{:S(2)}) copy-start(f32[4,88,32,128]{3,2,1,0:T(8,128)} %copy-done.2) | copy-start | bytes 17301508
  49.5 1.4 %copy-start.5 = (f32[88,32,128]{2,1,0:T(8,128)S(1)}, f32[88,32,128]{2,1,0:T(8,128)}, u32[]{:S(2)}) copy-start(f32[88,32,128]{2,1,0:T(8,128)} %copy-done.4) | copy-start | bytes 4325380
  50.9 0.8 %copy-start.17 = (f32[88,128]{1,0:T(8,128)S(1)}, f32[88,128]{1,0:T(8,128)}, u32[]{:S(2)}) copy-start(f32[88,128]{1,0:T(8,128)} %copy-done.16) | copy-start | bytes 135172
  51.6 18.3 %copy-start.8 = (f32[256,128]{1,0:T(8,128)S(1)}, f32[256,128]{1,0:T(8,128)}, u32[]{:S(2)}) copy-start(f32[256,128]{1,0:T(8,128)} %copy-done.7) | copy-start | bytes 393220
  51.6 18.3 %copy-start.13 = (bf16[256,128]{1,0:T(8,128)(2,1)S(1)}, bf16[256,128]{1,0:T(8,128)(2,1)}, u32[]{:S(2)}) copy-start(bf16[256,128]{1,0:T(8,128)(2,1)} %copy-done.12) | copy-start | bytes 196612
  51.7 18.3 %copy-start.22 = (f32[128]{0:T(128)S(1)}, f32[128]{0:T(128)}, u32[]{:S(2)}) copy-start(f32[128]{0:T(128)} %param.9) | copy-start | bytes 1540

commit v3 on v2

v3 whole, which is shorter than its diff:
```python
import functools

import jax
import jax.numpy as jnp
from jax import lax
from jax.experimental import pallas as pl
from jax.experimental.pallas import tpu as pltpu
from jax.sharding import PartitionSpec as P

MAX_SUB = 4
RELAX = 0.25
HORIZ = 0.12
VERTIC = 0.1
LATENT = 2.5
VMIX = 0.2
HIGH = lax.Precision.HIGHEST
LANES = 128
F32 = jnp.float32
BF16 = jnp.bfloat16
STEP = 10
SHRINK = 1.0 / LATENT
I32 = jnp.int32


def iota(shape, dim):
    return lax.broadcasted_iota(I32, shape, dim)


def mm(a, b, contract, precision=HIGH):
    return lax.dot_general(
        a, b, (contract, ((), ())), precision=precision, preferred_element_type=F32
    )


NN = ((1,), (0,))
NT = ((1,), (1,))
TN = ((0,), (0,))


def divided(value, by):
    return jnp.floor((value.astype(F32) + 0.5) * (1.0 / by)).astype(I32)


def split(values):
    high = values.astype(BF16)
    rest = values - high.astype(F32)
    middle = rest.astype(BF16)
    low = (rest - middle.astype(F32)).astype(BF16)
    return low, middle, high


def select(picks, values, contract, swap=False):
    total = None
    for part in split(values):
        a, b = (part, picks) if swap else (picks, part)
        term = lax.dot_general(a, b, (contract, ((), ())), preferred_element_type=F32)
        total = term if total is None else total + term
    return total


def vertical_mix(values, levels):
    upper = jnp.concatenate([values[1:levels], values[levels - 1 : levels]], axis=0)
    lower = jnp.concatenate([values[0:1], values[0 : levels - 1]], axis=0)
    inner = values[0:levels]
    return inner + VERTIC * (upper + lower - 2.0 * inner)


def means_kernel(columns_ref, means_ref):
    elements = means_ref.shape[0]
    total = columns_ref[pl.ds(0, elements, stride=4), :]
    for k in range(1, 4):
        total = total + columns_ref[pl.ds(k, elements, stride=4), :]
    means_ref[...] = 0.25 * total


def host_kernel(
    columns_ref,
    means_ref,
    mixing_ref,
    neighbours_ref,
    targets_ref,
    substeps_ref,
    map_ref,
    base_ref,
    sides_ref,
    wanted_ref,
    constant_ref,
    slots_ref,
    fold_ref,
    unfold_ref,
    *,
    col_count,
    padded,
    clouds,
):
    section = lax.axis_index("sec")
    position = lax.axis_index("col")
    rows, width = columns_ref.shape
    levels = map_ref.shape[1]
    cloud_levels = map_ref.shape[0]
    elements = rows // 4
    block = col_count * padded
    near = neighbours_ref[...] - (position - 1) * elements
    near = jnp.where(near < 0, near + elements * col_count, near)
    near = jnp.where(near >= elements * col_count, near - elements * col_count, near)
    window = iota((3 * elements, elements), 0)
    picks = jnp.where(window == iota((3 * elements, elements), 1) + elements, -4.0, 0.0)
    for k in range(near.shape[0]):
        picks = picks + jnp.where(window == near[k : k + 1, :], 1.0, 0.0)
    row_element = divided(iota((rows, elements), 0), 4)
    spread_rows = jnp.where(row_element == iota((rows, elements), 1), 1.0, 0.0)
    weights = mm(spread_rows.astype(BF16), picks.astype(BF16), NT, None)
    sides = jnp.concatenate([weights[:, :elements], weights[:, 2 * elements :]], axis=1)
    sides = sides.astype(BF16)
    sides_ref[...] = sides
    own = select(weights[:, elements : 2 * elements].astype(BF16), means_ref[...], NN)
    values = columns_ref[...]
    lane = iota((rows, width), 1)
    level = lane - levels * divided(lane, levels)
    upper = jnp.where(level == levels - 1, values, pltpu.roll(values, width - 1, 1))
    lower = jnp.where(level == 0, values, pltpu.roll(values, 1, 1))
    base = values + mixing_ref[...] * own + VMIX * (upper + lower - 2.0 * values)
    base_ref[...] = base
    targets = targets_ref[...]
    onehot = jnp.where(iota((clouds, rows), 0) == targets, 1.0, 0.0)
    before = jnp.where(iota((rows, rows), 0) < iota((rows, rows), 1), 1.0, 0.0)
    running = mm(onehot.astype(BF16), before.astype(BF16), NN, None)
    ranks = jnp.sum(running * onehot, axis=0, keepdims=True).astype(I32)
    owner = divided(targets, col_count)
    slot = (targets - owner * col_count) * padded + ranks
    mine = jnp.where(owner + 1 == section, slot, -1)
    pack = jnp.where(iota((block, rows), 0) == mine, 1.0, 0.0).astype(BF16)
    wanted_ref[...] = mm(pack, sides, NN, None).astype(BF16)
    plain = map_ref[...]
    folded = RELAX * vertical_mix(plain, cloud_levels)
    for ref, value in ((fold_ref, folded), (unfold_ref, plain)):
        ref[...] = jnp.zeros_like(ref)
        for f in range(width // levels):
            ref[f * levels : f * levels + cloud_levels, f * levels : (f + 1) * levels] = value
    count_rows = jnp.where(
        iota((width, rows), 0) == levels - 1, substeps_ref[...].astype(F32), 0.0
    )
    counts = mm(pack, count_rows.astype(BF16), NT, None)
    constant_ref[...] = mm(select(pack, base, NN), fold_ref[...], NT) + counts
    fold_ref[...] = fold_ref[...] * mixing_ref[...]
    everywhere = jnp.broadcast_to((owner * block + slot).astype(F32), (LANES, rows))
    identity = jnp.where(iota((rows, rows), 0) == iota((rows, rows), 1), 1.0, 0.0)
    slots_ref[...] = select(identity.astype(BF16), everywhere, NT)


def pack_kernel(wanted_ref, left_ref, right_ref, constant_ref, fold_ref, out_ref):
    halo = jnp.concatenate([left_ref[...], right_ref[...]], axis=0)
    spread = select(wanted_ref[...], halo, NN)
    out_ref[...] = constant_ref[...] + mm(spread, fold_ref[...], NT)


class Segment:
    def __init__(self, lane0, width, levels, begin):
        self.lane0, self.width, self.begin, self.levels = lane0, width, begin, levels
        self.steps = -(-levels // (LANES // width))
        self.groups = -(-levels // self.steps)
        self.missing = self.groups * self.steps - levels
        self.blocks = -(-self.steps // STEP)
        self.rows = (begin + 1, begin + 1 + self.steps)

    def group_steps(self, g):
        return self.steps - (self.missing if g == self.groups - 1 else 0)


def segments_of(slots, levels):
    segments, begin = [], 0
    for lane0 in range(0, slots, LANES):
        segments.append(Segment(lane0, min(LANES, slots - lane0), levels, begin))
        begin += segments[-1].steps + 2
    rows = max([begin] + [s.begin + 2 + s.blocks * STEP for s in segments])
    return segments, rows, -(-rows // 8) * 8


def fill_spare(segments, load, store):
    def turned(value, shift):
        tall = jnp.broadcast_to(value, (8, LANES)) if value.shape[0] == 1 else value
        return pltpu.roll(tall, shift % LANES, 1)[: value.shape[0]]

    for s in segments:
        if s.missing:
            row = s.rows[1] - s.missing
            value = load(row - 1)
            lane = iota(value.shape, 1)
            store(row, jnp.where(lane >= (s.groups - 1) * s.width, value, load(row)))
        first, last = load(s.rows[0]), load(s.rows[1] - 1)
        before, after = first, last
        if s.groups > 1:
            lane = iota(first.shape, 1)
            before = jnp.where(lane < s.width, first, turned(last, s.width))
            after = jnp.where(lane < (s.groups - 1) * s.width, turned(first, -s.width), last)
        store(s.begin, before)
        store(s.rows[1], after)


def fill_wide(segments, ref):
    def store(row, value):
        ref[row] = value

    fill_spare(segments, lambda row: ref[row], store)


def fill_flat(segments, ref):
    def store(row, value):
        ref[row : row + 1, :] = value

    fill_spare(segments, lambda row: ref[row : row + 1, :], store)


def linear(below, here, above):
    east = [pltpu.roll(here[3], 1, 0), here[0], here[1], here[2]]
    west = [here[1], here[2], here[3], pltpu.roll(here[0], 7, 0)]
    keep = (1.0 - 2.0 * HORIZ - 2.0 * VERTIC) / VERTIC
    return [
        (below[j] + above[j]) + ((HORIZ / VERTIC) * (east[j] + west[j]) + keep * here[j])
        for j in range(4)
    ]


def groups(ref, index):
    return [ref[index + (pl.ds(8 * j, 8),)] for j in range(4)]


def strided(ref, row):
    return [ref[row, pl.ds(j, 8, stride=4), :] for j in range(4)]


def sweep(segment, load, work):
    def block(i, carry):
        row = segment.begin + i * STEP
        held = [load(row), load(row + 1)]
        for k in range(STEP):
            held.append(load(row + k + 2))
            work(row + k + 1, held[k], held[k + 1], held[k + 2])
        return carry

    lax.fori_loop(0, segment.blocks, block, 0)


def each(count, size, work):
    size = min(size, count)

    def run(first):
        for k in range(size):
            work(first + k)

    if count // size:
        lax.fori_loop(0, count // size, lambda i, c: (run(i * size), c)[1], 0)
    if count % size:
        run(count - size)


def widen(state_ref, natural_ref, segments, scale):
    levels, columns, _ = state_ref.shape
    for s in segments:
        at = slice(s.lane0, s.lane0 + s.width)

        def one(k):
            parts = []
            for g in range(s.groups):
                level = jnp.minimum(g * s.steps + k, levels - 1)
                parts.append(state_ref[level, :, at].astype(F32))
            spare = LANES - s.groups * s.width
            if spare:
                parts.append(jnp.zeros((columns, spare), F32))
            value = jnp.concatenate(parts, axis=1) if len(parts) > 1 else parts[0]
            natural_ref[s.begin + 1 + k] = scale * value if scale != 1.0 else value

        each(s.steps, STEP, one)


def folded_sums(sums_ref, columns):
    rows = sums_ref.shape[0] // 8
    total = sums_ref[pl.ds(0, rows, stride=8), :]
    for k in range(1, 8):
        total = total + sums_ref[pl.ds(k, rows, stride=8), :]
    return total * (1.0 / columns)


def slab(row):
    return pl.ds(pl.multiple_of(row * 8, 8), 8)


def spread_row(ref, row):
    return jnp.broadcast_to(ref[pl.ds(row, 1), :], (8, LANES))


def lane_places(segments):
    return [(s, g) for s in segments for g in range(s.groups)]


def slot_map(segments, block, capacity, padded):
    tiles = []
    for s, g in lane_places(segments):
        lane = iota((8, LANES), 1) - g * s.width
        slot = s.lane0 + lane
        row = slot + (padded - capacity) * divided(jnp.maximum(slot, 0), capacity)
        row = jnp.where((lane >= 0) & (lane < s.width), row, -1)[0:1]
        tiles.append(jnp.where(iota((block, LANES), 0) == row, 1.0, 0.0).astype(BF16))
    return jnp.concatenate(tiles, axis=1)


def prepare_kernel(
    state_ref,
    saturation_ref,
    moved_ref,
    means_ref,
    limits_ref,
    state_buf,
    natural_ref,
    sums_ref,
    flat_ref,
    sems,
    *,
    segments,
):
    fields, levels, columns, _ = state_ref.shape
    loads = [
        pltpu.make_async_copy(state_ref.at[f], state_buf.at[f], sems.at[f]) for f in range(fields)
    ]
    loads[1].start()
    loads[0].start()
    tall = flat_ref.shape[0]
    here = iota((tall, levels), 0) == iota((tall, levels), 1)
    diagonal = jnp.where(here, 0.5 * saturation_ref[...], 0.0)
    flat_ref[...] = select(jnp.ones((levels, LANES), BF16), diagonal, NN, swap=True)
    limits_ref[...] = jnp.zeros_like(limits_ref)
    for s in segments:
        lane = iota((s.steps, LANES), 1)
        value = flat_ref[0 : s.steps, :]
        for g in range(1, s.groups):
            other = flat_ref[g * s.steps : (g + 1) * s.steps, :]
            value = jnp.where(lane >= g * s.width, other, value)
        limits_ref[s.rows[0] : s.rows[1], :] = value
    sums_ref[...] = jnp.zeros_like(sums_ref)
    loads[1].wait()
    widen(state_buf.at[1], natural_ref, segments, 1.0)
    fill_wide(segments, natural_ref)
    for s in segments:

        def work(row, below, here, above):
            out = linear(below, here, above)
            for j in range(4):
                moved_ref[row, pl.ds(8 * j, 8), :] = out[j]
            sums_ref[slab(row), :] = (here[0] + here[1]) + (here[2] + here[3])

        sweep(s, lambda row: strided(natural_ref, row), work)
    means_ref[1] = folded_sums(sums_ref, columns)
    loads[0].wait()
    widen(state_buf.at[0], natural_ref, segments, 1.0)
    for s in segments:

        def total(k):
            value = groups(natural_ref, (s.begin + 1 + k,))
            sums_ref[slab(s.begin + 1 + k), :] = (value[0] + value[1]) + (value[2] + value[3])

        each(s.steps, STEP, total)
    means_ref[0] = folded_sums(sums_ref, columns)


def water_kernel(
    received_ref,
    moved_ref,
    means_ref,
    limits_ref,
    unfold_far,
    water_far,
    spill_far,
    flats_far,
    back_far,
    unfold_ref,
    even_ref,
    odd_ref,
    spill_buf,
    flats_ref,
    goal_ref,
    mean_ref,
    shift_ref,
    limit_ref,
    sums_ref,
    change_ref,
    back_ref,
    in_sem,
    spill_sems,
    water_sem,
    flat_sem,
    back_sems,
    *,
    segments,
    capacity,
    padded,
    stride,
):
    rows = means_ref.shape[1]
    columns = even_ref.shape[1]
    load = pltpu.make_async_copy(unfold_far, unfold_ref, in_sem)
    load.start()
    places = slot_map(segments, received_ref.shape[0], capacity, padded)
    arrived = select(places, received_ref[...], TN, swap=True)
    goal_ref[...] = jnp.zeros_like(goal_ref)
    flats_ref[...] = jnp.zeros_like(flats_ref)
    sums_ref[...] = jnp.zeros_like(sums_ref)
    counts = flats_ref.at[MAX_SUB + 2]
    for s in segments:
        count = None
        for t, (owner, g) in enumerate(lane_places(segments)):
            if owner is not s:
                continue
            lanes = slice(t * LANES, (t + 1) * LANES)
            number = s.group_steps(g)
            for f in range(2):
                first = f * stride + g * s.steps
                at = slice(s.rows[0], s.rows[0] + number)
                goal_ref[f, at, :] = goal_ref[f, at, :] + arrived[first : first + number, lanes]
            part = arrived[stride - 1 : stride, lanes]
            count = part if count is None else count + part
        counts[s.rows[0] : s.rows[1], :] = jnp.broadcast_to(count, (s.steps, LANES))
    for f in range(2):
        mean_ref[f] = means_ref[f]
    copies = []
    source, target = None, even_ref
    for n in range(MAX_SUB):
        scale = 10.0 ** (n + 1)
        last = n + 1 == MAX_SUB
        expected = []
        for f in range(2):
            fill_flat(segments, mean_ref.at[f])
            mean = mean_ref[f]
            mixed = mean + VERTIC * (
                pltpu.roll(mean, 1, 0) + pltpu.roll(mean, rows - 1, 0) - 2.0 * mean
            )
            offset = goal_ref[f] - RELAX * mixed
            expected.append(mixed + offset)
            if f == 1:
                shift_ref[...] = scale * offset
            else:
                flats_ref[n] = (scale * SHRINK) * offset
        limit_ref[...] = scale * limits_ref[...]
        if last:
            flats_ref[MAX_SUB] = shift_ref[...]
            flats_ref[MAX_SUB + 1] = limit_ref[...]
            copies.append(pltpu.make_async_copy(flats_ref, flats_far, flat_sem))
            copies[-1].start()
        for s in segments:
            active = spread_row(counts, s.rows[0]) > float(n)

            def finish(row, lin, old):
                shift = spread_row(shift_ref, row)
                limit = spread_row(limit_ref, row)
                total = None
                for j in range(4):
                    v = lin[j] + shift
                    c = jnp.maximum(0.5 * v - limit, 0.0)
                    total = c if total is None else total + c
                    if last:
                        continue
                    u = v - c
                    if old is not None:
                        u = jnp.where(active, u, old[j])
                    spill_buf[n, row, pl.ds(8 * j, 8), :] = c
                    target[row, pl.ds(8 * j, 8), :] = u
                sums_ref[slab(row), :] = total

            if n == 0:

                def block(i, carry):
                    for k in range(STEP):
                        row = s.begin + 1 + i * STEP + k
                        finish(row, groups(moved_ref, (row,)), None)
                    return carry

                lax.fori_loop(0, s.blocks, block, 0)
            else:

                def work(row, below, here, above):
                    finish(row, linear(below, here, above), here)

                sweep(s, lambda row: groups(source, (row,)), work)
        if not last:
            copies.append(
                pltpu.make_async_copy(spill_buf.at[n], spill_far.at[n], spill_sems.at[n])
            )
            copies[-1].start()
            fill_wide(segments, target)
            source, target = target, (odd_ref if target is even_ref else even_ref)
        if n + 2 == MAX_SUB:
            copies.append(pltpu.make_async_copy(source, water_far, water_sem))
            copies[-1].start()
        spilled = folded_sums(sums_ref, columns) * (1.0 / scale)
        step = [expected[0] + LATENT * spilled, expected[1] - spilled]
        keep = counts[...] > float(n)
        for f in range(2):
            mean_ref[f] = jnp.where(keep, step[f], mean_ref[f])
    change_ref[...] = jnp.zeros_like(change_ref)
    for f in range(2):
        change = mean_ref[f] - means_ref[f]
        for t, (s, g) in enumerate(lane_places(segments)):
            first, number = f * stride + g * s.steps, s.group_steps(g)
            change_ref[first : first + number, t * LANES : (t + 1) * LANES] = change[
                s.rows[0] : s.rows[0] + number
            ]
    spread = select(places, change_ref[...], NT)
    load.wait()
    back = mm(spread, unfold_ref[...], NN)
    for j in range(back_ref.shape[0]):
        back_ref[j] = back[j * padded : j * padded + capacity]
    for i in range(back_far.shape[0]):
        copies.append(pltpu.make_async_copy(back_ref, back_far.at[i], back_sems.at[i]))
        copies[-1].start()
    for copy in copies:
        copy.wait()


def energy_kernel(
    state_ref,
    water_far,
    spill_far,
    flats_far,
    base_ref,
    sides_ref,
    left_ref,
    right_ref,
    mixing_ref,
    homes_ref,
    out_ref,
    advanced_ref,
    places_ref,
    state_buf,
    water_buf,
    spill_buf,
    flats_ref,
    out_buf,
    even_ref,
    odd_ref,
    last_ref,
    natural_ref,
    state_sems,
    water_sem,
    spill_sems,
    flat_sem,
    out_sems,
    *,
    segments,
):
    fields, levels, columns, _ = state_ref.shape
    states = [
        pltpu.make_async_copy(state_ref.at[f], state_buf.at[f], state_sems.at[f])
        for f in range(fields)
    ]
    flats = pltpu.make_async_copy(flats_far, flats_ref, flat_sem)
    waters = pltpu.make_async_copy(water_far, water_buf, water_sem)
    spills = [
        pltpu.make_async_copy(spill_far.at[n], spill_buf.at[n], spill_sems.at[n])
        for n in range(MAX_SUB - 1)
    ]
    leaves = [
        pltpu.make_async_copy(out_buf.at[f], out_ref.at[f], out_sems.at[f]) for f in range(fields)
    ]
    states[0].start()
    flats.start()
    for copy in spills:
        copy.start()
    waters.start()
    states[1].start()
    halo = jnp.concatenate([left_ref[...], right_ref[...]], axis=0)
    advanced_ref[...] = base_ref[...] + mixing_ref[...] * select(sides_ref[...], halo, NN)
    places_ref[...] = homes_ref[...]
    states[0].wait()
    widen(state_buf.at[0], natural_ref, segments, SHRINK)
    fill_wide(segments, natural_ref)
    flats.wait()
    counts = flats_ref.at[MAX_SUB + 2]
    source, target = natural_ref, even_ref
    for n in range(MAX_SUB):
        last = n + 1 == MAX_SUB
        (waters if last else spills[n]).wait()
        for s in segments:
            active = spread_row(counts, s.rows[0]) > float(n)

            def load(row):
                here = strided(source, row) if n == 0 else groups(source, (row,))
                return (here, groups(water_buf, (row,))) if last else (here, None)

            def work(row, below, here, above):
                shift = spread_row(flats_ref.at[n], row)
                lin = linear(below[0], here[0], above[0])
                if last:
                    water = linear(below[1], here[1], above[1])
                    push = spread_row(flats_ref.at[MAX_SUB], row)
                    limit = spread_row(flats_ref.at[MAX_SUB + 1], row)
                else:
                    spill = groups(spill_buf, (n, row))
                for j in range(4):
                    if last:
                        v = water[j] + push
                        c = jnp.maximum(0.5 * v - limit, 0.0)
                        last_ref[row, pl.ds(8 * j, 8), :] = jnp.where(active, v - c, here[1][j])
                    else:
                        c = spill[j]
                    u = (lin[j] + shift) + c
                    if n:
                        u = jnp.where(active, u, here[0][j])
                    target[row, pl.ds(8 * j, 8), :] = u

            sweep(s, load, work)
        if not last:
            fill_wide(segments, target)
        source, target = target, (odd_ref if target is even_ref else even_ref)
    for f in (1, 0):
        states[1].wait() if f == 1 else None
        found = last_ref if f == 1 else source
        for s in segments:
            count = spread_row(counts, s.rows[0])
            back = jnp.zeros((8, LANES), F32)
            for n in range(1, MAX_SUB + 1):
                scale = 10.0**-n * (LATENT if f == 0 else 1.0)
                back = jnp.where(count == float(n), scale, back)

            def permute(k):
                row = s.begin + 1 + k
                value = groups(found, (row,))
                for j in range(4):
                    natural_ref[row, pl.ds(j, 8, stride=4), :] = value[j] * back

            each(s.steps, STEP, permute)
            at = slice(s.lane0, s.lane0 + s.width)
            held = jnp.broadcast_to(count[0:1, : s.width], (columns, s.width)) > 0.0
            for g in range(s.groups):
                lanes = slice(g * s.width, (g + 1) * s.width)

                def narrow(k):
                    level = g * s.steps + k
                    old = state_buf[f, level, :, at].astype(F32)
                    value = jnp.where(held, natural_ref[s.begin + 1 + k, :, lanes], old)
                    out_buf[f, level, :, at] = value.astype(BF16)

                each(s.group_steps(g), STEP, narrow)
        leaves[f].start()
    for f in range(fields):
        leaves[f].wait()


def final_kernel(advanced_ref, places_ref, gathered_ref, out_ref, table_ref, *, levels, idle, padded):
    rows, width = advanced_ref.shape
    sources, capacity, _ = gathered_ref.shape
    if capacity != padded:
        table_ref[...] = jnp.zeros_like(table_ref)
    for j in range(idle, sources):
        first = (j - idle) * padded
        table_ref[first : first + capacity, :] = gathered_ref[j]
    place = places_ref[:, :1].astype(I32)
    picks = jnp.where(iota((rows, table_ref.shape[0]), 1) == place, 1.0, 0.0)
    summed = advanced_ref[...] + select(picks.astype(BF16), table_ref[...], NN)
    water = divided(iota((rows, width), 1), levels) == 1
    out_ref[...] = jnp.where(water, jnp.maximum(summed, 0.0), summed)


SPACES = dict(
    auto=pl.BlockSpec(memory_space=pltpu.VMEM),
    near=pl.BlockSpec(memory_space=pltpu.VMEM),
    far=pl.BlockSpec(memory_space=pl.ANY),
    scalar=pl.BlockSpec(memory_space=pltpu.SMEM),
)


def call(kernel, name, inputs, outputs, scratch=(), limit=8):
    kept = dict(near=pltpu.VMEM, auto=pltpu.HBM, far=pltpu.HBM, scalar=pltpu.HBM)
    arrays = [pltpu.with_memory_space_constraint(x, kept[space]) for space, x in inputs]
    shapes = [kept[space](dims, dtype) for space, dims, dtype in outputs]
    return pl.pallas_call(
        kernel,
        out_shape=shapes,
        in_specs=[SPACES[space] for space, _ in inputs],
        out_specs=[SPACES[space] for space, _, _ in outputs],
        scratch_shapes=list(scratch),
        compiler_params=pltpu.CompilerParams(vmem_limit_bytes=limit << 20),
        name=name,
    )(*arrays)


def body(
    column_state, mixing_rate, neighbours, assignment, substeps, cloud_state, level_map, saturation
):
    col_count = lax.axis_size("col")
    sec_count = lax.axis_size("sec")
    count, width = column_state.shape
    cloud_levels, levels = level_map.shape
    _, fields, _, columns, slots = cloud_state.shape
    elements = count // 4
    capacity = slots // col_count
    padded = -(-capacity // 8) * 8
    block = col_count * padded
    clouds = (sec_count - 1) * col_count
    segments, used, rows = segments_of(slots, cloud_levels)
    mapped = LANES * len(lane_places(segments))
    mixing = mixing_rate.reshape(1, width)
    state = cloud_state[0]
    dma = pltpu.SemaphoreType.DMA

    def wide(*lead):
        return pltpu.VMEM((*lead, rows, columns, LANES), F32)

    (means,) = call(
        means_kernel, "means", [("auto", column_state)], [("near", (elements, width), F32)]
    )
    ring = [(i, (i + 1) % col_count) for i in range(col_count)]
    left = lax.ppermute(means, "col", ring)
    right = lax.ppermute(means, "col", [(j, i) for i, j in ring])

    base, sides, wanted, constant, homes, fold, unfold = call(
        functools.partial(host_kernel, col_count=col_count, padded=padded, clouds=clouds),
        "host",
        [
            ("auto", column_state),
            ("near", means),
            ("auto", mixing),
            ("auto", neighbours.T),
            ("auto", assignment.reshape(1, count)),
            ("auto", substeps.reshape(1, count)),
            ("auto", level_map),
        ],
        [
            ("auto", (count, width), F32),
            ("auto", (count, 2 * elements), BF16),
            ("near", (block, 2 * elements), BF16),
            ("near", (block, width), F32),
            ("auto", (count, LANES), F32),
            ("near", (width, width), F32),
            ("auto", (width, width), F32),
        ],
    )
    (outgoing,) = call(
        pack_kernel,
        "pack",
        [
            ("near", wanted),
            ("near", left),
            ("near", right),
            ("near", constant),
            ("near", fold),
        ],
        [("auto", (block, width), F32)],
    )
    received = lax.all_to_all(outgoing, "col", split_axis=0, concat_axis=0, tiled=True)
    moved, cloud_means, limits = call(
        functools.partial(prepare_kernel, segments=segments),
        "prepare",
        [("far", state), ("auto", saturation.reshape(1, cloud_levels))],
        [
            ("near", (used, columns, LANES), F32),
            ("near", (fields, rows, LANES), F32),
            ("near", (rows, LANES), F32),
        ],
        scratch=[
            pltpu.VMEM(state.shape, BF16),
            wide(),
            pltpu.VMEM((rows * 8, LANES), F32),
            pltpu.VMEM((max(s.groups * s.steps for s in segments), LANES), F32),
            dma((fields,)),
        ],
        limit=16,
    )
    water, spill, flats, back = call(
        functools.partial(
            water_kernel, segments=segments, capacity=capacity, padded=padded, stride=levels
        ),
        "water",
        [
            ("near", received),
            ("near", moved),
            ("near", cloud_means),
            ("near", limits),
            ("far", unfold),
        ],
        [
            ("far", (rows, columns, LANES), F32),
            ("far", (MAX_SUB - 1, rows, columns, LANES), F32),
            ("far", (MAX_SUB + 3, rows, LANES), F32),
            ("far", (sec_count, col_count, capacity, width), F32),
        ],
        scratch=[
            pltpu.VMEM((width, width), F32),
            wide(),
            wide(),
            wide(MAX_SUB - 1),
            pltpu.VMEM((MAX_SUB + 3, rows, LANES), F32),
            pltpu.VMEM((fields, rows, LANES), F32),
            pltpu.VMEM((fields, rows, LANES), F32),
            pltpu.VMEM((rows, LANES), F32),
            pltpu.VMEM((rows, LANES), F32),
            pltpu.VMEM((rows * 8, LANES), F32),
            pltpu.VMEM((width, mapped), F32),
            pltpu.VMEM((col_count, capacity, width), F32),
            dma(()),
            dma((MAX_SUB - 1,)),
            dma(()),
            dma(()),
            dma((sec_count,)),
        ],
        limit=24,
    )
    returned = lax.all_to_all(
        back.reshape(sec_count * col_count, capacity, width),
        ("sec", "col"),
        split_axis=0,
        concat_axis=0,
        tiled=True,
    )
    new_block, advanced, places = call(
        functools.partial(energy_kernel, segments=segments),
        "energy",
        [
            ("far", state),
            ("far", water),
            ("far", spill),
            ("far", flats),
            ("auto", base),
            ("auto", sides),
            ("near", left),
            ("near", right),
            ("auto", mixing),
            ("auto", homes),
        ],
        [
            ("far", state.shape, BF16),
            ("near", (count, width), F32),
            ("near", (count, LANES), F32),
        ],
        scratch=[
            pltpu.VMEM(state.shape, BF16),
            wide(),
            wide(MAX_SUB - 1),
            pltpu.VMEM((MAX_SUB + 3, rows, LANES), F32),
            pltpu.VMEM(state.shape, BF16),
            wide(),
            wide(),
            wide(),
            wide(),
            dma((fields,)),
            dma(()),
            dma((MAX_SUB - 1,)),
            dma(()),
            dma((fields,)),
        ],
        limit=32,
    )
    (new_columns,) = call(
        functools.partial(final_kernel, levels=levels, idle=col_count, padded=padded),
        "final",
        [("near", advanced), ("near", places), ("near", returned)],
        [("auto", (count, width), F32)],
        scratch=[pltpu.VMEM((clouds * padded, width), F32)],
    )
    return new_columns, new_block[None]


def solution(mesh):
    in_specs = (
        P("col", None),
        P(),
        P("col", None),
        P("col", None),
        P("col"),
        P("sec", None, None, None, "col"),
        P(),
        P(),
    )
    out_specs = (P("col", None), P("sec", None, None, None, "col"))
    return jax.shard_map(body, mesh=mesh, in_specs=in_specs, out_specs=out_specs, check_vma=False)
```

time: 71.9 us -> 47.7 us (0.66)
  local copies, waits for them, and re-layouts: 22.7 us -> 0 us
  waiting for transfers between devices: 0.01 us -> 12.9 us
  blocking collectives: 6.77 us -> 0 us
  Pallas kernels: 25.5 us -> 21.6 us
  starting transfers between devices: 15.4 us -> 12.1 us
    unnamed x54 -> x0, local copies, waits for them, and re-layouts: 22.7 us -> none
    all_gather x1 -> x0, blocking collectives: 6.77 us -> none  [body(): gathered = lax.all_gather(returned, 'sec', axis=0, tiled=False)]
    all_to_all x1, waiting for transfers between devices: 0.01 us -> 5.06 us  [body(): lax.all_to_all(back.reshape(sec_count * col_count, capacity, width), ('se...]
    ppermute x1, waiting for transfers between devices: 0.01 us -> 4 us  [body(): left = lax.ppermute(means, 'col', ring)]
    all_to_all x1, waiting for transfers between devices: 0.01 us -> 3.86 us  [body(): lax.all_to_all(outgoing, 'col', split_axis=0, concat_axis=0, tiled=True)]
    pallas_call x7, Pallas kernels: 25.5 us -> 21.6 us  [call(): pl.pallas_call(kernel, out_shape=shapes, in_specs=[SPACES[space] for spac...]
    all_to_all x1, starting transfers between devices: 5.93 us -> 2.61 us  [body(): lax.all_to_all(back.reshape(sec_count * col_count, capacity, width), ('se...]
    ppermute x1, starting transfers between devices: 3.05 us -> 0.01 us  [body(): left = lax.ppermute(means, 'col', ring)]
  transfers between devices with their start and end apart: 4 -> 4, of which waited for: 0 -> 3; matrix products, arithmetic and copies ran while one was open for 0% -> 0% of each run, Pallas kernels for 25% -> 30%
where the time goes in v3:
time: 47.7 us; the launch traced here: 47.3 us
  Pallas kernels  21.6 us (45%)
  waiting for transfers between devices  12.9 us (27%)
  starting transfers between devices  12.1 us (25%)
  between operations  0.68 us (1%)
    pallas_call x7, Pallas kernels, call(): pl.pallas_call(kernel, out_shape=shapes, in_specs=[SPACES[space] for spac...  21.6 us
    ppermute x1, starting transfers between devices, body(): right = lax.ppermute(means, 'col', [(j, i) for i, j in ring])  6.09 us
    all_to_all x1, waiting for transfers between devices, body(): lax.all_to_all(back.reshape(sec_count * col_count, capacity, width), ('se...  5.06 us
    ppermute x1, waiting for transfers between devices, body(): left = lax.ppermute(means, 'col', ring)  4 us
    all_to_all x1, waiting for transfers between devices, body(): lax.all_to_all(outgoing, 'col', split_axis=0, concat_axis=0, tiled=True)  3.86 us
    all_to_all x1, starting transfers between devices, body(): lax.all_to_all(outgoing, 'col', split_axis=0, concat_axis=0, tiled=True)  3.36 us
    all_to_all x1, starting transfers between devices, body(): lax.all_to_all(back.reshape(sec_count * col_count, capacity, width), ('se...  2.61 us
  transfers between devices with their start and end apart: 4, of which 3 were waited for; matrix products, arithmetic and copies ran while one was open for 0% of the time, Pallas kernels for 30%

profile of v3, /device:TPU:0, one launch (start us, length us, event | category | flops | bytes accessed | tf_op | source)
XLA Modules:
  0.0 47.3 jit_solution(7738341204867144800)
XLA Ops:
  0.6 0.9 %means.1.means_ref = f32[64,128]{1,0:T(8,128)S(1)} custom-call(f32[256,128]{1,0:T(8,128)} %columns_ref.3), custom_call_target="tpu_custom_call" | custom-call | tf_op jit(solution)/shard_map/means/pallas_call | solution.py:674
  1.5 6.1 %collective-permute-start.1 = (f32[64,128]{1,0:T(8,128)S(1)}, f32[64,128]{1,0:T(8,128)S(1)}, u32[]{:S(2)}, u32[]{:S(2)}) collective-permute-start(f32[64,128]{1,0:T(8,128)S(1)} %means.1.means_ref), channel_id=1, source_target_pairs={{1,0},{2,1},{3,2},{4,3},{5,4},{6,5},{7,6},{0,7},{9,8},{10,9},{11,1... | collective-permute-start | bytes 98312 | tf_op jit(solution)/shard_map/ppermute | solution.py:712
  7.6 0.0 collective-permute-start
  7.6 2.6 %host.1 = (f32[256,128]{1,0:T(8,128)}, bf16[256,128]{1,0:T(8,128)(2,1)}, bf16[192,128]{1,0:T(8,128)(2,1)S(1)}, f32[192,128]{1,0:T(8,128)S(1)}, f32[256,128]{1,0:...) custom-call(f32[256,128]{1,0:T(8,128)} %columns_ref.3, f32[64,128]{1,0:T(8,128)S(1)} %means.1.means_ref, ...), custom_call_target="tpu_custom_call" | custom-call | tf_op jit(solution)/shard_map/host/pallas_call | solution.py:674
  10.2 0.0 collective-permute-done.1.right_ref
  10.2 4.0 %collective-permute-done.left_ref = f32[64,128]{1,0:T(8,128)S(1)} collective-permute-done((f32[64,128]{1,0:T(8,128)S(1)}, f32[64,128]{1,0:T(8,128)S(1)}, u32[]{:S(2)}, u32[]{:S(2)}) %collective-permute-start) | collective-permute-done | bytes 32800 | tf_op jit(solution)/shard_map/ppermute | solution.py:711
  14.2 1.1 %pack.1 = f32[192,128]{1,0:T(8,128)} custom-call(bf16[192,128]{1,0:T(8,128)(2,1)S(1)} %get-tuple-element.19.wanted_ref, f32[64,128]{1,0:T(8,128)S(1)} %collective-permute-done.left_ref, f32[64,128]{1,0:T(8,128)S(1)} %collective-permute-done.1.right_ref, f32[192,128]{1,0:T(8,128)S(1)} %get-tuple-element.20.constant_ref, f32[128,128]{1,0:T(8,128)S(1)} %get-tuple-element.21.fold_ref), custom_call_target="tpu_custom_call" | custom-call | tf_op jit(solution)/shard_map/pack/pallas_call | solution.py:674
  15.3 3.4 %all-to-all-start = ((f32[8,24,128]{2,1,0:T(8,128)}), f32[8,24,128]{2,1,0:T(8,128)S(1)}, u32[]{:S(2)}, u32[]{:S(2)}) async-start(f32[8,24,128]{2,1,0:T(8,128)} %bitcast.14), calls=%async_computation | async-start | bytes 196608 | tf_op jit(solution)/shard_map/all_to_all | solution.py:748
  18.7 3.2 %prepare.1 = (f32[82,32,128]{2,1,0:T(8,128)S(1)}, f32[2,88,128]{2,1,0:T(8,128)S(1)}, f32[88,128]{1,0:T(8,128)S(1)}) custom-call(bf16[2,58,32,168]{3,2,1,0:T(8,128)(2,1)} %bitcast.11, f32[1,58]{1,0:T(1,128)} %bitcast.20), custom_call_target="tpu_custom_call" | custom-call | tf_op jit(solution)/shard_map/prepare/pallas_call | solution.py:674
  21.9 3.9 %all-to-all-done = f32[8,24,128]{2,1,0:T(8,128)S(1)} async-done(((f32[8,24,128]{2,1,0:T(8,128)}), f32[8,24,128]{2,1,0:T(8,128)S(1)}, u32[]{:S(2)}, u32[]{:S(2)}) %all-to-all-start) | async-done | bytes 98336 | tf_op jit(solution)/shard_map/all_to_all | solution.py:748
  25.8 4.3 %water.1 = (f32[88,32,128]{2,1,0:T(8,128)}, f32[3,88,32,128]{3,2,1,0:T(8,128)}, f32[7,88,128]{2,1,0:T(8,128)}, f32[4,8,21,128]{3,2,1,0:T(8,128)}) custom-call(f32[192,128]{1,0:T(8,128)S(1)} %bitcast.10, f32[82,32,128]{2,1,0:T(8,128)S(1)} %get-tuple-element.22.moved_ref, f32[2,88,128]{2,1,0:T(8,128)S(1)} %get-tuple-element.23.means_ref, ...), custom_call_target="tpu_custom_call" | custom-call | tf_op jit(solution)/shard_map/water/pallas_call | solution.py:674
  30.1 2.6 %all-to-all-start.1 = ((f32[32,21,128]{2,1,0:T(8,128)}), f32[32,21,128]{2,1,0:T(8,128)S(1)}, u32[]{:S(2)}, u32[]{:S(2)}) async-start(f32[32,21,128]{2,1,0:T(8,128)} %bitcast.13), calls=%async_computation.1 | async-start | bytes 786432 | tf_op jit(solution)/shard_map/all_to_all | solution.py:806
  32.7 8.4 %energy.1 = (bf16[2,58,32,168]{3,2,1,0:T(8,128)(2,1)}, f32[256,128]{1,0:T(8,128)S(1)}, f32[256,128]{1,0:T(8,128)S(1)}) custom-call(bf16[2,58,32,168]{3,2,1,0:T(8,128)(2,1)} %bitcast.12, f32[88,32,128]{2,1,0:T(8,128)} %get-tuple-element.26.water_far, f32[3,88,32,128]{3,2,1,0:T(8,128)} %get-tuple-element.27.spill_far, ...), custom_call_target="tpu_custom_call" | custom-call | tf_op jit(solution)/shard_map/energy/pallas_call | solution.py:674
  41.1 5.1 %all-to-all-done.1.gathered_ref = f32[32,21,128]{2,1,0:T(8,128)S(1)} async-done(((f32[32,21,128]{2,1,0:T(8,128)}), f32[32,21,128]{2,1,0:T(8,128)S(1)}, u32[]{:S(2)}, u32[]{:S(2)}) %all-to-all-start.1) | async-done | bytes 344096 | tf_op jit(solution)/shard_map/all_to_all | solution.py:806
  46.2 1.1 %final.1 = f32[256,128]{1,0:T(8,128)} custom-call(f32[256,128]{1,0:T(8,128)S(1)} %get-tuple-element.32.advanced_ref, f32[256,128]{1,0:T(8,128)S(1)} %get-tuple-element.33.places_ref, f32[32,21,128]{2,1,0:T(8,128)S(1)} %all-to-all-done.1.gathered_ref), custom_call_target="tpu_custom_call" | custom-call | tf_op jit(solution)/shard_map/final/pallas_call | solution.py:674
Async XLA Ops:
  1.5 8.7 %collective-permute-start.1 = (f32[64,128]{1,0:T(8,128)S(1)}, f32[64,128]{1,0:T(8,128)S(1)}, u32[]{:S(2)}, u32[]{:S(2)}) collective-permute-start(f32[64,128]{1,0:T(8,128)S(1)} %means.1.means_ref), channel_id=1, source_target_pairs={{1,0},{2,1},{3,2},{4,3},{5,4},{6,5},{7,6},{0,7},{9,8},{10,9},{11,1... | collective-permute-start | bytes 98312 | tf_op jit(solution)/shard_map/ppermute | solution.py:712
  7.6 6.6 %collective-permute-start = (f32[64,128]{1,0:T(8,128)S(1)}, f32[64,128]{1,0:T(8,128)S(1)}, u32[]{:S(2)}, u32[]{:S(2)}) collective-permute-start(f32[64,128]{1,0:T(8,128)S(1)} %means.1.means_ref), channel_id=1, source_target_pairs={{0,1},{1,2},{2,3},{3,4},{4,5},{5,6},{6,7},{7,0},{8,9},{9,10},{10,1... | collective-permute-start | bytes 98312 | tf_op jit(solution)/shard_map/ppermute | solution.py:711
  15.3 10.4 %all-to-all-start = ((f32[8,24,128]{2,1,0:T(8,128)}), f32[8,24,128]{2,1,0:T(8,128)S(1)}, u32[]{:S(2)}, u32[]{:S(2)}) async-start(f32[8,24,128]{2,1,0:T(8,128)} %bitcast.14), calls=%async_computation | async-start | bytes 196608 | tf_op jit(solution)/shard_map/all_to_all | solution.py:748
  30.1 16.0 %all-to-all-start.1 = ((f32[32,21,128]{2,1,0:T(8,128)}), f32[32,21,128]{2,1,0:T(8,128)S(1)}, u32[]{:S(2)}, u32[]{:S(2)}) async-start(f32[32,21,128]{2,1,0:T(8,128)} %bitcast.13), calls=%async_computation.1 | async-start | bytes 786432 | tf_op jit(solution)/shard_map/all_to_all | solution.py:806

commit v4 on v3

--- a/solution.py
+++ b/solution.py
@@ -65,27 +65,97 @@
     return inner + VERTIC * (upper + lower - 2.0 * inner)
 
 
-def means_kernel(columns_ref, means_ref):
-    elements = means_ref.shape[0]
+def element_of_row(rows):
+    elements = rows // 4
+    hit = divided(iota((rows, elements), 0), 4) == iota((rows, elements), 1)
+    return jnp.where(hit, 1.0, 0.0).astype(BF16)
+
+
+def element_means(columns_ref):
+    elements = columns_ref.shape[0] // 4
     total = columns_ref[pl.ds(0, elements, stride=4), :]
     for k in range(1, 4):
         total = total + columns_ref[pl.ds(k, elements, stride=4), :]
-    means_ref[...] = 0.25 * total
+    return 0.25 * total
+
+
+def own_part(values, means, mixing, levels):
+    rows, width = values.shape
+    lane = iota((rows, width), 1)
+    level = lane - levels * divided(lane, levels)
+    upper = jnp.where(level == levels - 1, values, pltpu.roll(values, width - 1, 1))
+    lower = jnp.where(level == 0, values, pltpu.roll(values, 1, 1))
+    mean = select(element_of_row(rows), means, NN)
+    return values - (4.0 * mixing) * mean + VMIX * (upper + lower - 2.0 * values)
+
+
+def slots_of(targets, col_count, padded, clouds):
+    rows = targets.shape[1]
+    onehot = jnp.where(iota((clouds, rows), 0) == targets, 1.0, 0.0)
+    before = jnp.where(iota((rows, rows), 0) < iota((rows, rows), 1), 1.0, 0.0)
+    running = mm(onehot.astype(BF16), before.astype(BF16), NN, None)
+    ranks = jnp.sum(running * onehot, axis=0, keepdims=True).astype(I32)
+    owner = divided(targets, col_count)
+    return owner, (targets - owner * col_count) * padded + ranks
+
+
+def blocked(ref, value, levels):
+    ref[...] = jnp.zeros_like(ref)
+    for f in range(ref.shape[0] // levels):
+        ref[f * levels : f * levels + value.shape[0], f * levels : (f + 1) * levels] = value
 
 
 def host_kernel(
     columns_ref,
-    means_ref,
     mixing_ref,
     neighbours_ref,
     targets_ref,
     substeps_ref,
     map_ref,
+    out_ref,
+    fold_ref,
+    *,
+    padded,
+    clouds,
+):
+    rows, width = columns_ref.shape
+    cloud_levels, levels = map_ref.shape
+    col_count = out_ref.shape[0]
+    block = col_count * padded
+    means = element_means(columns_ref)
+    for c in range(col_count):
+        out_ref[c, padded:, :] = means
+    blocked(fold_ref, RELAX * vertical_mix(map_ref[...], cloud_levels), levels)
+    owner, slot = slots_of(targets_ref[...], col_count, padded, clouds)
+    mine = jnp.where(owner + 1 == lax.axis_index("sec"), slot, -1)
+    pack = jnp.where(iota((block, rows), 0) == mine, 1.0, 0.0).astype(BF16)
+    base = own_part(columns_ref[...], means, mixing_ref[...], levels)
+    count = neighbours_ref.shape[0]
+    ids = select(element_of_row(rows), neighbours_ref[...].astype(F32), NT, swap=True)
+    extras = jnp.concatenate(
+        [
+            jnp.zeros((cloud_levels, rows), F32),
+            ids,
+            jnp.zeros((levels - 1 - cloud_levels - count, rows), F32),
+            substeps_ref[...].astype(F32),
+            jnp.zeros((width - levels, rows), F32),
+        ],
+        axis=0,
+    )
+    sent = mm(select(pack, base, NN), fold_ref[...], NT) + select(pack, extras, NT)
+    for c in range(col_count):
+        out_ref[c, :padded, :] = sent[c * padded : (c + 1) * padded]
+
+
+def aside_kernel(
+    columns_ref,
+    mixing_ref,
+    neighbours_ref,
+    targets_ref,
+    map_ref,
     base_ref,
-    sides_ref,
-    wanted_ref,
-    constant_ref,
-    slots_ref,
+    weights_ref,
+    homes_ref,
     fold_ref,
     unfold_ref,
     *,
@@ -93,65 +163,30 @@
     padded,
     clouds,
 ):
-    section = lax.axis_index("sec")
+    rows, width = columns_ref.shape
+    cloud_levels, levels = map_ref.shape
+    elements = rows // 4
     position = lax.axis_index("col")
-    rows, width = columns_ref.shape
-    levels = map_ref.shape[1]
-    cloud_levels = map_ref.shape[0]
-    elements = rows // 4
-    block = col_count * padded
+    base_ref[...] = own_part(
+        columns_ref[...], element_means(columns_ref), mixing_ref[...], levels
+    )
     near = neighbours_ref[...] - (position - 1) * elements
     near = jnp.where(near < 0, near + elements * col_count, near)
     near = jnp.where(near >= elements * col_count, near - elements * col_count, near)
     window = iota((3 * elements, elements), 0)
-    picks = jnp.where(window == iota((3 * elements, elements), 1) + elements, -4.0, 0.0)
+    picks = jnp.zeros((3 * elements, elements), F32)
     for k in range(near.shape[0]):
         picks = picks + jnp.where(window == near[k : k + 1, :], 1.0, 0.0)
-    row_element = divided(iota((rows, elements), 0), 4)
-    spread_rows = jnp.where(row_element == iota((rows, elements), 1), 1.0, 0.0)
-    weights = mm(spread_rows.astype(BF16), picks.astype(BF16), NT, None)
-    sides = jnp.concatenate([weights[:, :elements], weights[:, 2 * elements :]], axis=1)
-    sides = sides.astype(BF16)
-    sides_ref[...] = sides
-    own = select(weights[:, elements : 2 * elements].astype(BF16), means_ref[...], NN)
-    values = columns_ref[...]
-    lane = iota((rows, width), 1)
-    level = lane - levels * divided(lane, levels)
-    upper = jnp.where(level == levels - 1, values, pltpu.roll(values, width - 1, 1))
-    lower = jnp.where(level == 0, values, pltpu.roll(values, 1, 1))
-    base = values + mixing_ref[...] * own + VMIX * (upper + lower - 2.0 * values)
-    base_ref[...] = base
-    targets = targets_ref[...]
-    onehot = jnp.where(iota((clouds, rows), 0) == targets, 1.0, 0.0)
-    before = jnp.where(iota((rows, rows), 0) < iota((rows, rows), 1), 1.0, 0.0)
-    running = mm(onehot.astype(BF16), before.astype(BF16), NN, None)
-    ranks = jnp.sum(running * onehot, axis=0, keepdims=True).astype(I32)
-    owner = divided(targets, col_count)
-    slot = (targets - owner * col_count) * padded + ranks
-    mine = jnp.where(owner + 1 == section, slot, -1)
-    pack = jnp.where(iota((block, rows), 0) == mine, 1.0, 0.0).astype(BF16)
-    wanted_ref[...] = mm(pack, sides, NN, None).astype(BF16)
-    plain = map_ref[...]
-    folded = RELAX * vertical_mix(plain, cloud_levels)
-    for ref, value in ((fold_ref, folded), (unfold_ref, plain)):
-        ref[...] = jnp.zeros_like(ref)
-        for f in range(width // levels):
-            ref[f * levels : f * levels + cloud_levels, f * levels : (f + 1) * levels] = value
-    count_rows = jnp.where(
-        iota((width, rows), 0) == levels - 1, substeps_ref[...].astype(F32), 0.0
-    )
-    counts = mm(pack, count_rows.astype(BF16), NT, None)
-    constant_ref[...] = mm(select(pack, base, NN), fold_ref[...], NT) + counts
+    weights_ref[...] = mm(element_of_row(rows), picks.astype(BF16), NT, None).astype(BF16)
+    owner, slot = slots_of(targets_ref[...], col_count, padded, clouds)
+    everywhere = (owner * (col_count * padded) + slot).astype(F32)
+    identity = jnp.where(iota((rows, rows), 0) == iota((rows, rows), 1), 1.0, 0.0)
+    homes_ref[...] = select(
+        identity.astype(BF16), jnp.broadcast_to(everywhere, (LANES, rows)), NT
+    )
+    blocked(fold_ref, RELAX * vertical_mix(map_ref[...], cloud_levels), levels)
     fold_ref[...] = fold_ref[...] * mixing_ref[...]
-    everywhere = jnp.broadcast_to((owner * block + slot).astype(F32), (LANES, rows))
-    identity = jnp.where(iota((rows, rows), 0) == iota((rows, rows), 1), 1.0, 0.0)
-    slots_ref[...] = select(identity.astype(BF16), everywhere, NT)
-
-
-def pack_kernel(wanted_ref, left_ref, right_ref, constant_ref, fold_ref, out_ref):
-    halo = jnp.concatenate([left_ref[...], right_ref[...]], axis=0)
-    spread = select(wanted_ref[...], halo, NN)
-    out_ref[...] = constant_ref[...] + mm(spread, fold_ref[...], NT)
+    blocked(unfold_ref, map_ref[...], levels)
 
 
 class Segment:
@@ -289,17 +324,76 @@
     return jnp.broadcast_to(ref[pl.ds(row, 1), :], (8, LANES))
 
 
+def turn(value, shift):
+    if not shift:
+        return value
+    height = value.shape[0]
+    tall = -(-height // 8) * 8
+    if tall != height:
+        fill = jnp.zeros((tall - height, LANES), F32)
+        value = jnp.concatenate([value, fill], axis=0)
+    return pltpu.roll(value, shift % LANES, 1)[:height]
+
+
+def each(count, size, work):
+    size = min(size, count)
+
+    def run(first):
+        for k in range(size):
+            work(first + k)
+
+    if count // size:
+        lax.fori_loop(0, count // size, lambda i, c: (run(i * size), c)[1], 0)
+    if count % size:
+        run(count - size)
+
+
+def widen(state_ref, natural_ref, segments, scale):
+    levels, columns, _ = state_ref.shape
+    for s in segments:
+        at = slice(s.lane0, s.lane0 + s.width)
+
+        def one(k):
+            parts = []
+            for g in range(s.groups):
+                level = jnp.minimum(g * s.steps + k, levels - 1)
+                parts.append(state_ref[level, :, at].astype(F32))
+            spare = LANES - s.groups * s.width
+            if spare:
+                parts.append(jnp.zeros((columns, spare), F32))
+            value = jnp.concatenate(parts, axis=1) if len(parts) > 1 else parts[0]
+            natural_ref[s.begin + 1 + k] = scale * value if scale != 1.0 else value
+
+        each(s.steps, STEP, one)
+
+
+def folded_sums(sums_ref, columns):
+    rows = sums_ref.shape[0] // 8
+    total = sums_ref[pl.ds(0, rows, stride=8), :]
+    for k in range(1, 8):
+        total = total + sums_ref[pl.ds(k, rows, stride=8), :]
+    return total * (1.0 / columns)
+
+
+def slab(row):
+    return pl.ds(pl.multiple_of(row * 8, 8), 8)
+
+
+def spread_row(ref, row):
+    return jnp.broadcast_to(ref[pl.ds(row, 1), :], (8, LANES))
+
+
 def lane_places(segments):
     return [(s, g) for s in segments for g in range(s.groups)]
 
 
 def slot_map(segments, block, capacity, padded):
     tiles = []
-    for s, g in lane_places(segments):
-        lane = iota((8, LANES), 1) - g * s.width
+    for s in segments:
+        lane = iota((8, LANES), 1)
         slot = s.lane0 + lane
-        row = slot + (padded - capacity) * divided(jnp.maximum(slot, 0), capacity)
-        row = jnp.where((lane >= 0) & (lane < s.width), row, -1)[0:1]
+        row = slot + (padded - capacity) * divided(slot, capacity)
+        row = jnp.where(lane < s.width, row, -1)[0:1]
         tiles.append(jnp.where(iota((block, LANES), 0) == row, 1.0, 0.0).astype(BF16))
     return jnp.concatenate(tiles, axis=1)
 
@@ -367,11 +461,13 @@
     moved_ref,
     means_ref,
     limits_ref,
+    fold_far,
     unfold_far,
     water_far,
     spill_far,
     flats_far,
     back_far,
+    fold_ref,
     unfold_ref,
     even_ref,
     odd_ref,
@@ -384,7 +480,7 @@
     sums_ref,
     change_ref,
     back_ref,
-    in_sem,
+    in_sems,
     spill_sems,
     water_sem,
     flat_sem,
@@ -394,29 +490,47 @@
     capacity,
     padded,
     stride,
+    levels,
+    neighbours,
 ):
     rows = means_ref.shape[1]
     columns = even_ref.shape[1]
-    load = pltpu.make_async_copy(unfold_far, unfold_ref, in_sem)
-    load.start()
-    places = slot_map(segments, received_ref.shape[0], capacity, padded)
-    arrived = select(places, received_ref[...], TN, swap=True)
+    loads = [
+        pltpu.make_async_copy(fold_far, fold_ref, in_sems.at[0]),
+        pltpu.make_async_copy(unfold_far, unfold_ref, in_sems.at[1]),
+    ]
+    for load in loads:
+        load.start()
+    hosts = received_ref.shape[0]
+    block = hosts * padded
+    places = slot_map(segments, block, capacity, padded)
+    sent = jnp.concatenate([received_ref[j, :padded, :] for j in range(hosts)], axis=0)
+    arrived = select(places, sent, TN, swap=True)
+    means = jnp.concatenate([received_ref[j, padded:, :] for j in range(hosts)], axis=0)
+    element = iota((means.shape[0], arrived.shape[1]), 0).astype(F32)
+    wanted = jnp.zeros(element.shape, F32)
+    taken = arrived[stride - 1 : stride] > 0.0
+    for k in range(neighbours):
+        ids = jnp.where(taken, arrived[levels + k : levels + k + 1], -1.0)
+        wanted = wanted + jnp.where(element == ids, 1.0, 0.0)
+    spread = select(wanted.astype(BF16), means, TN, swap=True)
+    loads[0].wait()
+    arrived = arrived + mm(fold_ref[...], spread, NN)
     goal_ref[...] = jnp.zeros_like(goal_ref)
     flats_ref[...] = jnp.zeros_like(flats_ref)
     sums_ref[...] = jnp.zeros_like(sums_ref)
     counts = flats_ref.at[MAX_SUB + 2]
-    for s in segments:
+    for t, s in enumerate(segments):
+        lanes = slice(t * LANES, (t + 1) * LANES)
         count = None
-        for t, (owner, g) in enumerate(lane_places(segments)):
-            if owner is not s:
-                continue
-            lanes = slice(t * LANES, (t + 1) * LANES)
+        for g in range(s.groups):
             number = s.group_steps(g)
+            at = slice(s.rows[0], s.rows[0] + number)
             for f in range(2):
                 first = f * stride + g * s.steps
-                at = slice(s.rows[0], s.rows[0] + number)
-                goal_ref[f, at, :] = goal_ref[f, at, :] + arrived[first : first + number, lanes]
-            part = arrived[stride - 1 : stride, lanes]
+                part = turn(arrived[first : first + number, lanes], g * s.width)
+                goal_ref[f, at, :] = goal_ref[f, at, :] + part if g else part
+            part = turn(arrived[stride - 1 : stride, lanes], g * s.width)
             count = part if count is None else count + part
         counts[s.rows[0] : s.rows[1], :] = jnp.broadcast_to(count, (s.steps, LANES))
     for f in range(2):
@@ -498,13 +612,13 @@
     change_ref[...] = jnp.zeros_like(change_ref)
     for f in range(2):
         change = mean_ref[f] - means_ref[f]
-        for t, (s, g) in enumerate(lane_places(segments)):
-            first, number = f * stride + g * s.steps, s.group_steps(g)
-            change_ref[first : first + number, t * LANES : (t + 1) * LANES] = change[
-                s.rows[0] : s.rows[0] + number
-            ]
+        for t, s in enumerate(segments):
+            for g in range(s.groups):
+                first, number = f * stride + g * s.steps, s.group_steps(g)
+                part = turn(change[s.rows[0] : s.rows[0] + number], -g * s.width)
+                change_ref[first : first + number, t * LANES : (t + 1) * LANES] = part
     spread = select(places, change_ref[...], NT)
-    load.wait()
+    loads[1].wait()
     back = mm(spread, unfold_ref[...], NN)
     for j in range(back_ref.shape[0]):
         back_ref[j] = back[j * padded : j * padded + capacity]
@@ -521,9 +635,8 @@
     spill_far,
     flats_far,
     base_ref,
-    sides_ref,
-    left_ref,
-    right_ref,
+    weights_ref,
+    received_ref,
     mixing_ref,
     homes_ref,
     out_ref,
@@ -545,6 +658,7 @@
     out_sems,
     *,
     segments,
+    padded,
 ):
     fields, levels, columns, _ = state_ref.shape
     states = [
@@ -566,8 +680,12 @@
         copy.start()
     waters.start()
     states[1].start()
-    halo = jnp.concatenate([left_ref[...], right_ref[...]], axis=0)
-    advanced_ref[...] = base_ref[...] + mixing_ref[...] * select(sides_ref[...], halo, NN)
+    hosts = received_ref.shape[0]
+    position = lax.axis_index("col")
+    around = [jnp.where(position == 0, hosts - 1, position - 1), position]
+    around.append(jnp.where(position == hosts - 1, 0, position + 1))
+    means = jnp.concatenate([received_ref[j, padded:, :] for j in around], axis=0)
+    advanced_ref[...] = base_ref[...] + mixing_ref[...] * select(weights_ref[...], means, NN)
     places_ref[...] = homes_ref[...]
     states[0].wait()
     widen(state_buf.at[0], natural_ref, segments, SHRINK)
@@ -696,7 +814,7 @@
     block = col_count * padded
     clouds = (sec_count - 1) * col_count
     segments, used, rows = segments_of(slots, cloud_levels)
-    mapped = LANES * len(lane_places(segments))
+    mapped = LANES * len(segments)
     mixing = mixing_rate.reshape(1, width)
     state = cloud_state[0]
     dma = pltpu.SemaphoreType.DMA
@@ -704,48 +822,32 @@
     def wide(*lead):
         return pltpu.VMEM((*lead, rows, columns, LANES), F32)
 
-    (means,) = call(
-        means_kernel, "means", [("auto", column_state)], [("near", (elements, width), F32)]
-    )
-    ring = [(i, (i + 1) % col_count) for i in range(col_count)]
-    left = lax.ppermute(means, "col", ring)
-    right = lax.ppermute(means, "col", [(j, i) for i, j in ring])
-
-    base, sides, wanted, constant, homes, fold, unfold = call(
-        functools.partial(host_kernel, col_count=col_count, padded=padded, clouds=clouds),
+    hosts = dict(padded=padded, clouds=clouds)
+    places_in = [
+        ("auto", column_state),
+        ("auto", mixing),
+        ("auto", neighbours.T),
+        ("auto", assignment.reshape(1, count)),
+    ]
+    outgoing, _ = call(
+        functools.partial(host_kernel, **hosts),
         "host",
-        [
-            ("auto", column_state),
-            ("near", means),
-            ("auto", mixing),
-            ("auto", neighbours.T),
-            ("auto", assignment.reshape(1, count)),
-            ("auto", substeps.reshape(1, count)),
-            ("auto", level_map),
-        ],
+        places_in + [("auto", substeps.reshape(1, count)), ("auto", level_map)],
+        [("auto", (col_count, padded + elements, width), F32), ("near", (width, width), F32)],
+    )
+    received = lax.all_to_all(outgoing, "col", split_axis=0, concat_axis=0, tiled=True)
+    base, weights, homes, fold, unfold = call(
+        functools.partial(aside_kernel, col_count=col_count, **hosts),
+        "aside",
+        places_in + [("auto", level_map)],
         [
             ("auto", (count, width), F32),
-            ("auto", (count, 2 * elements), BF16),
-            ("near", (block, 2 * elements), BF16),
-            ("near", (block, width), F32),
+            ("auto", (count, 3 * elements), BF16),
             ("auto", (count, LANES), F32),
-            ("near", (width, width), F32),
+            ("auto", (width, width), F32),
             ("auto", (width, width), F32),
         ],
     )
-    (outgoing,) = call(
-        pack_kernel,
-        "pack",
-        [
-            ("near", wanted),
-            ("near", left),
-            ("near", right),
-            ("near", constant),
-            ("near", fold),
-        ],
-        [("auto", (block, width), F32)],
-    )
-    received = lax.all_to_all(outgoing, "col", split_axis=0, concat_axis=0, tiled=True)
     moved, cloud_means, limits = call(
         functools.partial(prepare_kernel, segments=segments),
         "prepare",
@@ -766,7 +868,13 @@
     )
     water, spill, flats, back = call(
         functools.partial(
-            water_kernel, segments=segments, capacity=capacity, padded=padded, stride=levels
+            water_kernel,
+            segments=segments,
+            capacity=capacity,
+            padded=padded,
+            stride=levels,
+            levels=cloud_levels,
+            neighbours=neighbours.shape[1],
         ),
         "water",
         [
@@ -774,6 +882,7 @@
             ("near", moved),
             ("near", cloud_means),
             ("near", limits),
+            ("far", fold),
             ("far", unfold),
         ],
         [
@@ -783,6 +892,7 @@
             ("far", (sec_count, col_count, capacity, width), F32),
         ],
         scratch=[
+            pltpu.VMEM((width, width), F32),
             pltpu.VMEM((width, width), F32),
             wide(),
             wide(),
@@ -795,7 +905,7 @@
             pltpu.VMEM((rows * 8, LANES), F32),
             pltpu.VMEM((width, mapped), F32),
             pltpu.VMEM((col_count, capacity, width), F32),
-            dma(()),
+            dma((2,)),
             dma((MAX_SUB - 1,)),
             dma(()),
             dma(()),
@@ -811,7 +921,7 @@
         tiled=True,
     )
     new_block, advanced, places = call(
-        functools.partial(energy_kernel, segments=segments),
+        functools.partial(energy_kernel, segments=segments, padded=padded),
         "energy",
         [
             ("far", state),
@@ -819,9 +929,8 @@
             ("far", spill),
             ("far", flats),
             ("auto", base),
-            ("auto", sides),
-            ("near", left),
-            ("near", right),
+            ("auto", weights),
+            ("near", received),
             ("auto", mixing),
             ("auto", homes),
         ],

time: 47.7 us -> 45.7 us (0.958)
  waiting for transfers between devices: 12.9 us -> 10.9 us
  starting transfers between devices: 12.1 us -> 11 us
  Pallas kernels: 21.6 us -> 22.7 us
    ppermute x2 -> x0, starting transfers between devices: 6.09 us -> none  [the longest x1 6.09 us: body(): right = lax.ppermute(means, 'col', [(j, i) for i, j in ring])]
    ppermute x2 -> x0, waiting for transfers between devices: 4.01 us -> none  [the longest x1 4 us: body(): left = lax.ppermute(means, 'col', ring)]
    all_to_all x1, starting transfers between devices: 3.36 us -> 7.31 us  [body(): lax.all_to_all(outgoing, 'col', split_axis=0, concat_axis=0, tiled=True)]
    all_to_all x1, waiting for transfers between devices: 3.86 us -> 5.46 us  [body(): lax.all_to_all(outgoing, 'col', split_axis=0, concat_axis=0, tiled=True)]
    pallas_call x7 -> x6, Pallas kernels: 21.6 us -> 22.7 us  [call(): pl.pallas_call(kernel, out_shape=shapes, in_specs=[SPACES[space] for spac...]
    all_to_all x1, starting transfers between devices: 2.61 us -> 3.66 us  [body(): lax.all_to_all(back.reshape(sec_count * col_count, capacity, width), ('se...]
  transfers between devices with their start and end apart: 4 -> 2, of which waited for: 3 -> 2; matrix products, arithmetic and copies ran while one was open for 0% -> 0% of each run, Pallas kernels for 30% -> 30%
where the time goes in v4:
time: 45.7 us; the launch traced here: 45.3 us
  Pallas kernels  22.7 us (50%)
  starting transfers between devices  11 us (24%)
  waiting for transfers between devices  10.9 us (24%)
  between operations  0.66 us (1%)
    pallas_call x6, Pallas kernels, call(): pl.pallas_call(kernel, out_shape=shapes, in_specs=[SPACES[space] for spac...  22.7 us
    all_to_all x1, starting transfers between devices, body(): lax.all_to_all(outgoing, 'col', split_axis=0, concat_axis=0, tiled=True)  7.31 us
    all_to_all x1, waiting for transfers between devices, body(): lax.all_to_all(outgoing, 'col', split_axis=0, concat_axis=0, tiled=True)  5.46 us
    all_to_all x1, waiting for transfers between devices, body(): lax.all_to_all(back.reshape(sec_count * col_count, capacity, width), ('se...  5.46 us
    all_to_all x1, starting transfers between devices, body(): lax.all_to_all(back.reshape(sec_count * col_count, capacity, width), ('se...  3.66 us
  transfers between devices with their start and end apart: 2, of which 2 were waited for; matrix products, arithmetic and copies ran while one was open for 0% of the time, Pallas kernels for 30%

profile of v4, /device:TPU:0, one launch (start us, length us, event | category | flops | bytes accessed | tf_op | source)
XLA Modules:
  0.0 45.3 jit_solution(16338075540099878756)
XLA Ops:
  0.6 2.5 %host.1 = (f32[8,88,128]{2,1,0:T(8,128)}, f32[128,128]{1,0:T(8,128)}) custom-call(f32[256,128]{1,0:T(8,128)} %columns_ref.3, f32[1,128]{1,0:T(1,128)} %bitcast.13, s32[4,64]{1,0:T(4,128)} %bitcast.11, s32[1,256]{1,0:T(1,128)} %bitcast.16, s32[1,256]{1,0:T(1,128)} %bitcast.18, f32[58,64]{1,0:T(8,128)} %map_ref.3), custom_call_target="tpu_custom_call" | custom-call | tf_op jit(solution)/shard_map/host/pallas_call | solution.py:792
  3.1 7.3 %all-to-all-start = ((f32[8,88,128]{2,1,0:T(8,128)}), f32[8,88,128]{2,1,0:T(8,128)S(1)}, u32[]{:S(2)}, u32[]{:S(2)}) async-start(f32[8,88,128]{2,1,0:T(8,128)} %get-tuple-element.18), calls=%async_computation | async-start | bytes 720896 | tf_op jit(solution)/shard_map/all_to_all | solution.py:838
  10.4 2.3 %aside.1 = (f32[256,128]{1,0:T(8,128)}, bf16[256,192]{1,0:T(8,128)(2,1)}, f32[256,128]{1,0:T(8,128)}, f32[128,128]{1,0:T(8,128)}, f32[128,128]{1,0:T(8,128)}) custom-call(f32[256,128]{1,0:T(8,128)} %columns_ref.3, f32[1,128]{1,0:T(1,128)} %bitcast.14, s32[4,64]{1,0:T(4,128)} %bitcast.12, s32[1,256]{1,0:T(1,128)} %bitcast.17, f32[58,64]{1,0:T(8,128)} %map_ref.3), custom_call_target="tpu_custom_call" | custom-call | tf_op jit(solution)/shard_map/aside/pallas_call | solution.py:792
  12.7 3.2 %prepare.1 = (f32[82,32,128]{2,1,0:T(8,128)S(1)}, f32[2,88,128]{2,1,0:T(8,128)S(1)}, f32[88,128]{1,0:T(8,128)S(1)}) custom-call(bf16[2,58,32,168]{3,2,1,0:T(8,128)(2,1)} %bitcast.8, f32[1,58]{1,0:T(1,128)} %bitcast.19), custom_call_target="tpu_custom_call" | custom-call | tf_op jit(solution)/shard_map/prepare/pallas_call | solution.py:792
  15.9 5.5 %all-to-all-done.received_ref = f32[8,88,128]{2,1,0:T(8,128)S(1)} async-done(((f32[8,88,128]{2,1,0:T(8,128)}), f32[8,88,128]{2,1,0:T(8,128)S(1)}, u32[]{:S(2)}, u32[]{:S(2)}) %all-to-all-start) | async-done | bytes 360480 | tf_op jit(solution)/shard_map/all_to_all | solution.py:838
  21.4 5.7 %water.1 = (f32[88,32,128]{2,1,0:T(8,128)}, f32[3,88,32,128]{3,2,1,0:T(8,128)}, f32[7,88,128]{2,1,0:T(8,128)}, f32[4,8,21,128]{3,2,1,0:T(8,128)}) custom-call(f32[8,88,128]{2,1,0:T(8,128)S(1)} %all-to-all-done.received_ref, f32[82,32,128]{2,1,0:T(8,128)S(1)} %get-tuple-element.19.moved_ref, f32[2,88,128]{2,1,0:T(8,128)S(1)} %get-tuple-element.20.means_ref, ...), custom_call_target="tpu_custom_call" | custom-call | tf_op jit(solution)/shard_map/water/pallas_call | solution.py:792
  27.0 3.7 %all-to-all-start.1 = ((f32[32,21,128]{2,1,0:T(8,128)}), f32[32,21,128]{2,1,0:T(8,128)S(1)}, u32[]{:S(2)}, u32[]{:S(2)}) async-start(f32[32,21,128]{2,1,0:T(8,128)} %bitcast.10), calls=%async_computation.1 | async-start | bytes 786432 | tf_op jit(solution)/shard_map/all_to_all | solution.py:916
  30.7 8.0 %energy.1 = (bf16[2,58,32,168]{3,2,1,0:T(8,128)(2,1)}, f32[256,128]{1,0:T(8,128)S(1)}, f32[256,128]{1,0:T(8,128)S(1)}) custom-call(bf16[2,58,32,168]{3,2,1,0:T(8,128)(2,1)} %bitcast.9, f32[88,32,128]{2,1,0:T(8,128)} %get-tuple-element.24.water_far, f32[3,88,32,128]{3,2,1,0:T(8,128)} %get-tuple-element.25.spill_far, ...), custom_call_target="tpu_custom_call" | custom-call | tf_op jit(solution)/shard_map/energy/pallas_call | solution.py:792
  38.7 5.5 %all-to-all-done.1.gathered_ref = f32[32,21,128]{2,1,0:T(8,128)S(1)} async-done(((f32[32,21,128]{2,1,0:T(8,128)}), f32[32,21,128]{2,1,0:T(8,128)S(1)}, u32[]{:S(2)}, u32[]{:S(2)}) %all-to-all-start.1) | async-done | bytes 344096 | tf_op jit(solution)/shard_map/all_to_all | solution.py:916
  44.1 1.1 %final.1 = f32[256,128]{1,0:T(8,128)} custom-call(f32[256,128]{1,0:T(8,128)S(1)} %get-tuple-element.30.advanced_ref, f32[256,128]{1,0:T(8,128)S(1)} %get-tuple-element.31.places_ref, f32[32,21,128]{2,1,0:T(8,128)S(1)} %all-to-all-done.1.gathered_ref), custom_call_target="tpu_custom_call" | custom-call | tf_op jit(solution)/shard_map/final/pallas_call | solution.py:792
Async XLA Ops:
  3.1 18.3 %all-to-all-start = ((f32[8,88,128]{2,1,0:T(8,128)}), f32[8,88,128]{2,1,0:T(8,128)S(1)}, u32[]{:S(2)}, u32[]{:S(2)}) async-start(f32[8,88,128]{2,1,0:T(8,128)} %get-tuple-element.18), calls=%async_computation | async-start | bytes 720896 | tf_op jit(solution)/shard_map/all_to_all | solution.py:838
  27.0 17.1 %all-to-all-start.1 = ((f32[32,21,128]{2,1,0:T(8,128)}), f32[32,21,128]{2,1,0:T(8,128)S(1)}, u32[]{:S(2)}, u32[]{:S(2)}) async-start(f32[32,21,128]{2,1,0:T(8,128)} %bitcast.10), calls=%async_computation.1 | async-start | bytes 786432 | tf_op jit(solution)/shard_map/all_to_all | solution.py:916

commit v5 on v4

--- a/solution.py
+++ b/solution.py
@@ -162,6 +162,8 @@
     col_count,
     padded,
     clouds,
+    half,
+    held,
 ):
     rows, width = columns_ref.shape
     cloud_levels, levels = map_ref.shape
@@ -179,7 +181,12 @@
         picks = picks + jnp.where(window == near[k : k + 1, :], 1.0, 0.0)
     weights_ref[...] = mm(element_of_row(rows), picks.astype(BF16), NT, None).astype(BF16)
     owner, slot = slots_of(targets_ref[...], col_count, padded, clouds)
-    everywhere = (owner * (col_count * padded) + slot).astype(F32)
+    place = divided(slot, padded)
+    rank = slot - place * padded
+    upper = jnp.where(rank >= half, 1, 0)
+    parity = lax.axis_index("sec") % 2
+    cloud = owner * col_count + place + jnp.where(upper == parity, 0, clouds)
+    everywhere = (cloud * held + rank - half * upper).astype(F32)
     identity = jnp.where(iota((rows, rows), 0) == iota((rows, rows), 1), 1.0, 0.0)
     homes_ref[...] = select(
         identity.astype(BF16), jnp.broadcast_to(everywhere, (LANES, rows)), NT
@@ -404,11 +411,14 @@
     moved_ref,
     means_ref,
     limits_ref,
+    energy_far,
     state_buf,
     natural_ref,
     sums_ref,
     flat_ref,
+    energy_buf,
     sems,
+    out_sem,
     *,
     segments,
 ):
@@ -431,29 +441,23 @@
             value = jnp.where(lane >= g * s.width, other, value)
         limits_ref[s.rows[0] : s.rows[1], :] = value
     sums_ref[...] = jnp.zeros_like(sums_ref)
-    loads[1].wait()
-    widen(state_buf.at[1], natural_ref, segments, 1.0)
-    fill_wide(segments, natural_ref)
-    for s in segments:
-
-        def work(row, below, here, above):
-            out = linear(below, here, above)
-            for j in range(4):
-                moved_ref[row, pl.ds(8 * j, 8), :] = out[j]
-            sums_ref[slab(row), :] = (here[0] + here[1]) + (here[2] + here[3])
-
-        sweep(s, lambda row: strided(natural_ref, row), work)
-    means_ref[1] = folded_sums(sums_ref, columns)
-    loads[0].wait()
-    widen(state_buf.at[0], natural_ref, segments, 1.0)
-    for s in segments:
-
-        def total(k):
-            value = groups(natural_ref, (s.begin + 1 + k,))
-            sums_ref[slab(s.begin + 1 + k), :] = (value[0] + value[1]) + (value[2] + value[3])
-
-        each(s.steps, STEP, total)
-    means_ref[0] = folded_sums(sums_ref, columns)
+    for f, scale, target in ((1, 1.0, moved_ref), (0, SHRINK, energy_buf)):
+        loads[f].wait()
+        widen(state_buf.at[f], natural_ref, segments, scale)
+        fill_wide(segments, natural_ref)
+        for s in segments:
+
+            def work(row, below, here, above):
+                out = linear(below, here, above)
+                for j in range(4):
+                    target[row, pl.ds(8 * j, 8), :] = out[j]
+                sums_ref[slab(row), :] = (here[0] + here[1]) + (here[2] + here[3])
+
+            sweep(s, lambda row: strided(natural_ref, row), work)
+        means_ref[f] = folded_sums(sums_ref, columns) * (1.0 / scale)
+    leave = pltpu.make_async_copy(energy_buf, energy_far, out_sem)
+    leave.start()
+    leave.wait()
 
 
 def water_kernel(
@@ -505,17 +509,17 @@
     block = hosts * padded
     places = slot_map(segments, block, capacity, padded)
     sent = jnp.concatenate([received_ref[j, :padded, :] for j in range(hosts)], axis=0)
+    means = jnp.concatenate([received_ref[j, padded:, :] for j in range(hosts)], axis=0)
+    element = iota((block, means.shape[0]), 1).astype(F32)
+    taken = sent[:, stride - 1 : stride] > 0.0
+    wanted = jnp.zeros(element.shape, F32)
+    for k in range(neighbours):
+        ids = jnp.where(taken, sent[:, levels + k : levels + k + 1], -1.0)
+        wanted = wanted + jnp.where(element == ids, 1.0, 0.0)
+    spread = select(wanted.astype(BF16), means, NN)
+    loads[0].wait()
+    sent = sent + mm(spread, fold_ref[...], NT)
     arrived = select(places, sent, TN, swap=True)
-    means = jnp.concatenate([received_ref[j, padded:, :] for j in range(hosts)], axis=0)
-    element = iota((means.shape[0], arrived.shape[1]), 0).astype(F32)
-    wanted = jnp.zeros(element.shape, F32)
-    taken = arrived[stride - 1 : stride] > 0.0
-    for k in range(neighbours):
-        ids = jnp.where(taken, arrived[levels + k : levels + k + 1], -1.0)
-        wanted = wanted + jnp.where(element == ids, 1.0, 0.0)
-    spread = select(wanted.astype(BF16), means, TN, swap=True)
-    loads[0].wait()
-    arrived = arrived + mm(fold_ref[...], spread, NN)
     goal_ref[...] = jnp.zeros_like(goal_ref)
     flats_ref[...] = jnp.zeros_like(flats_ref)
     sums_ref[...] = jnp.zeros_like(sums_ref)
@@ -620,10 +624,13 @@
     spread = select(places, change_ref[...], NT)
     loads[1].wait()
     back = mm(spread, unfold_ref[...], NN)
-    for j in range(back_ref.shape[0]):
-        back_ref[j] = back[j * padded : j * padded + capacity]
+    half = back_ref.shape[2]
+    for h in range(2):
+        for j in range(hosts):
+            first = j * padded + h * half
+            back_ref[h, j] = back[first : first + half]
     for i in range(back_far.shape[0]):
-        copies.append(pltpu.make_async_copy(back_ref, back_far.at[i], back_sems.at[i]))
+        copies.append(pltpu.make_async_copy(back_ref.at[i % 2], back_far.at[i], back_sems.at[i]))
         copies[-1].start()
     for copy in copies:
         copy.wait()
@@ -631,145 +638,186 @@
 
 def energy_kernel(
     state_ref,
+    energy_far,
     water_far,
     spill_far,
     flats_far,
-    base_ref,
-    weights_ref,
+    base_far,
+    weights_far,
+    mixing_far,
+    homes_far,
     received_ref,
-    mixing_ref,
-    homes_ref,
     out_ref,
     advanced_ref,
     places_ref,
     state_buf,
+    energy_buf,
     water_buf,
     spill_buf,
     flats_ref,
+    base_ref,
+    weights_ref,
+    mixing_ref,
     out_buf,
     even_ref,
     odd_ref,
-    last_ref,
     natural_ref,
     state_sems,
-    water_sem,
+    in_sems,
     spill_sems,
-    flat_sem,
     out_sems,
     *,
     segments,
     padded,
 ):
     fields, levels, columns, _ = state_ref.shape
+    final = MAX_SUB - 1
+    pairs = (
+        (flats_far, flats_ref),
+        (base_far, base_ref),
+        (weights_far, weights_ref),
+        (mixing_far, mixing_ref),
+        (water_far, water_buf),
+        (energy_far, energy_buf),
+        (homes_far, places_ref),
+    )
+    loads = [pltpu.make_async_copy(x, y, in_sems.at[i]) for i, (x, y) in enumerate(pairs)]
+    flats, bases, shares, mixings, waters, first, homes = loads
     states = [
         pltpu.make_async_copy(state_ref.at[f], state_buf.at[f], state_sems.at[f])
         for f in range(fields)
     ]
-    flats = pltpu.make_async_copy(flats_far, flats_ref, flat_sem)
-    waters = pltpu.make_async_copy(water_far, water_buf, water_sem)
     spills = [
         pltpu.make_async_copy(spill_far.at[n], spill_buf.at[n], spill_sems.at[n])
-        for n in range(MAX_SUB - 1)
+        for n in range(final)
     ]
-    leaves = [
-        pltpu.make_async_copy(out_buf.at[f], out_ref.at[f], out_sems.at[f]) for f in range(fields)
-    ]
-    states[0].start()
-    flats.start()
-    for copy in spills:
+    for copy in loads[:5] + [states[1], first] + spills + [states[0], homes]:
         copy.start()
-    waters.start()
-    states[1].start()
+    cut = -(-levels // 2)
+    spans = ((0, cut), (cut, levels - cut))
+
+    def leave(f, part):
+        at = pl.ds(*spans[part])
+        return pltpu.make_async_copy(
+            out_buf.at[f, at], out_ref.at[f, at], out_sems.at[2 * f + part]
+        )
+
+    counts = flats_ref.at[MAX_SUB + 2]
+
+    def finish_field(f, found):
+        for s in segments[::-1]:
+            count = spread_row(counts, s.rows[0])
+            back = jnp.zeros((8, LANES), F32)
+            for n in range(1, MAX_SUB + 1):
+                scale = 10.0**-n * (LATENT if f == 0 else 1.0)
+                back = jnp.where(count == float(n), scale, back)
+            at = slice(s.lane0, s.lane0 + s.width)
+            held = jnp.broadcast_to(count[0:1, : s.width], (columns, s.width)) > 0.0
+
+            def permute(k):
+                row = s.begin + 1 + k
+                value = groups(found, (row,))
+                for j in range(4):
+                    natural_ref[row, pl.ds(j, 8, stride=4), :] = value[j] * back
+
+            def narrow(g, k):
+                level = g * s.steps + k
+                lanes = slice(g * s.width, (g + 1) * s.width)
+                old = state_buf[f, level, :, at].astype(F32)
+                value = jnp.where(held, natural_ref[s.begin + 1 + k, :, lanes], old)
+                out_buf[f, level, :, at] = value.astype(BF16)
+
+            each(s.steps, STEP, permute)
+            if s is segments[0] and s.groups == 1:
+                for part, (begin, number) in enumerate(spans):
+                    each(number, STEP, lambda k: narrow(0, begin + k))
+                    leave(f, part).start()
+            else:
+                for g in range(s.groups):
+                    each(s.group_steps(g), STEP, lambda k: narrow(g, k))
+        if segments[0].groups > 1:
+            for part in range(2):
+                leave(f, part).start()
+
+    bases.wait()
+    shares.wait()
+    mixings.wait()
     hosts = received_ref.shape[0]
     position = lax.axis_index("col")
     around = [jnp.where(position == 0, hosts - 1, position - 1), position]
     around.append(jnp.where(position == hosts - 1, 0, position + 1))
     means = jnp.concatenate([received_ref[j, padded:, :] for j in around], axis=0)
     advanced_ref[...] = base_ref[...] + mixing_ref[...] * select(weights_ref[...], means, NN)
-    places_ref[...] = homes_ref[...]
-    states[0].wait()
-    widen(state_buf.at[0], natural_ref, segments, SHRINK)
-    fill_wide(segments, natural_ref)
     flats.wait()
-    counts = flats_ref.at[MAX_SUB + 2]
-    source, target = natural_ref, even_ref
+    waters.wait()
+    for s in segments:
+        active = spread_row(counts, s.rows[0]) > float(final)
+
+        def last(row, below, here, above):
+            water = linear(below, here, above)
+            push = spread_row(flats_ref.at[MAX_SUB], row)
+            limit = spread_row(flats_ref.at[MAX_SUB + 1], row)
+            for j in range(4):
+                v = water[j] + push
+                c = jnp.maximum(0.5 * v - limit, 0.0)
+                spill_buf[final, row, pl.ds(8 * j, 8), :] = c
+                even_ref[row, pl.ds(8 * j, 8), :] = jnp.where(active, v - c, here[j])
+
+        sweep(s, lambda row: groups(water_buf, (row,)), last)
+    states[1].wait()
+    finish_field(1, even_ref)
+    first.wait()
+    source, target = None, odd_ref
     for n in range(MAX_SUB):
-        last = n + 1 == MAX_SUB
-        (waters if last else spills[n]).wait()
+        if n < final:
+            spills[n].wait()
         for s in segments:
             active = spread_row(counts, s.rows[0]) > float(n)
 
-            def load(row):
-                here = strided(source, row) if n == 0 else groups(source, (row,))
-                return (here, groups(water_buf, (row,))) if last else (here, None)
+            def start(i, carry):
+                for k in range(STEP):
+                    row = s.begin + 1 + i * STEP + k
+                    shift = spread_row(flats_ref.at[n], row)
+                    lin, spill = groups(energy_buf, (row,)), groups(spill_buf, (n, row))
+                    for j in range(4):
+                        target[row, pl.ds(8 * j, 8), :] = (lin[j] + shift) + spill[j]
+                return carry
 
             def work(row, below, here, above):
                 shift = spread_row(flats_ref.at[n], row)
-                lin = linear(below[0], here[0], above[0])
-                if last:
-                    water = linear(below[1], here[1], above[1])
-                    push = spread_row(flats_ref.at[MAX_SUB], row)
-                    limit = spread_row(flats_ref.at[MAX_SUB + 1], row)
-                else:
-                    spill = groups(spill_buf, (n, row))
+                lin = linear(below, here, above)
+                spill = groups(spill_buf, (n, row))
                 for j in range(4):
-                    if last:
-                        v = water[j] + push
-                        c = jnp.maximum(0.5 * v - limit, 0.0)
-                        last_ref[row, pl.ds(8 * j, 8), :] = jnp.where(active, v - c, here[1][j])
-                    else:
-                        c = spill[j]
-                    u = (lin[j] + shift) + c
-                    if n:
-                        u = jnp.where(active, u, here[0][j])
-                    target[row, pl.ds(8 * j, 8), :] = u
-
-            sweep(s, load, work)
-        if not last:
+                    u = (lin[j] + shift) + spill[j]
+                    target[row, pl.ds(8 * j, 8), :] = jnp.where(active, u, here[j])
+
+            if n == 0:
+                lax.fori_loop(0, s.blocks, start, 0)
+            else:
+                sweep(s, lambda row: groups(source, (row,)), work)
+        if n < final:
             fill_wide(segments, target)
         source, target = target, (odd_ref if target is even_ref else even_ref)
-    for f in (1, 0):
-        states[1].wait() if f == 1 else None
-        found = last_ref if f == 1 else source
-        for s in segments:
-            count = spread_row(counts, s.rows[0])
-            back = jnp.zeros((8, LANES), F32)
-            for n in range(1, MAX_SUB + 1):
-                scale = 10.0**-n * (LATENT if f == 0 else 1.0)
-                back = jnp.where(count == float(n), scale, back)
-
-            def permute(k):
-                row = s.begin + 1 + k
-                value = groups(found, (row,))
-                for j in range(4):
-                    natural_ref[row, pl.ds(j, 8, stride=4), :] = value[j] * back
-
-            each(s.steps, STEP, permute)
-            at = slice(s.lane0, s.lane0 + s.width)
-            held = jnp.broadcast_to(count[0:1, : s.width], (columns, s.width)) > 0.0
-            for g in range(s.groups):
-                lanes = slice(g * s.width, (g + 1) * s.width)
-
-                def narrow(k):
-                    level = g * s.steps + k
-                    old = state_buf[f, level, :, at].astype(F32)
-                    value = jnp.where(held, natural_ref[s.begin + 1 + k, :, lanes], old)
-                    out_buf[f, level, :, at] = value.astype(BF16)
-
-                each(s.group_steps(g), STEP, narrow)
-        leaves[f].start()
+    states[0].wait()
+    finish_field(0, source)
+    homes.wait()
     for f in range(fields):
-        leaves[f].wait()
-
-
-def final_kernel(advanced_ref, places_ref, gathered_ref, out_ref, table_ref, *, levels, idle, padded):
+        for part in range(2):
+            leave(f, part).wait()
+
+
+def final_kernel(
+    advanced_ref, places_ref, mine_ref, other_ref, out_ref, table_ref, *, levels, idle, held
+):
     rows, width = advanced_ref.shape
-    sources, capacity, _ = gathered_ref.shape
-    if capacity != padded:
+    sources, half, _ = mine_ref.shape
+    clouds = sources - idle
+    if half != held:
         table_ref[...] = jnp.zeros_like(table_ref)
-    for j in range(idle, sources):
-        first = (j - idle) * padded
-        table_ref[first : first + capacity, :] = gathered_ref[j]
+    for i, ref in enumerate((mine_ref, other_ref)):
+        for j in range(clouds):
+            first = (i * clouds + j) * held
+            table_ref[first : first + half, :] = ref[idle + j]
     place = places_ref[:, :1].astype(I32)
     picks = jnp.where(iota((rows, table_ref.shape[0]), 1) == place, 1.0, 0.0)
     summed = advanced_ref[...] + select(picks.astype(BF16), table_ref[...], NN)
@@ -811,6 +859,8 @@
     elements = count // 4
     capacity = slots // col_count
     padded = -(-capacity // 8) * 8
+    half = -(-capacity // 2)
+    held = -(-half // 8) * 8
     block = col_count * padded
     clouds = (sec_count - 1) * col_count
     segments, used, rows = segments_of(slots, cloud_levels)
@@ -837,7 +887,7 @@
     )
     received = lax.all_to_all(outgoing, "col", split_axis=0, concat_axis=0, tiled=True)
     base, weights, homes, fold, unfold = call(
-        functools.partial(aside_kernel, col_count=col_count, **hosts),
+        functools.partial(aside_kernel, col_count=col_count, half=half, held=held, **hosts),
         "aside",
         places_in + [("auto", level_map)],
         [
@@ -848,7 +898,7 @@
             ("auto", (width, width), F32),
         ],
     )
-    moved, cloud_means, limits = call(
+    moved, cloud_means, limits, energy = call(
         functools.partial(prepare_kernel, segments=segments),
         "prepare",
         [("far", state), ("auto", saturation.reshape(1, cloud_levels))],
@@ -856,13 +906,16 @@
             ("near", (used, columns, LANES), F32),
             ("near", (fields, rows, LANES), F32),
             ("near", (rows, LANES), F32),
+            ("far", (used, columns, LANES), F32),
         ],
         scratch=[
             pltpu.VMEM(state.shape, BF16),
             wide(),
             pltpu.VMEM((rows * 8, LANES), F32),
             pltpu.VMEM((max(s.groups * s.steps for s in segments), LANES), F32),
+            pltpu.VMEM((used, columns, LANES), F32),
             dma((fields,)),
+            dma(()),
         ],
         limit=16,
     )
@@ -889,7 +942,7 @@
             ("far", (rows, columns, LANES), F32),
             ("far", (MAX_SUB - 1, rows, columns, LANES), F32),
             ("far", (MAX_SUB + 3, rows, LANES), F32),
-            ("far", (sec_count, col_count, capacity, width), F32),
+            ("far", (sec_count, col_count, half, width), F32),
         ],
         scratch=[
             pltpu.VMEM((width, width), F32),
@@ -904,7 +957,7 @@
             pltpu.VMEM((rows, LANES), F32),
             pltpu.VMEM((rows * 8, LANES), F32),
             pltpu.VMEM((width, mapped), F32),
-            pltpu.VMEM((col_count, capacity, width), F32),
+            pltpu.VMEM((2, col_count, half, width), F32),
             dma((2,)),
             dma((MAX_SUB - 1,)),
             dma(()),
@@ -914,7 +967,7 @@
         limit=24,
     )
     returned = lax.all_to_all(
-        back.reshape(sec_count * col_count, capacity, width),
+        back.reshape(sec_count * col_count, half, width),
         ("sec", "col"),
         split_axis=0,
         concat_axis=0,
@@ -925,14 +978,15 @@
         "energy",
         [
             ("far", state),
+            ("far", energy),
             ("far", water),
             ("far", spill),
             ("far", flats),
-            ("auto", base),
-            ("auto", weights),
+            ("far", base),
+            ("far", weights),
+            ("far", mixing),
+            ("far", homes),
             ("near", received),
-            ("auto", mixing),
-            ("auto", homes),
         ],
         [
             ("far", state.shape, BF16),
@@ -941,28 +995,33 @@
         ],
         scratch=[
             pltpu.VMEM(state.shape, BF16),
+            pltpu.VMEM((used, columns, LANES), F32),
             wide(),
-            wide(MAX_SUB - 1),
+            wide(MAX_SUB),
             pltpu.VMEM((MAX_SUB + 3, rows, LANES), F32),
+            pltpu.VMEM((count, width), F32),
+            pltpu.VMEM((count, 3 * elements), BF16),
+            pltpu.VMEM((1, width), F32),
             pltpu.VMEM(state.shape, BF16),
             wide(),
             wide(),
             wide(),
-            wide(),
             dma((fields,)),
-            dma(()),
+            dma((7,)),
             dma((MAX_SUB - 1,)),
-            dma(()),
-            dma((fields,)),
+            dma((2 * fields,)),
         ],
         limit=32,
     )
+    returned, advanced = lax.optimization_barrier((returned, advanced))
+    pairs = [(i, i ^ 1) for i in range(sec_count)]
+    partner = lax.ppermute(returned, "sec", pairs)
     (new_columns,) = call(
-        functools.partial(final_kernel, levels=levels, idle=col_count, padded=padded),
+        functools.partial(final_kernel, levels=levels, idle=col_count, held=held),
         "final",
-        [("near", advanced), ("near", places), ("near", returned)],
+        [("near", advanced), ("near", places), ("near", returned), ("near", partner)],
         [("auto", (count, width), F32)],
-        scratch=[pltpu.VMEM((clouds * padded, width), F32)],
+        scratch=[pltpu.VMEM((2 * clouds * held, width), F32)],
     )
     return new_columns, new_block[None]
 

time: 45.7 us -> 44.5 us (0.974)
  waiting for transfers between devices: 10.9 us -> 9.63 us
    ppermute x0 -> x1, waiting for transfers between devices: none -> 1.53 us  [body(): partner = lax.ppermute(returned, 'sec', pairs)]
    all_to_all x1, waiting for transfers between devices: 5.46 us -> 4.01 us  [body(): lax.all_to_all(outgoing, 'col', split_axis=0, concat_axis=0, tiled=True)]
    all_to_all x1, waiting for transfers between devices: 5.46 us -> 4.08 us  [body(): lax.all_to_all(back.reshape(sec_count * col_count, half, width), ('sec',...]
  transfers between devices with their start and end apart: 2 -> 3, of which waited for: 2 -> 3; matrix products, arithmetic and copies ran while one was open for 0% -> 0% of each run, Pallas kernels for 30% -> 30%
where the time goes in v5:
time: 44.5 us; the launch traced here: 44.1 us
  Pallas kernels  22.9 us (51%)
  starting transfers between devices  11 us (25%)
  waiting for transfers between devices  9.63 us (22%)
  between operations  0.66 us (1%)
    pallas_call x6, Pallas kernels, call(): pl.pallas_call(kernel, out_shape=shapes, in_specs=[SPACES[space] for spac...  22.9 us
    all_to_all x1, starting transfers between devices, body(): lax.all_to_all(outgoing, 'col', split_axis=0, concat_axis=0, tiled=True)  7.31 us
    all_to_all x1, waiting for transfers between devices, body(): lax.all_to_all(back.reshape(sec_count * col_count, half, width), ('sec',...  4.08 us
    all_to_all x1, waiting for transfers between devices, body(): lax.all_to_all(outgoing, 'col', split_axis=0, concat_axis=0, tiled=True)  4.01 us
    all_to_all x1, starting transfers between devices, body(): lax.all_to_all(back.reshape(sec_count * col_count, half, width), ('sec',...  3.66 us
    ppermute x1, waiting for transfers between devices, body(): partner = lax.ppermute(returned, 'sec', pairs)  1.53 us
  transfers between devices with their start and end apart: 3, of which 3 were waited for; matrix products, arithmetic and copies ran while one was open for 0% of the time, Pallas kernels for 30%

profile of v5, /device:TPU:0, one launch (start us, length us, event | category | flops | bytes accessed | tf_op | source)
XLA Modules:
  0.0 44.1 jit_solution(6219160166991755958)
XLA Ops:
  0.6 2.5 %host.1 = (f32[8,88,128]{2,1,0:T(8,128)}, f32[128,128]{1,0:T(8,128)}) custom-call(f32[256,128]{1,0:T(8,128)} %columns_ref.3, f32[1,128]{1,0:T(1,128)} %bitcast.13, s32[4,64]{1,0:T(4,128)} %bitcast.11, s32[1,256]{1,0:T(1,128)} %bitcast.16, s32[1,256]{1,0:T(1,128)} %bitcast.18, f32[58,64]{1,0:T(8,128)} %map_ref.3), custom_call_target="tpu_custom_call" | custom-call | tf_op jit(solution)/shard_map/host/pallas_call | solution.py:840
  3.1 7.3 %all-to-all-start = ((f32[8,88,128]{2,1,0:T(8,128)}), f32[8,88,128]{2,1,0:T(8,128)S(1)}, u32[]{:S(2)}, u32[]{:S(2)}) async-start(f32[8,88,128]{2,1,0:T(8,128)} %get-tuple-element.21), calls=%async_computation | async-start | bytes 720896 | tf_op jit(solution)/shard_map/all_to_all | solution.py:888
  10.4 2.3 %aside.1 = (f32[256,128]{1,0:T(8,128)}, bf16[256,192]{1,0:T(8,128)(2,1)}, f32[256,128]{1,0:T(8,128)}, f32[128,128]{1,0:T(8,128)}, f32[128,128]{1,0:T(8,128)}) custom-call(f32[256,128]{1,0:T(8,128)} %columns_ref.3, f32[1,128]{1,0:T(1,128)} %bitcast.14, s32[4,64]{1,0:T(4,128)} %bitcast.12, s32[1,256]{1,0:T(1,128)} %bitcast.17, f32[58,64]{1,0:T(8,128)} %map_ref.3), custom_call_target="tpu_custom_call" | custom-call | tf_op jit(solution)/shard_map/aside/pallas_call | solution.py:840
  12.7 4.6 %prepare.1 = (f32[82,32,128]{2,1,0:T(8,128)S(1)}, f32[2,88,128]{2,1,0:T(8,128)S(1)}, f32[88,128]{1,0:T(8,128)S(1)}, f32[82,32,128]{2,1,0:T(8,128)}) custom-call(bf16[2,58,32,168]{3,2,1,0:T(8,128)(2,1)} %bitcast.8, f32[1,58]{1,0:T(1,128)} %bitcast.19), custom_call_target="tpu_custom_call" | custom-call | tf_op jit(solution)/shard_map/prepare/pallas_call | solution.py:840
  17.4 4.0 %all-to-all-done.received_ref = f32[8,88,128]{2,1,0:T(8,128)S(1)} async-done(((f32[8,88,128]{2,1,0:T(8,128)}), f32[8,88,128]{2,1,0:T(8,128)S(1)}, u32[]{:S(2)}, u32[]{:S(2)}) %all-to-all-start) | async-done | bytes 360480 | tf_op jit(solution)/shard_map/all_to_all | solution.py:888
  21.4 5.9 %water.1 = (f32[88,32,128]{2,1,0:T(8,128)}, f32[3,88,32,128]{3,2,1,0:T(8,128)}, f32[7,88,128]{2,1,0:T(8,128)}, f32[4,8,11,128]{3,2,1,0:T(8,128)}) custom-call(f32[8,88,128]{2,1,0:T(8,128)S(1)} %all-to-all-done.received_ref, f32[82,32,128]{2,1,0:T(8,128)S(1)} %get-tuple-element.22.moved_ref, f32[2,88,128]{2,1,0:T(8,128)S(1)} %get-tuple-element.23.means_ref, ...), custom_call_target="tpu_custom_call" | custom-call | tf_op jit(solution)/shard_map/water/pallas_call | solution.py:840
  27.2 3.7 %all-to-all-start.1 = ((f32[32,11,128]{2,1,0:T(8,128)}), f32[32,11,128]{2,1,0:T(8,128)S(1)}, u32[]{:S(2)}, u32[]{:S(2)}) async-start(f32[32,11,128]{2,1,0:T(8,128)} %bitcast.10), calls=%async_computation.1 | async-start | bytes 524288 | tf_op jit(solution)/shard_map/all_to_all | solution.py:969
  30.9 6.4 %energy.1 = (bf16[2,58,32,168]{3,2,1,0:T(8,128)(2,1)}, f32[256,128]{1,0:T(8,128)S(1)}, f32[256,128]{1,0:T(8,128)S(1)}) custom-call(bf16[2,58,32,168]{3,2,1,0:T(8,128)(2,1)} %bitcast.9, f32[82,32,128]{2,1,0:T(8,128)} %get-tuple-element.28.energy_far, f32[88,32,128]{2,1,0:T(8,128)} %get-tuple-element.29.water_far, ...), custom_call_target="tpu_custom_call" | custom-call | tf_op jit(solution)/shard_map/energy/pallas_call | solution.py:840
  37.3 4.1 %all-to-all-done.1.mine_ref = f32[32,11,128]{2,1,0:T(8,128)S(1)} async-done(((f32[32,11,128]{2,1,0:T(8,128)}), f32[32,11,128]{2,1,0:T(8,128)S(1)}, u32[]{:S(2)}, u32[]{:S(2)}) %all-to-all-start.1) | async-done | bytes 180256 | tf_op jit(solution)/shard_map/all_to_all | solution.py:969
  41.4 0.0 collective-permute-start
  41.4 1.5 %collective-permute-done.other_ref = f32[32,11,128]{2,1,0:T(8,128)S(1)} collective-permute-done((f32[32,11,128]{2,1,0:T(8,128)S(1)}, f32[32,11,128]{2,1,0:T(8,128)S(1)}, u32[]{:S(2)}, u32[]{:S(2)}) %collective-permute-start) | collective-permute-done | bytes 180256 | tf_op jit(solution)/shard_map/ppermute | solution.py:1018
  42.9 1.2 %final.1 = f32[256,128]{1,0:T(8,128)} custom-call(f32[256,128]{1,0:T(8,128)S(1)} %get-tuple-element.36.advanced_ref, f32[256,128]{1,0:T(8,128)S(1)} %get-tuple-element.37.places_ref, f32[32,11,128]{2,1,0:T(8,128)S(1)} %all-to-all-done.1.mine_ref, f32[32,11,128]{2,1,0:T(8,128)S(1)} %collective-permute-done.other_ref), custom_call_target="tpu_custom_call" | custom-call | tf_op jit(solution)/shard_map/final/pallas_call | solution.py:840
Async XLA Ops:
  3.1 18.3 %all-to-all-start = ((f32[8,88,128]{2,1,0:T(8,128)}), f32[8,88,128]{2,1,0:T(8,128)S(1)}, u32[]{:S(2)}, u32[]{:S(2)}) async-start(f32[8,88,128]{2,1,0:T(8,128)} %get-tuple-element.21), calls=%async_computation | async-start | bytes 720896 | tf_op jit(solution)/shard_map/all_to_all | solution.py:888
  27.2 14.1 %all-to-all-start.1 = ((f32[32,11,128]{2,1,0:T(8,128)}), f32[32,11,128]{2,1,0:T(8,128)S(1)}, u32[]{:S(2)}, u32[]{:S(2)}) async-start(f32[32,11,128]{2,1,0:T(8,128)} %bitcast.10), calls=%async_computation.1 | async-start | bytes 524288 | tf_op jit(solution)/shard_map/all_to_all | solution.py:969
  41.4 1.5 %collective-permute-start = (f32[32,11,128]{2,1,0:T(8,128)S(1)}, f32[32,11,128]{2,1,0:T(8,128)S(1)}, u32[]{:S(2)}, u32[]{:S(2)}) collective-permute-start(f32[32,11,128]{2,1,0:T(8,128)S(1)} %all-to-all-done.1.mine_ref), channel_id=1, source_target_pairs={{0,8},{8,0},{16,24},{24,16},{1,9},{9,1},{17,25},{25,17},{2,10},{10... | collective-permute-start | bytes 540680 | tf_op jit(solution)/shard_map/ppermute | solution.py:1018

commit v6 on v5

--- a/solution.py
+++ b/solution.py
@@ -58,6 +58,15 @@
     return total
 
 
+def product(a, b, contract):
+    (al, am, ah), (bl, bm, bh) = split(a), split(b)
+    total = None
+    for x, y in ((al, bh), (ah, bl), (am, bm), (am, bh), (ah, bm), (ah, bh)):
+        term = lax.dot_general(x, y, (contract, ((), ())), preferred_element_type=F32)
+        total = term if total is None else total + term
+    return total
+
+
 def vertical_mix(values, levels):
     upper = jnp.concatenate([values[1:levels], values[levels - 1 : levels]], axis=0)
     lower = jnp.concatenate([values[0:1], values[0 : levels - 1]], axis=0)
@@ -87,6 +96,15 @@
     lower = jnp.where(level == 0, values, pltpu.roll(values, 1, 1))
     mean = select(element_of_row(rows), means, NN)
     return values - (4.0 * mixing) * mean + VMIX * (upper + lower - 2.0 * values)
+
+
+def joined_means(mine_ref, other_ref, share, order):
+    first = lax.axis_index("sec") % 2 == 0
+    parts = []
+    for j in order:
+        mine, other = mine_ref[j, :share, :], other_ref[j, :share, :]
+        parts += [jnp.where(first, mine, other), jnp.where(first, other, mine)]
+    return jnp.concatenate(parts, axis=0)
 
 
 def slots_of(targets, col_count, padded, clouds):
@@ -123,11 +141,14 @@
     col_count = out_ref.shape[0]
     block = col_count * padded
     means = element_means(columns_ref)
+    share = means.shape[0] // 2
+    section = lax.axis_index("sec")
+    part = jnp.where(section % 2 == 0, means[:share], means[share:])
     for c in range(col_count):
-        out_ref[c, padded:, :] = means
+        out_ref[c, :share, :] = part
     blocked(fold_ref, RELAX * vertical_mix(map_ref[...], cloud_levels), levels)
     owner, slot = slots_of(targets_ref[...], col_count, padded, clouds)
-    mine = jnp.where(owner + 1 == lax.axis_index("sec"), slot, -1)
+    mine = jnp.where(owner + 1 == section, slot, -1)
     pack = jnp.where(iota((block, rows), 0) == mine, 1.0, 0.0).astype(BF16)
     base = own_part(columns_ref[...], means, mixing_ref[...], levels)
     count = neighbours_ref.shape[0]
@@ -142,12 +163,13 @@
         ],
         axis=0,
     )
-    sent = mm(select(pack, base, NN), fold_ref[...], NT) + select(pack, extras, NT)
+    sent = product(select(pack, base, NN), fold_ref[...], NT) + select(pack, extras, NT)
+    capacity = out_ref.shape[1] - share
     for c in range(col_count):
-        out_ref[c, :padded, :] = sent[c * padded : (c + 1) * padded]
-
-
-def aside_kernel(
+        out_ref[c, share:, :] = sent[c * padded : c * padded + capacity]
+
+
+def aside(
     columns_ref,
     mixing_ref,
     neighbours_ref,
@@ -158,7 +180,6 @@
     homes_ref,
     fold_ref,
     unfold_ref,
-    *,
     col_count,
     padded,
     clouds,
@@ -407,27 +428,70 @@
 
 def prepare_kernel(
     state_ref,
-    saturation_ref,
+    columns_far,
+    mixing_far,
+    neighbours_far,
+    targets_far,
+    map_far,
+    saturation_far,
     moved_ref,
     means_ref,
     limits_ref,
     energy_far,
+    base_far,
+    weights_far,
+    homes_far,
+    fold_far,
+    unfold_far,
     state_buf,
     natural_ref,
     sums_ref,
     flat_ref,
     energy_buf,
+    columns_ref,
+    mixing_ref,
+    neighbours_ref,
+    targets_ref,
+    map_ref,
+    saturation_ref,
+    base_ref,
+    weights_ref,
+    homes_ref,
+    fold_ref,
+    unfold_ref,
     sems,
-    out_sem,
+    in_sems,
+    out_sems,
     *,
     segments,
+    **host,
 ):
     fields, levels, columns, _ = state_ref.shape
+    given = (
+        (columns_far, columns_ref),
+        (mixing_far, mixing_ref),
+        (neighbours_far, neighbours_ref),
+        (targets_far, targets_ref),
+        (map_far, map_ref),
+        (saturation_far, saturation_ref),
+    )
+    starts = [pltpu.make_async_copy(x, y, in_sems.at[i]) for i, (x, y) in enumerate(given)]
     loads = [
         pltpu.make_async_copy(state_ref.at[f], state_buf.at[f], sems.at[f]) for f in range(fields)
     ]
-    loads[1].start()
-    loads[0].start()
+    for copy in starts + loads:
+        copy.start()
+    made = (
+        (base_ref, base_far),
+        (weights_ref, weights_far),
+        (homes_ref, homes_far),
+        (fold_ref, fold_far),
+        (unfold_ref, unfold_far),
+        (energy_buf, energy_far),
+    )
+    leaves = [pltpu.make_async_copy(x, y, out_sems.at[i]) for i, (x, y) in enumerate(made)]
+    for copy in starts:
+        copy.wait()
     tall = flat_ref.shape[0]
     here = iota((tall, levels), 0) == iota((tall, levels), 1)
     diagonal = jnp.where(here, 0.5 * saturation_ref[...], 0.0)
@@ -441,7 +505,22 @@
             value = jnp.where(lane >= g * s.width, other, value)
         limits_ref[s.rows[0] : s.rows[1], :] = value
     sums_ref[...] = jnp.zeros_like(sums_ref)
-    for f, scale, target in ((1, 1.0, moved_ref), (0, SHRINK, energy_buf)):
+    aside(
+        columns_ref,
+        mixing_ref,
+        neighbours_ref,
+        targets_ref,
+        map_ref,
+        base_ref,
+        weights_ref,
+        homes_ref,
+        fold_ref,
+        unfold_ref,
+        **host,
+    )
+    for copy in leaves[:5]:
+        copy.start()
+    for f, scale, target in ((0, SHRINK, energy_buf), (1, 1.0, moved_ref)):
         loads[f].wait()
         widen(state_buf.at[f], natural_ref, segments, scale)
         fill_wide(segments, natural_ref)
@@ -454,14 +533,16 @@
                 sums_ref[slab(row), :] = (here[0] + here[1]) + (here[2] + here[3])
 
             sweep(s, lambda row: strided(natural_ref, row), work)
+        if f == 0:
+            leaves[5].start()
         means_ref[f] = folded_sums(sums_ref, columns) * (1.0 / scale)
-    leave = pltpu.make_async_copy(energy_buf, energy_far, out_sem)
-    leave.start()
-    leave.wait()
+    for copy in leaves:
+        copy.wait()
 
 
 def water_kernel(
     received_ref,
+    other_ref,
     moved_ref,
     means_ref,
     limits_ref,
@@ -508,18 +589,29 @@
     hosts = received_ref.shape[0]
     block = hosts * padded
     places = slot_map(segments, block, capacity, padded)
-    sent = jnp.concatenate([received_ref[j, :padded, :] for j in range(hosts)], axis=0)
-    means = jnp.concatenate([received_ref[j, padded:, :] for j in range(hosts)], axis=0)
-    element = iota((block, means.shape[0]), 1).astype(F32)
-    taken = sent[:, stride - 1 : stride] > 0.0
-    wanted = jnp.zeros(element.shape, F32)
-    for k in range(neighbours):
-        ids = jnp.where(taken, sent[:, levels + k : levels + k + 1], -1.0)
-        wanted = wanted + jnp.where(element == ids, 1.0, 0.0)
-    spread = select(wanted.astype(BF16), means, NN)
+    share = received_ref.shape[1] - capacity
+    parts = []
+    for j in range(hosts):
+        parts.append(received_ref[j, share:, :])
+        if padded != capacity:
+            parts.append(jnp.zeros((padded - capacity, LANES), F32))
+    sent = jnp.concatenate(parts, axis=0)
+    means = joined_means(received_ref, other_ref, share, range(hosts))
+    arrived = select(places, sent, TN, swap=True)
     loads[0].wait()
-    sent = sent + mm(spread, fold_ref[...], NT)
-    arrived = select(places, sent, TN, swap=True)
+    folded = product(fold_ref[...], means, NT)
+    taken = arrived[stride - 1 : stride] > 0.0
+    ids = [
+        jnp.where(taken, arrived[levels + k : levels + k + 1], -1.0) for k in range(neighbours)
+    ]
+    chunk = min(256, means.shape[0])
+    for first in range(0, means.shape[0], chunk):
+        element = (iota((chunk, arrived.shape[1]), 0) + first).astype(F32)
+        wanted = jnp.where(element == ids[0], 1.0, 0.0)
+        for k in range(1, neighbours):
+            wanted = wanted + jnp.where(element == ids[k], 1.0, 0.0)
+        part = folded[:, first : first + chunk]
+        arrived = arrived + select(wanted.astype(BF16), part, NN, swap=True)
     goal_ref[...] = jnp.zeros_like(goal_ref)
     flats_ref[...] = jnp.zeros_like(flats_ref)
     sums_ref[...] = jnp.zeros_like(sums_ref)
@@ -623,7 +715,7 @@
                 change_ref[first : first + number, t * LANES : (t + 1) * LANES] = part
     spread = select(places, change_ref[...], NT)
     loads[1].wait()
-    back = mm(spread, unfold_ref[...], NN)
+    back = product(spread, unfold_ref[...], NN)
     half = back_ref.shape[2]
     for h in range(2):
         for j in range(hosts):
@@ -647,6 +739,7 @@
     mixing_far,
     homes_far,
     received_ref,
+    other_ref,
     out_ref,
     advanced_ref,
     places_ref,
@@ -668,7 +761,7 @@
     out_sems,
     *,
     segments,
-    padded,
+    share,
 ):
     fields, levels, columns, _ = state_ref.shape
     final = MAX_SUB - 1
@@ -746,7 +839,7 @@
     position = lax.axis_index("col")
     around = [jnp.where(position == 0, hosts - 1, position - 1), position]
     around.append(jnp.where(position == hosts - 1, 0, position + 1))
-    means = jnp.concatenate([received_ref[j, padded:, :] for j in around], axis=0)
+    means = joined_means(received_ref, other_ref, share, around)
     advanced_ref[...] = base_ref[...] + mixing_ref[...] * select(weights_ref[...], means, NN)
     flats.wait()
     waters.wait()
@@ -883,30 +976,32 @@
         functools.partial(host_kernel, **hosts),
         "host",
         places_in + [("auto", substeps.reshape(1, count)), ("auto", level_map)],
-        [("auto", (col_count, padded + elements, width), F32), ("near", (width, width), F32)],
+        [("auto", (col_count, elements // 2 + capacity, width), F32), ("near", (width, width), F32)],
     )
     received = lax.all_to_all(outgoing, "col", split_axis=0, concat_axis=0, tiled=True)
-    base, weights, homes, fold, unfold = call(
-        functools.partial(aside_kernel, col_count=col_count, half=half, held=held, **hosts),
-        "aside",
-        places_in + [("auto", level_map)],
-        [
-            ("auto", (count, width), F32),
-            ("auto", (count, 3 * elements), BF16),
-            ("auto", (count, LANES), F32),
-            ("auto", (width, width), F32),
-            ("auto", (width, width), F32),
-        ],
-    )
-    moved, cloud_means, limits, energy = call(
-        functools.partial(prepare_kernel, segments=segments),
+    moved, cloud_means, limits, energy, base, weights, homes, fold, unfold = call(
+        functools.partial(
+            prepare_kernel,
+            segments=segments,
+            col_count=col_count,
+            half=half,
+            held=held,
+            **hosts,
+        ),
         "prepare",
-        [("far", state), ("auto", saturation.reshape(1, cloud_levels))],
+        [("far", state)]
+        + [("far", x) for _, x in places_in]
+        + [("far", level_map), ("far", saturation.reshape(1, cloud_levels))],
         [
             ("near", (used, columns, LANES), F32),
             ("near", (fields, rows, LANES), F32),
             ("near", (rows, LANES), F32),
             ("far", (used, columns, LANES), F32),
+            ("far", (count, width), F32),
+            ("far", (count, 3 * elements), BF16),
+            ("far", (count, LANES), F32),
+            ("far", (width, width), F32),
+            ("far", (width, width), F32),
         ],
         scratch=[
             pltpu.VMEM(state.shape, BF16),
@@ -914,11 +1009,26 @@
             pltpu.VMEM((rows * 8, LANES), F32),
             pltpu.VMEM((max(s.groups * s.steps for s in segments), LANES), F32),
             pltpu.VMEM((used, columns, LANES), F32),
+            pltpu.VMEM((count, width), F32),
+            pltpu.VMEM((1, width), F32),
+            pltpu.VMEM((neighbours.shape[1], elements), I32),
+            pltpu.VMEM((1, count), I32),
+            pltpu.VMEM((cloud_levels, levels), F32),
+            pltpu.VMEM((1, cloud_levels), F32),
+            pltpu.VMEM((count, width), F32),
+            pltpu.VMEM((count, 3 * elements), BF16),
+            pltpu.VMEM((count, LANES), F32),
+            pltpu.VMEM((width, width), F32),
+            pltpu.VMEM((width, width), F32),
             dma((fields,)),
-            dma(()),
+            dma((6,)),
+            dma((6,)),
         ],
         limit=16,
     )
+    received, moved, base = lax.optimization_barrier((received, moved, base))
+    pairs = [(i, i ^ 1) for i in range(sec_count)]
+    other = lax.ppermute(received, "sec", pairs)
     water, spill, flats, back = call(
         functools.partial(
             water_kernel,
@@ -932,6 +1042,7 @@
         "water",
         [
             ("near", received),
+            ("near", other),
             ("near", moved),
             ("near", cloud_means),
             ("near", limits),
@@ -974,7 +1085,7 @@
         tiled=True,
     )
     new_block, advanced, places = call(
-        functools.partial(energy_kernel, segments=segments, padded=padded),
+        functools.partial(energy_kernel, segments=segments, share=elements // 2),
         "energy",
         [
             ("far", state),
@@ -987,6 +1098,7 @@
             ("far", mixing),
             ("far", homes),
             ("near", received),
+            ("near", other),
         ],
         [
             ("far", state.shape, BF16),
@@ -1014,7 +1126,6 @@
         limit=32,
     )
     returned, advanced = lax.optimization_barrier((returned, advanced))
-    pairs = [(i, i ^ 1) for i in range(sec_count)]
     partner = lax.ppermute(returned, "sec", pairs)
     (new_columns,) = call(
         functools.partial(final_kernel, levels=levels, idle=col_count, held=held),

time: 44.5 us -> 43.1 us (0.969)
  Pallas kernels: 22.9 us -> 19.7 us
  waiting for transfers between devices: 9.63 us -> 11.7 us
    pallas_call x6 -> x5, Pallas kernels: 22.9 us -> 19.7 us  [call(): pl.pallas_call(kernel, out_shape=shapes, in_specs=[SPACES[space] for spac...]
    ppermute x0 -> x1, waiting for transfers between devices: none -> 1.49 us  [body(): other = lax.ppermute(received, 'sec', pairs)]
    all_to_all x1, waiting for transfers between devices: 4.01 us -> 4.59 us  [body(): lax.all_to_all(outgoing, 'col', split_axis=0, concat_axis=0, tiled=True)]
  transfers between devices with their start and end apart: 3 -> 4, of which waited for: 3 -> 4; matrix products, arithmetic and copies ran while one was open for 0% -> 0% of each run, Pallas kernels for 30% -> 24%
where the time goes in v6:
time: 43.1 us; the launch traced here: 42.7 us
  Pallas kernels  19.7 us (46%)
  waiting for transfers between devices  11.7 us (27%)
  starting transfers between devices  10.7 us (25%)
  between operations  0.67 us (2%)
    pallas_call x5, Pallas kernels, call(): pl.pallas_call(kernel, out_shape=shapes, in_specs=[SPACES[space] for spac...  19.7 us
    all_to_all x1, starting transfers between devices, body(): lax.all_to_all(outgoing, 'col', split_axis=0, concat_axis=0, tiled=True)  7.31 us
    all_to_all x1, waiting for transfers between devices, body(): lax.all_to_all(outgoing, 'col', split_axis=0, concat_axis=0, tiled=True)  4.59 us
    all_to_all x1, waiting for transfers between devices, body(): lax.all_to_all(back.reshape(sec_count * col_count, half, width), ('sec',...  4.08 us
    all_to_all x1, starting transfers between devices, body(): lax.all_to_all(back.reshape(sec_count * col_count, half, width), ('sec',...  3.39 us
    ppermute x1, waiting for transfers between devices, body(): partner = lax.ppermute(returned, 'sec', pairs)  1.53 us
    ppermute x1, waiting for transfers between devices, body(): other = lax.ppermute(received, 'sec', pairs)  1.49 us
  transfers between devices with their start and end apart: 4, of which 4 were waited for; matrix products, arithmetic and copies ran while one was open for 0% of the time, Pallas kernels for 24%

profile of v6, /device:TPU:0, one launch (start us, length us, event | category | flops | bytes accessed | tf_op | source)
XLA Modules:
  0.0 42.7 jit_solution(2247900453362644650)
XLA Ops:
  0.6 2.4 %host.1 = (f32[8,53,128]{2,1,0:T(8,128)}, f32[128,128]{1,0:T(8,128)}) custom-call(f32[256,128]{1,0:T(8,128)} %columns_far.1, f32[1,128]{1,0:T(1,128)} %bitcast.13, s32[4,64]{1,0:T(4,128)} %bitcast.11, s32[1,256]{1,0:T(1,128)} %bitcast.16, s32[1,256]{1,0:T(1,128)} %bitcast.18, f32[58,64]{1,0:T(8,128)} %map_far.1), custom_call_target="tpu_custom_call" | custom-call | tf_op jit(solution)/shard_map/host/pallas_call | solution.py:933
  3.1 7.3 %all-to-all-start = ((f32[8,53,128]{2,1,0:T(8,128)}), f32[8,53,128]{2,1,0:T(8,128)S(1)}, u32[]{:S(2)}, u32[]{:S(2)}) async-start(f32[8,53,128]{2,1,0:T(8,128)} %get-tuple-element.24), calls=%async_computation | async-start | bytes 458752 | tf_op jit(solution)/shard_map/all_to_all | solution.py:981
  10.4 3.8 %prepare.1 = (f32[82,32,128]{2,1,0:T(8,128)S(1)}, f32[2,88,128]{2,1,0:T(8,128)S(1)}, f32[88,128]{1,0:T(8,128)S(1)}, f32[82,32,128]{2,1,0:T(8,128)}, f32[256,128]...) custom-call(bf16[2,58,32,168]{3,2,1,0:T(8,128)(2,1)} %bitcast.8, ...), custom_call_target="tpu_custom_call" | custom-call | tf_op jit(solution)/shard_map/prepare/pallas_call | solution.py:933
  14.2 4.6 %all-to-all-done.received_ref = f32[8,53,128]{2,1,0:T(8,128)S(1)} async-done(((f32[8,53,128]{2,1,0:T(8,128)}), f32[8,53,128]{2,1,0:T(8,128)S(1)}, u32[]{:S(2)}, u32[]{:S(2)}) %all-to-all-start) | async-done | bytes 217120 | tf_op jit(solution)/shard_map/all_to_all | solution.py:981
  18.8 0.0 collective-permute-start
  18.8 1.5 %collective-permute-done.other_ref = f32[8,53,128]{2,1,0:T(8,128)S(1)} collective-permute-done((f32[8,53,128]{2,1,0:T(8,128)S(1)}, f32[8,53,128]{2,1,0:T(8,128)S(1)}, u32[]{:S(2)}, u32[]{:S(2)}) %collective-permute-start) | collective-permute-done | bytes 217120 | tf_op jit(solution)/shard_map/ppermute | solution.py:1031
  20.3 5.8 %water.1 = (f32[88,32,128]{2,1,0:T(8,128)}, f32[3,88,32,128]{3,2,1,0:T(8,128)}, f32[7,88,128]{2,1,0:T(8,128)}, f32[4,8,11,128]{3,2,1,0:T(8,128)}) custom-call(f32[8,53,128]{2,1,0:T(8,128)S(1)} %all-to-all-done.received_ref, f32[8,53,128]{2,1,0:T(8,128)S(1)} %collective-permute-done.other_ref, f32[82,32,128]{2,1,0:T(8,128)S(1)} %get-tuple-element.28.moved_ref, ...), custom_call_target="tpu_custom_call" | custom-call | tf_op jit(solution)/shard_map/water/pallas_call | solution.py:933
  26.1 3.4 %all-to-all-start.1 = ((f32[32,11,128]{2,1,0:T(8,128)}), f32[32,11,128]{2,1,0:T(8,128)S(1)}, u32[]{:S(2)}, u32[]{:S(2)}) async-start(f32[32,11,128]{2,1,0:T(8,128)} %bitcast.10), calls=%async_computation.1 | async-start | bytes 524288 | tf_op jit(solution)/shard_map/all_to_all | solution.py:1080
  29.5 6.3 %energy.1 = (bf16[2,58,32,168]{3,2,1,0:T(8,128)(2,1)}, f32[256,128]{1,0:T(8,128)S(1)}, f32[256,128]{1,0:T(8,128)S(1)}) custom-call(bf16[2,58,32,168]{3,2,1,0:T(8,128)(2,1)} %bitcast.9, f32[82,32,128]{2,1,0:T(8,128)} %get-tuple-element.34.energy_far, f32[88,32,128]{2,1,0:T(8,128)} %get-tuple-element.35.water_far, ...), custom_call_target="tpu_custom_call" | custom-call | tf_op jit(solution)/shard_map/energy/pallas_call | solution.py:933
  35.9 4.1 %all-to-all-done.1.mine_ref = f32[32,11,128]{2,1,0:T(8,128)S(1)} async-done(((f32[32,11,128]{2,1,0:T(8,128)}), f32[32,11,128]{2,1,0:T(8,128)S(1)}, u32[]{:S(2)}, u32[]{:S(2)}) %all-to-all-start.1) | async-done | bytes 180256 | tf_op jit(solution)/shard_map/all_to_all | solution.py:1080
  40.0 0.0 collective-permute-start.1
  40.0 1.5 %collective-permute-done.1.other_ref = f32[32,11,128]{2,1,0:T(8,128)S(1)} collective-permute-done((f32[32,11,128]{2,1,0:T(8,128)S(1)}, f32[32,11,128]{2,1,0:T(8,128)S(1)}, u32[]{:S(2)}, u32[]{:S(2)}) %collective-permute-start.1) | collective-permute-done | bytes 180256 | tf_op jit(solution)/shard_map/ppermute | solution.py:1129
  41.5 1.2 %final.1 = f32[256,128]{1,0:T(8,128)} custom-call(f32[256,128]{1,0:T(8,128)S(1)} %get-tuple-element.42.advanced_ref, f32[256,128]{1,0:T(8,128)S(1)} %get-tuple-element.43.places_ref, f32[32,11,128]{2,1,0:T(8,128)S(1)} %all-to-all-done.1.mine_ref, f32[32,11,128]{2,1,0:T(8,128)S(1)} %collective-permute-done.1.other_ref), custom_call_target="tpu_custom_call" | custom-call | tf_op jit(solution)/shard_map/final/pallas_call | solution.py:933
Async XLA Ops:
  3.1 15.7 %all-to-all-start = ((f32[8,53,128]{2,1,0:T(8,128)}), f32[8,53,128]{2,1,0:T(8,128)S(1)}, u32[]{:S(2)}, u32[]{:S(2)}) async-start(f32[8,53,128]{2,1,0:T(8,128)} %get-tuple-element.24), calls=%async_computation | async-start | bytes 458752 | tf_op jit(solution)/shard_map/all_to_all | solution.py:981
  18.8 1.5 %collective-permute-start = (f32[8,53,128]{2,1,0:T(8,128)S(1)}, f32[8,53,128]{2,1,0:T(8,128)S(1)}, u32[]{:S(2)}, u32[]{:S(2)}) collective-permute-start(f32[8,53,128]{2,1,0:T(8,128)S(1)} %all-to-all-done.received_ref), channel_id=1, source_target_pairs={{0,8},{8,0},{16,24},{24,16},{1,9},{9,1},{17,25},{25,17},{2,10},{10... | collective-permute-start | bytes 651272 | tf_op jit(solution)/shard_map/ppermute | solution.py:1031
  26.1 13.8 %all-to-all-start.1 = ((f32[32,11,128]{2,1,0:T(8,128)}), f32[32,11,128]{2,1,0:T(8,128)S(1)}, u32[]{:S(2)}, u32[]{:S(2)}) async-start(f32[32,11,128]{2,1,0:T(8,128)} %bitcast.10), calls=%async_computation.1 | async-start | bytes 524288 | tf_op jit(solution)/shard_map/all_to_all | solution.py:1080
  40.0 1.5 %collective-permute-start.1 = (f32[32,11,128]{2,1,0:T(8,128)S(1)}, f32[32,11,128]{2,1,0:T(8,128)S(1)}, u32[]{:S(2)}, u32[]{:S(2)}) collective-permute-start(f32[32,11,128]{2,1,0:T(8,128)S(1)} %all-to-all-done.1.mine_ref), channel_id=1, source_target_pairs={{0,8},{8,0},{16,24},{24,16},{1,9},{9,1},{17,25},{25,17},{2,10},{10... | collective-permute-start | bytes 540680 | tf_op jit(solution)/shard_map/ppermute | solution.py:1129

commit v7 on v6

--- a/solution.py
+++ b/solution.py
@@ -163,7 +163,8 @@
         ],
         axis=0,
     )
-    sent = product(select(pack, base, NN), fold_ref[...], NT) + select(pack, extras, NT)
+    folded = product(base, fold_ref[...], NT)
+    sent = select(pack, folded, NN) + select(pack, extras, NT)
     capacity = out_ref.shape[1] - share
     for c in range(col_count):
         out_ref[c, share:, :] = sent[c * padded : c * padded + capacity]
@@ -441,7 +442,7 @@
     base_far,
     weights_far,
     homes_far,
-    fold_far,
+    fold_ref,
     unfold_far,
     state_buf,
     natural_ref,
@@ -457,7 +458,6 @@
     base_ref,
     weights_ref,
     homes_ref,
-    fold_ref,
     unfold_ref,
     sems,
     in_sems,
@@ -485,7 +485,6 @@
         (base_ref, base_far),
         (weights_ref, weights_far),
         (homes_ref, homes_far),
-        (fold_ref, fold_far),
         (unfold_ref, unfold_far),
         (energy_buf, energy_far),
     )
@@ -518,7 +517,7 @@
         unfold_ref,
         **host,
     )
-    for copy in leaves[:5]:
+    for copy in leaves[:4]:
         copy.start()
     for f, scale, target in ((0, SHRINK, energy_buf), (1, 1.0, moved_ref)):
         loads[f].wait()
@@ -534,25 +533,68 @@
 
             sweep(s, lambda row: strided(natural_ref, row), work)
         if f == 0:
-            leaves[5].start()
+            leaves[4].start()
         means_ref[f] = folded_sums(sums_ref, columns) * (1.0 / scale)
     for copy in leaves:
         copy.wait()
 
 
+def neighbour_part(arrived, means, fold, share, parity, levels, stride, neighbours):
+    folded = product(fold, means, NT)
+    taken = arrived[stride - 1 : stride] > 0.0
+    ids = [
+        jnp.where(taken, arrived[levels + k : levels + k + 1], -1.0) for k in range(neighbours)
+    ]
+    total = None
+    chunk = min(256, means.shape[0])
+    for first in range(0, means.shape[0], chunk):
+        row = iota((chunk, arrived.shape[1]), 0) + first
+        element = (row + share * divided(row, share) + share * parity).astype(F32)
+        wanted = jnp.where(element == ids[0], 1.0, 0.0)
+        for k in range(1, neighbours):
+            wanted = wanted + jnp.where(element == ids[k], 1.0, 0.0)
+        part = folded[:, first : first + chunk]
+        term = select(wanted.astype(BF16), part, NN, swap=True)
+        total = term if total is None else total + term
+    return total
+
+
+def halves(ref, share):
+    return jnp.concatenate([ref[j, :share, :] for j in range(ref.shape[0])], axis=0)
+
+
+def arrive_kernel(
+    received_ref, fold_ref, arrived_ref, places_ref, *, segments, capacity, padded, **sizes
+):
+    hosts = received_ref.shape[0]
+    share = received_ref.shape[1] - capacity
+    places = slot_map(segments, hosts * padded, capacity, padded)
+    places_ref[...] = places
+    parts = []
+    for j in range(hosts):
+        parts.append(received_ref[j, share:, :])
+        if padded != capacity:
+            parts.append(jnp.zeros((padded - capacity, LANES), F32))
+    arrived = select(places, jnp.concatenate(parts, axis=0), TN, swap=True)
+    parity = lax.axis_index("sec") % 2
+    arrived_ref[...] = arrived + neighbour_part(
+        arrived, halves(received_ref, share), fold_ref[...], share, parity, **sizes
+    )
+
+
 def water_kernel(
-    received_ref,
+    arrived_ref,
+    places_ref,
     other_ref,
     moved_ref,
     means_ref,
     limits_ref,
-    fold_far,
+    fold_ref,
     unfold_far,
     water_far,
     spill_far,
     flats_far,
     back_far,
-    fold_ref,
     unfold_ref,
     even_ref,
     odd_ref,
@@ -565,14 +607,14 @@
     sums_ref,
     change_ref,
     back_ref,
-    in_sems,
+    in_sem,
     spill_sems,
     water_sem,
     flat_sem,
     back_sems,
     *,
     segments,
-    capacity,
+    share,
     padded,
     stride,
     levels,
@@ -580,38 +622,21 @@
 ):
     rows = means_ref.shape[1]
     columns = even_ref.shape[1]
-    loads = [
-        pltpu.make_async_copy(fold_far, fold_ref, in_sems.at[0]),
-        pltpu.make_async_copy(unfold_far, unfold_ref, in_sems.at[1]),
-    ]
-    for load in loads:
-        load.start()
-    hosts = received_ref.shape[0]
-    block = hosts * padded
-    places = slot_map(segments, block, capacity, padded)
-    share = received_ref.shape[1] - capacity
-    parts = []
-    for j in range(hosts):
-        parts.append(received_ref[j, share:, :])
-        if padded != capacity:
-            parts.append(jnp.zeros((padded - capacity, LANES), F32))
-    sent = jnp.concatenate(parts, axis=0)
-    means = joined_means(received_ref, other_ref, share, range(hosts))
-    arrived = select(places, sent, TN, swap=True)
-    loads[0].wait()
-    folded = product(fold_ref[...], means, NT)
-    taken = arrived[stride - 1 : stride] > 0.0
-    ids = [
-        jnp.where(taken, arrived[levels + k : levels + k + 1], -1.0) for k in range(neighbours)
-    ]
-    chunk = min(256, means.shape[0])
-    for first in range(0, means.shape[0], chunk):
-        element = (iota((chunk, arrived.shape[1]), 0) + first).astype(F32)
-        wanted = jnp.where(element == ids[0], 1.0, 0.0)
-        for k in range(1, neighbours):
-            wanted = wanted + jnp.where(element == ids[k], 1.0, 0.0)
-        part = folded[:, first : first + chunk]
-        arrived = arrived + select(wanted.astype(BF16), part, NN, swap=True)
+    load = pltpu.make_async_copy(unfold_far, unfold_ref, in_sem)
+    load.start()
+    hosts = other_ref.shape[0]
+    parity = 1 - lax.axis_index("sec") % 2
+    arrived = arrived_ref[...]
+    arrived = arrived + neighbour_part(
+        arrived,
+        halves(other_ref, share),
+        fold_ref[...],
+        share,
+        parity,
+        levels,
+        stride,
+        neighbours,
+    )
     goal_ref[...] = jnp.zeros_like(goal_ref)
     flats_ref[...] = jnp.zeros_like(flats_ref)
     sums_ref[...] = jnp.zeros_like(sums_ref)
@@ -713,8 +738,8 @@
                 first, number = f * stride + g * s.steps, s.group_steps(g)
                 part = turn(change[s.rows[0] : s.rows[0] + number], -g * s.width)
                 change_ref[first : first + number, t * LANES : (t + 1) * LANES] = part
-    spread = select(places, change_ref[...], NT)
-    loads[1].wait()
+    spread = select(places_ref[...], change_ref[...], NT)
+    load.wait()
     back = product(spread, unfold_ref[...], NN)
     half = back_ref.shape[2]
     for h in range(2):
@@ -742,7 +767,7 @@
     other_ref,
     out_ref,
     advanced_ref,
-    places_ref,
+    picks_ref,
     state_buf,
     energy_buf,
     water_buf,
@@ -751,6 +776,7 @@
     base_ref,
     weights_ref,
     mixing_ref,
+    homes_ref,
     out_buf,
     even_ref,
     odd_ref,
@@ -772,7 +798,7 @@
         (mixing_far, mixing_ref),
         (water_far, water_buf),
         (energy_far, energy_buf),
-        (homes_far, places_ref),
+        (homes_far, homes_ref),
     )
     loads = [pltpu.make_async_copy(x, y, in_sems.at[i]) for i, (x, y) in enumerate(pairs)]
     flats, bases, shares, mixings, waters, first, homes = loads
@@ -894,13 +920,15 @@
     states[0].wait()
     finish_field(0, source)
     homes.wait()
+    place = homes_ref[:, :1].astype(I32)
+    picks_ref[...] = jnp.where(iota(picks_ref.shape, 1) == place, 1.0, 0.0).astype(BF16)
     for f in range(fields):
         for part in range(2):
             leave(f, part).wait()
 
 
 def final_kernel(
-    advanced_ref, places_ref, mine_ref, other_ref, out_ref, table_ref, *, levels, idle, held
+    advanced_ref, picks_ref, mine_ref, other_ref, out_ref, table_ref, *, levels, idle, held
 ):
     rows, width = advanced_ref.shape
     sources, half, _ = mine_ref.shape
@@ -911,9 +939,7 @@
         for j in range(clouds):
             first = (i * clouds + j) * held
             table_ref[first : first + half, :] = ref[idle + j]
-    place = places_ref[:, :1].astype(I32)
-    picks = jnp.where(iota((rows, table_ref.shape[0]), 1) == place, 1.0, 0.0)
-    summed = advanced_ref[...] + select(picks.astype(BF16), table_ref[...], NN)
+    summed = advanced_ref[...] + select(picks_ref[...], table_ref[...], NN)
     water = divided(iota((rows, width), 1), levels) == 1
     out_ref[...] = jnp.where(water, jnp.maximum(summed, 0.0), summed)
 
@@ -1000,7 +1026,7 @@
             ("far", (count, width), F32),
             ("far", (count, 3 * elements), BF16),
             ("far", (count, LANES), F32),
-            ("far", (width, width), F32),
+            ("near", (width, width), F32),
             ("far", (width, width), F32),
         ],
         scratch=[
@@ -1019,34 +1045,37 @@
             pltpu.VMEM((count, 3 * elements), BF16),
             pltpu.VMEM((count, LANES), F32),
             pltpu.VMEM((width, width), F32),
-            pltpu.VMEM((width, width), F32),
             dma((fields,)),
             dma((6,)),
-            dma((6,)),
+            dma((5,)),
         ],
         limit=16,
     )
     received, moved, base = lax.optimization_barrier((received, moved, base))
     pairs = [(i, i ^ 1) for i in range(sec_count)]
     other = lax.ppermute(received, "sec", pairs)
+    sizes = dict(stride=levels, levels=cloud_levels, neighbours=neighbours.shape[1])
+    arrived, places = call(
+        functools.partial(
+            arrive_kernel, segments=segments, capacity=capacity, padded=padded, **sizes
+        ),
+        "arrive",
+        [("near", received), ("near", fold)],
+        [("near", (width, mapped), F32), ("near", (block, mapped), BF16)],
+    )
     water, spill, flats, back = call(
         functools.partial(
-            water_kernel,
-            segments=segments,
-            capacity=capacity,
-            padded=padded,
-            stride=levels,
-            levels=cloud_levels,
-            neighbours=neighbours.shape[1],
+            water_kernel, segments=segments, share=elements // 2, padded=padded, **sizes
         ),
         "water",
         [
-            ("near", received),
+            ("near", arrived),
+            ("near", places),
             ("near", other),
             ("near", moved),
             ("near", cloud_means),
             ("near", limits),
-            ("far", fold),
+            ("near", fold),
             ("far", unfold),
         ],
         [
@@ -1056,7 +1085,6 @@
             ("far", (sec_count, col_count, half, width), F32),
         ],
         scratch=[
-            pltpu.VMEM((width, width), F32),
             pltpu.VMEM((width, width), F32),
             wide(),
             wide(),
@@ -1069,7 +1097,7 @@
             pltpu.VMEM((rows * 8, LANES), F32),
             pltpu.VMEM((width, mapped), F32),
             pltpu.VMEM((2, col_count, half, width), F32),
-            dma((2,)),
+            dma(()),
             dma((MAX_SUB - 1,)),
             dma(()),
             dma(()),
@@ -1084,7 +1112,7 @@
         concat_axis=0,
         tiled=True,
     )
-    new_block, advanced, places = call(
+    new_block, advanced, picks = call(
         functools.partial(energy_kernel, segments=segments, share=elements // 2),
         "energy",
         [
@@ -1103,7 +1131,7 @@
         [
             ("far", state.shape, BF16),
             ("near", (count, width), F32),
-            ("near", (count, LANES), F32),
+            ("near", (count, 2 * clouds * held), BF16),
         ],
         scratch=[
             pltpu.VMEM(state.shape, BF16),
@@ -1114,6 +1142,7 @@
             pltpu.VMEM((count, width), F32),
             pltpu.VMEM((count, 3 * elements), BF16),
             pltpu.VMEM((1, width), F32),
+            pltpu.VMEM((count, LANES), F32),
             pltpu.VMEM(state.shape, BF16),
             wide(),
             wide(),
@@ -1130,7 +1159,7 @@
     (new_columns,) = call(
         functools.partial(final_kernel, levels=levels, idle=col_count, held=held),
         "final",
-        [("near", advanced), ("near", places), ("near", returned), ("near", partner)],
+        [("near", advanced), ("near", picks), ("near", returned), ("near", partner)],
         [("auto", (count, width), F32)],
         scratch=[pltpu.VMEM((2 * clouds * held, width), F32)],
     )

time: 43.1 us -> 41.9 us (0.972)
  waiting for transfers between devices: 11.7 us -> 11 us
  Pallas kernels: 19.7 us -> 19.2 us
    ppermute x1, waiting for transfers between devices: 1.49 us -> 0.84 us  [body(): other = lax.ppermute(received, 'sec', pairs)]
    pallas_call x5 -> x6, Pallas kernels: 19.7 us -> 19.2 us  [call(): pl.pallas_call(kernel, out_shape=shapes, in_specs=[SPACES[space] for spac...]
  transfers between devices with their start and end apart: 4 -> 4, of which waited for: 4 -> 4; matrix products, arithmetic and copies ran while one was open for 0% -> 0% of each run, Pallas kernels for 24% -> 26%
where the time goes in v7:
time: 41.9 us; the launch traced here: 41.5 us
  Pallas kernels  19.2 us (46%)
  waiting for transfers between devices  11 us (26%)
  starting transfers between devices  10.7 us (26%)
  between operations  0.67 us (2%)
    pallas_call x6, Pallas kernels, call(): pl.pallas_call(kernel, out_shape=shapes, in_specs=[SPACES[space] for spac...  19.2 us
    all_to_all x1, starting transfers between devices, body(): lax.all_to_all(outgoing, 'col', split_axis=0, concat_axis=0, tiled=True)  7.31 us
    all_to_all x1, waiting for transfers between devices, body(): lax.all_to_all(outgoing, 'col', split_axis=0, concat_axis=0, tiled=True)  4.58 us
    all_to_all x1, waiting for transfers between devices, body(): lax.all_to_all(back.reshape(sec_count * col_count, half, width), ('sec',...  4.05 us
    all_to_all x1, starting transfers between devices, body(): lax.all_to_all(back.reshape(sec_count * col_count, half, width), ('sec',...  3.39 us
    ppermute x1, waiting for transfers between devices, body(): partner = lax.ppermute(returned, 'sec', pairs)  1.53 us
    ppermute x1, waiting for transfers between devices, body(): other = lax.ppermute(received, 'sec', pairs)  0.84 us
  transfers between devices with their start and end apart: 4, of which 4 were waited for; matrix products, arithmetic and copies ran while one was open for 0% of the time, Pallas kernels for 26%

profile of v7, /device:TPU:0, one launch (start us, length us, event | category | flops | bytes accessed | tf_op | source)
XLA Modules:
  0.0 41.5 jit_solution(16029730742688532609)
XLA Ops:
  0.6 2.5 %host.1 = (f32[8,53,128]{2,1,0:T(8,128)}, f32[128,128]{1,0:T(8,128)}) custom-call(f32[256,128]{1,0:T(8,128)} %columns_far.1, f32[1,128]{1,0:T(1,128)} %bitcast.13, s32[4,64]{1,0:T(4,128)} %bitcast.11, s32[1,256]{1,0:T(1,128)} %bitcast.16, s32[1,256]{1,0:T(1,128)} %bitcast.18, f32[58,64]{1,0:T(8,128)} %map_far.1), custom_call_target="tpu_custom_call" | custom-call | tf_op jit(solution)/shard_map/host/pallas_call | solution.py:959
  3.2 7.3 %all-to-all-start = ((f32[8,53,128]{2,1,0:T(8,128)}), f32[8,53,128]{2,1,0:T(8,128)S(1)}, u32[]{:S(2)}, u32[]{:S(2)}) async-start(f32[8,53,128]{2,1,0:T(8,128)} %get-tuple-element.26), calls=%async_computation | async-start | bytes 458752 | tf_op jit(solution)/shard_map/all_to_all | solution.py:1007
  10.5 3.8 %prepare.1 = (f32[82,32,128]{2,1,0:T(8,128)S(1)}, f32[2,88,128]{2,1,0:T(8,128)S(1)}, f32[88,128]{1,0:T(8,128)S(1)}, f32[82,32,128]{2,1,0:T(8,128)}, f32[256,128]...) custom-call(bf16[2,58,32,168]{3,2,1,0:T(8,128)(2,1)} %bitcast.8, ...), custom_call_target="tpu_custom_call" | custom-call | tf_op jit(solution)/shard_map/prepare/pallas_call | solution.py:959
  14.3 4.6 %all-to-all-done.received_ref = f32[8,53,128]{2,1,0:T(8,128)S(1)} async-done(((f32[8,53,128]{2,1,0:T(8,128)}), f32[8,53,128]{2,1,0:T(8,128)S(1)}, u32[]{:S(2)}, u32[]{:S(2)}) %all-to-all-start) | async-done | bytes 217120 | tf_op jit(solution)/shard_map/all_to_all | solution.py:1007
  18.9 0.0 collective-permute-start
  18.9 0.6 %arrive.1 = (f32[128,256]{1,0:T(8,128)S(1)}, bf16[192,256]{1,0:T(8,128)(2,1)S(1)}) custom-call(f32[8,53,128]{2,1,0:T(8,128)S(1)} %all-to-all-done.received_ref, f32[128,128]{1,0:T(8,128)S(1)} %get-tuple-element.30.fold_ref), custom_call_target="tpu_custom_call" | custom-call | tf_op jit(solution)/shard_map/arrive/pallas_call | solution.py:959
  19.6 0.8 %collective-permute-done.other_ref = f32[8,53,128]{2,1,0:T(8,128)S(1)} collective-permute-done((f32[8,53,128]{2,1,0:T(8,128)S(1)}, f32[8,53,128]{2,1,0:T(8,128)S(1)}, u32[]{:S(2)}, u32[]{:S(2)}) %collective-permute-start) | collective-permute-done | bytes 217120 | tf_op jit(solution)/shard_map/ppermute | solution.py:1056
  20.4 4.6 %water.1 = (f32[88,32,128]{2,1,0:T(8,128)}, f32[3,88,32,128]{3,2,1,0:T(8,128)}, f32[7,88,128]{2,1,0:T(8,128)}, f32[4,8,11,128]{3,2,1,0:T(8,128)}) custom-call(f32[128,256]{1,0:T(8,128)S(1)} %get-tuple-element.31.arrived_ref, bf16[192,256]{1,0:T(8,128)(2,1)S(1)} %get-tuple-element.32.places_ref, f32[8,53,128]{2,1,0:T(8,128)S(1)} %collective-permute-done.other_ref, ...), custom_call_target="tpu_custom_call" | custom-call | tf_op jit(solution)/shard_map/water/pallas_call | solution.py:959
  25.0 3.4 %all-to-all-start.1 = ((f32[32,11,128]{2,1,0:T(8,128)}), f32[32,11,128]{2,1,0:T(8,128)S(1)}, u32[]{:S(2)}, u32[]{:S(2)}) async-start(f32[32,11,128]{2,1,0:T(8,128)} %bitcast.10), calls=%async_computation.1 | async-start | bytes 524288 | tf_op jit(solution)/shard_map/all_to_all | solution.py:1108
  28.4 6.4 %energy.1 = (bf16[2,58,32,168]{3,2,1,0:T(8,128)(2,1)}, f32[256,128]{1,0:T(8,128)S(1)}, bf16[256,768]{1,0:T(8,128)(2,1)S(1)}) custom-call(bf16[2,58,32,168]{3,2,1,0:T(8,128)(2,1)} %bitcast.9, f32[82,32,128]{2,1,0:T(8,128)} %get-tuple-element.38.energy_far, f32[88,32,128]{2,1,0:T(8,128)} %get-tuple-element.39.water_far, ...), custom_call_target="tpu_custom_call" | custom-call | tf_op jit(solution)/shard_map/energy/pallas_call | solution.py:959
  34.8 4.1 %all-to-all-done.1.mine_ref = f32[32,11,128]{2,1,0:T(8,128)S(1)} async-done(((f32[32,11,128]{2,1,0:T(8,128)}), f32[32,11,128]{2,1,0:T(8,128)S(1)}, u32[]{:S(2)}, u32[]{:S(2)}) %all-to-all-start.1) | async-done | bytes 180256 | tf_op jit(solution)/shard_map/all_to_all | solution.py:1108
  38.8 0.0 collective-permute-start.1
  38.8 1.5 %collective-permute-done.1.other_ref = f32[32,11,128]{2,1,0:T(8,128)S(1)} collective-permute-done((f32[32,11,128]{2,1,0:T(8,128)S(1)}, f32[32,11,128]{2,1,0:T(8,128)S(1)}, u32[]{:S(2)}, u32[]{:S(2)}) %collective-permute-start.1) | collective-permute-done | bytes 180256 | tf_op jit(solution)/shard_map/ppermute | solution.py:1158
  40.4 1.2 %final.1 = f32[256,128]{1,0:T(8,128)} custom-call(f32[256,128]{1,0:T(8,128)S(1)} %get-tuple-element.46.advanced_ref, bf16[256,768]{1,0:T(8,128)(2,1)S(1)} %get-tuple-element.47.picks_ref, f32[32,11,128]{2,1,0:T(8,128)S(1)} %all-to-all-done.1.mine_ref, f32[32,11,128]{2,1,0:T(8,128)S(1)} %collective-permute-done.1.other_ref), custom_call_target="tpu_custom_call" | custom-call | tf_op jit(solution)/shard_map/final/pallas_call | solution.py:959
Async XLA Ops:
  3.2 15.7 %all-to-all-start = ((f32[8,53,128]{2,1,0:T(8,128)}), f32[8,53,128]{2,1,0:T(8,128)S(1)}, u32[]{:S(2)}, u32[]{:S(2)}) async-start(f32[8,53,128]{2,1,0:T(8,128)} %get-tuple-element.26), calls=%async_computation | async-start | bytes 458752 | tf_op jit(solution)/shard_map/all_to_all | solution.py:1007
  18.9 1.5 %collective-permute-start = (f32[8,53,128]{2,1,0:T(8,128)S(1)}, f32[8,53,128]{2,1,0:T(8,128)S(1)}, u32[]{:S(2)}, u32[]{:S(2)}) collective-permute-start(f32[8,53,128]{2,1,0:T(8,128)S(1)} %all-to-all-done.received_ref), channel_id=1, source_target_pairs={{0,8},{8,0},{16,24},{24,16},{1,9},{9,1},{17,25},{25,17},{2,10},{10... | collective-permute-start | bytes 651272 | tf_op jit(solution)/shard_map/ppermute | solution.py:1056
  25.0 13.8 %all-to-all-start.1 = ((f32[32,11,128]{2,1,0:T(8,128)}), f32[32,11,128]{2,1,0:T(8,128)S(1)}, u32[]{:S(2)}, u32[]{:S(2)}) async-start(f32[32,11,128]{2,1,0:T(8,128)} %bitcast.10), calls=%async_computation.1 | async-start | bytes 524288 | tf_op jit(solution)/shard_map/all_to_all | solution.py:1108
  38.8 1.5 %collective-permute-start.1 = (f32[32,11,128]{2,1,0:T(8,128)S(1)}, f32[32,11,128]{2,1,0:T(8,128)S(1)}, u32[]{:S(2)}, u32[]{:S(2)}) collective-permute-start(f32[32,11,128]{2,1,0:T(8,128)S(1)} %all-to-all-done.1.mine_ref), channel_id=1, source_target_pairs={{0,8},{8,0},{16,24},{24,16},{1,9},{9,1},{17,25},{25,17},{2,10},{10... | collective-permute-start | bytes 540680 | tf_op jit(solution)/shard_map/ppermute | solution.py:1158

commit v8 on v7

--- a/solution.py
+++ b/solution.py
@@ -12,6 +12,7 @@
 HORIZ = 0.12
 VERTIC = 0.1
 LATENT = 2.5
+GROW = 20.0
 VMIX = 0.2
 HIGH = lax.Precision.HIGHEST
 LANES = 128
@@ -163,8 +164,7 @@
         ],
         axis=0,
     )
-    folded = product(base, fold_ref[...], NT)
-    sent = select(pack, folded, NN) + select(pack, extras, NT)
+    sent = product(select(pack, base, NN), fold_ref[...], NT) + select(pack, extras, NT)
     capacity = out_ref.shape[1] - share
     for c in range(col_count):
         out_ref[c, share:, :] = sent[c * padded : c * padded + capacity]
@@ -493,7 +493,7 @@
         copy.wait()
     tall = flat_ref.shape[0]
     here = iota((tall, levels), 0) == iota((tall, levels), 1)
-    diagonal = jnp.where(here, 0.5 * saturation_ref[...], 0.0)
+    diagonal = jnp.where(here, saturation_ref[...], 0.0)
     flat_ref[...] = select(jnp.ones((levels, LANES), BF16), diagonal, NN, swap=True)
     limits_ref[...] = jnp.zeros_like(limits_ref)
     for s in segments:
@@ -659,7 +659,7 @@
     copies = []
     source, target = None, even_ref
     for n in range(MAX_SUB):
-        scale = 10.0 ** (n + 1)
+        scale = 0.5 * GROW ** (n + 1)
         last = n + 1 == MAX_SUB
         expected = []
         for f in range(2):
@@ -689,14 +689,14 @@
                 total = None
                 for j in range(4):
                     v = lin[j] + shift
-                    c = jnp.maximum(0.5 * v - limit, 0.0)
-                    total = c if total is None else total + c
+                    low = jnp.minimum(v, limit)
+                    total = low if total is None else total + low
                     if last:
                         continue
-                    u = v - c
+                    u = v + low
                     if old is not None:
                         u = jnp.where(active, u, old[j])
-                    spill_buf[n, row, pl.ds(8 * j, 8), :] = c
+                    spill_buf[n, row, pl.ds(8 * j, 8), :] = v - low
                     target[row, pl.ds(8 * j, 8), :] = u
                 sums_ref[slab(row), :] = total
 
@@ -725,7 +725,7 @@
         if n + 2 == MAX_SUB:
             copies.append(pltpu.make_async_copy(source, water_far, water_sem))
             copies[-1].start()
-        spilled = folded_sums(sums_ref, columns) * (1.0 / scale)
+        spilled = 0.5 * (expected[1] - folded_sums(sums_ref, columns) * (1.0 / scale))
         step = [expected[0] + LATENT * spilled, expected[1] - spilled]
         keep = counts[...] > float(n)
         for f in range(2):
@@ -828,7 +828,7 @@
             count = spread_row(counts, s.rows[0])
             back = jnp.zeros((8, LANES), F32)
             for n in range(1, MAX_SUB + 1):
-                scale = 10.0**-n * (LATENT if f == 0 else 1.0)
+                scale = GROW**-n * (LATENT if f == 0 else 1.0)
                 back = jnp.where(count == float(n), scale, back)
             at = slice(s.lane0, s.lane0 + s.width)
             held = jnp.broadcast_to(count[0:1, : s.width], (columns, s.width)) > 0.0
@@ -878,9 +878,9 @@
             limit = spread_row(flats_ref.at[MAX_SUB + 1], row)
             for j in range(4):
                 v = water[j] + push
-                c = jnp.maximum(0.5 * v - limit, 0.0)
-                spill_buf[final, row, pl.ds(8 * j, 8), :] = c
-                even_ref[row, pl.ds(8 * j, 8), :] = jnp.where(active, v - c, here[j])
+                low = jnp.minimum(v, limit)
+                spill_buf[final, row, pl.ds(8 * j, 8), :] = v - low
+                even_ref[row, pl.ds(8 * j, 8), :] = jnp.where(active, v + low, here[j])
 
         sweep(s, lambda row: groups(water_buf, (row,)), last)
     states[1].wait()
@@ -899,7 +899,7 @@
                     shift = spread_row(flats_ref.at[n], row)
                     lin, spill = groups(energy_buf, (row,)), groups(spill_buf, (n, row))
                     for j in range(4):
-                        target[row, pl.ds(8 * j, 8), :] = (lin[j] + shift) + spill[j]
+                        target[row, pl.ds(8 * j, 8), :] = 2.0 * (lin[j] + shift) + spill[j]
                 return carry
 
             def work(row, below, here, above):
@@ -907,7 +907,7 @@
                 lin = linear(below, here, above)
                 spill = groups(spill_buf, (n, row))
                 for j in range(4):
-                    u = (lin[j] + shift) + spill[j]
+                    u = 2.0 * (lin[j] + shift) + spill[j]
                     target[row, pl.ds(8 * j, 8), :] = jnp.where(active, u, here[j])
 
             if n == 0:
@@ -927,20 +927,25 @@
             leave(f, part).wait()
 
 
-def final_kernel(
-    advanced_ref, picks_ref, mine_ref, other_ref, out_ref, table_ref, *, levels, idle, held
-):
-    rows, width = advanced_ref.shape
-    sources, half, _ = mine_ref.shape
-    clouds = sources - idle
+def gather_half(picks_ref, half_ref, table_ref, idle, part):
+    sources, half, _ = half_ref.shape
+    height = table_ref.shape[0]
+    held = height // (sources - idle)
     if half != held:
         table_ref[...] = jnp.zeros_like(table_ref)
-    for i, ref in enumerate((mine_ref, other_ref)):
-        for j in range(clouds):
-            first = (i * clouds + j) * held
-            table_ref[first : first + half, :] = ref[idle + j]
-    summed = advanced_ref[...] + select(picks_ref[...], table_ref[...], NN)
-    water = divided(iota((rows, width), 1), levels) == 1
+    for j in range(sources - idle):
+        table_ref[j * held : j * held + half, :] = half_ref[idle + j]
+    picks = picks_ref[:, part * height : (part + 1) * height]
+    return select(picks, table_ref[...], NN)
+
+
+def nearly_kernel(advanced_ref, picks_ref, mine_ref, out_ref, table_ref, *, idle):
+    out_ref[...] = advanced_ref[...] + gather_half(picks_ref, mine_ref, table_ref, idle, 0)
+
+
+def final_kernel(nearly_ref, picks_ref, other_ref, out_ref, table_ref, *, levels, idle):
+    summed = nearly_ref[...] + gather_half(picks_ref, other_ref, table_ref, idle, 1)
+    water = divided(iota(summed.shape, 1), levels) == 1
     out_ref[...] = jnp.where(water, jnp.maximum(summed, 0.0), summed)
 
 
@@ -1156,12 +1161,20 @@
     )
     returned, advanced = lax.optimization_barrier((returned, advanced))
     partner = lax.ppermute(returned, "sec", pairs)
+    table = pltpu.VMEM((clouds * held, width), F32)
+    (nearly,) = call(
+        functools.partial(nearly_kernel, idle=col_count),
+        "nearly",
+        [("near", advanced), ("near", picks), ("near", returned)],
+        [("near", (count, width), F32)],
+        scratch=[table],
+    )
     (new_columns,) = call(
-        functools.partial(final_kernel, levels=levels, idle=col_count, held=held),
+        functools.partial(final_kernel, levels=levels, idle=col_count),
         "final",
-        [("near", advanced), ("near", picks), ("near", returned), ("near", partner)],
+        [("near", nearly), ("near", picks), ("near", partner)],
         [("auto", (count, width), F32)],
-        scratch=[pltpu.VMEM((2 * clouds * held, width), F32)],
+        scratch=[table],
     )
     return new_columns, new_block[None]
 

time: 41.9 us -> 41.4 us (0.988)
    pallas_call x6 -> x7, Pallas kernels: 19.2 us -> 19.1 us  [call(): pl.pallas_call(kernel, out_shape=shapes, in_specs=[SPACES[space] for spac...]
  transfers between devices with their start and end apart: 4 -> 4, of which waited for: 4 -> 4; matrix products, arithmetic and copies ran while one was open for 0% -> 0% of each run, Pallas kernels for 26% -> 27%
where the time goes in v8:
time: 41.4 us; the launch traced here: 41.1 us
  Pallas kernels  19.1 us (46%)
  starting transfers between devices  10.7 us (26%)
  waiting for transfers between devices  10.6 us (26%)
  between operations  0.68 us (2%)
    pallas_call x7, Pallas kernels, call(): pl.pallas_call(kernel, out_shape=shapes, in_specs=[SPACES[space] for spac...  19.1 us
    all_to_all x1, starting transfers between devices, body(): lax.all_to_all(outgoing, 'col', split_axis=0, concat_axis=0, tiled=True)  7.31 us
    all_to_all x1, waiting for transfers between devices, body(): lax.all_to_all(outgoing, 'col', split_axis=0, concat_axis=0, tiled=True)  4.59 us
    all_to_all x1, waiting for transfers between devices, body(): lax.all_to_all(back.reshape(sec_count * col_count, half, width), ('sec',...  3.96 us
    all_to_all x1, starting transfers between devices, body(): lax.all_to_all(back.reshape(sec_count * col_count, half, width), ('sec',...  3.39 us
    ppermute x1, waiting for transfers between devices, body(): partner = lax.ppermute(returned, 'sec', pairs)  1.2 us
    ppermute x1, waiting for transfers between devices, body(): other = lax.ppermute(received, 'sec', pairs)  0.84 us
  transfers between devices with their start and end apart: 4, of which 4 were waited for; matrix products, arithmetic and copies ran while one was open for 0% of the time, Pallas kernels for 27%

profile of v8, /device:TPU:0, one launch (start us, length us, event | category | flops | bytes accessed | tf_op | source)
XLA Modules:
  0.0 41.1 jit_solution(15774256122798912415)
XLA Ops:
  0.6 2.4 %host.1 = (f32[8,53,128]{2,1,0:T(8,128)}, f32[128,128]{1,0:T(8,128)}) custom-call(f32[256,128]{1,0:T(8,128)} %columns_far.1, f32[1,128]{1,0:T(1,128)} %bitcast.13, s32[4,64]{1,0:T(4,128)} %bitcast.11, s32[1,256]{1,0:T(1,128)} %bitcast.16, s32[1,256]{1,0:T(1,128)} %bitcast.18, f32[58,64]{1,0:T(8,128)} %map_far.1), custom_call_target="tpu_custom_call" | custom-call | tf_op jit(solution)/shard_map/host/pallas_call | solution.py:964
  3.1 7.3 %all-to-all-start = ((f32[8,53,128]{2,1,0:T(8,128)}), f32[8,53,128]{2,1,0:T(8,128)S(1)}, u32[]{:S(2)}, u32[]{:S(2)}) async-start(f32[8,53,128]{2,1,0:T(8,128)} %get-tuple-element.26), calls=%async_computation | async-start | bytes 458752 | tf_op jit(solution)/shard_map/all_to_all | solution.py:1012
  10.4 3.8 %prepare.1 = (f32[82,32,128]{2,1,0:T(8,128)S(1)}, f32[2,88,128]{2,1,0:T(8,128)S(1)}, f32[88,128]{1,0:T(8,128)S(1)}, f32[82,32,128]{2,1,0:T(8,128)}, f32[256,128]...) custom-call(bf16[2,58,32,168]{3,2,1,0:T(8,128)(2,1)} %bitcast.8, ...), custom_call_target="tpu_custom_call" | custom-call | tf_op jit(solution)/shard_map/prepare/pallas_call | solution.py:964
  14.2 4.6 %all-to-all-done.received_ref = f32[8,53,128]{2,1,0:T(8,128)S(1)} async-done(((f32[8,53,128]{2,1,0:T(8,128)}), f32[8,53,128]{2,1,0:T(8,128)S(1)}, u32[]{:S(2)}, u32[]{:S(2)}) %all-to-all-start) | async-done | bytes 217120 | tf_op jit(solution)/shard_map/all_to_all | solution.py:1012
  18.8 0.0 collective-permute-start
  18.8 0.6 %arrive.1 = (f32[128,256]{1,0:T(8,128)S(1)}, bf16[192,256]{1,0:T(8,128)(2,1)S(1)}) custom-call(f32[8,53,128]{2,1,0:T(8,128)S(1)} %all-to-all-done.received_ref, f32[128,128]{1,0:T(8,128)S(1)} %get-tuple-element.30.fold_ref), custom_call_target="tpu_custom_call" | custom-call | tf_op jit(solution)/shard_map/arrive/pallas_call | solution.py:964
  19.5 0.8 %collective-permute-done.other_ref = f32[8,53,128]{2,1,0:T(8,128)S(1)} collective-permute-done((f32[8,53,128]{2,1,0:T(8,128)S(1)}, f32[8,53,128]{2,1,0:T(8,128)S(1)}, u32[]{:S(2)}, u32[]{:S(2)}) %collective-permute-start) | collective-permute-done | bytes 217120 | tf_op jit(solution)/shard_map/ppermute | solution.py:1061
  20.3 4.4 %water.1 = (f32[88,32,128]{2,1,0:T(8,128)}, f32[3,88,32,128]{3,2,1,0:T(8,128)}, f32[7,88,128]{2,1,0:T(8,128)}, f32[4,8,11,128]{3,2,1,0:T(8,128)}) custom-call(f32[128,256]{1,0:T(8,128)S(1)} %get-tuple-element.31.arrived_ref, bf16[192,256]{1,0:T(8,128)(2,1)S(1)} %get-tuple-element.32.places_ref, f32[8,53,128]{2,1,0:T(8,128)S(1)} %collective-permute-done.other_ref, ...), custom_call_target="tpu_custom_call" | custom-call | tf_op jit(solution)/shard_map/water/pallas_call | solution.py:964
  24.7 3.4 %all-to-all-start.1 = ((f32[32,11,128]{2,1,0:T(8,128)}), f32[32,11,128]{2,1,0:T(8,128)S(1)}, u32[]{:S(2)}, u32[]{:S(2)}) async-start(f32[32,11,128]{2,1,0:T(8,128)} %bitcast.10), calls=%async_computation.1 | async-start | bytes 524288 | tf_op jit(solution)/shard_map/all_to_all | solution.py:1113
  28.1 6.5 %energy.1 = (bf16[2,58,32,168]{3,2,1,0:T(8,128)(2,1)}, f32[256,128]{1,0:T(8,128)S(1)}, bf16[256,768]{1,0:T(8,128)(2,1)S(1)}) custom-call(bf16[2,58,32,168]{3,2,1,0:T(8,128)(2,1)} %bitcast.9, f32[82,32,128]{2,1,0:T(8,128)} %get-tuple-element.38.energy_far, f32[88,32,128]{2,1,0:T(8,128)} %get-tuple-element.39.water_far, ...), custom_call_target="tpu_custom_call" | custom-call | tf_op jit(solution)/shard_map/energy/pallas_call | solution.py:964
  34.6 4.0 %all-to-all-done.1.mine_ref = f32[32,11,128]{2,1,0:T(8,128)S(1)} async-done(((f32[32,11,128]{2,1,0:T(8,128)}), f32[32,11,128]{2,1,0:T(8,128)S(1)}, u32[]{:S(2)}, u32[]{:S(2)}) %all-to-all-start.1) | async-done | bytes 180256 | tf_op jit(solution)/shard_map/all_to_all | solution.py:1113
  38.5 0.0 collective-permute-start.1
  38.5 0.3 nearly.1.nearly_ref
  38.9 1.2 %collective-permute-done.1.other_ref = f32[32,11,128]{2,1,0:T(8,128)S(1)} collective-permute-done((f32[32,11,128]{2,1,0:T(8,128)S(1)}, f32[32,11,128]{2,1,0:T(8,128)S(1)}, u32[]{:S(2)}, u32[]{:S(2)}) %collective-permute-start.1) | collective-permute-done | bytes 180256 | tf_op jit(solution)/shard_map/ppermute | solution.py:1163
  40.1 1.0 %final.1 = f32[256,128]{1,0:T(8,128)} custom-call(f32[256,128]{1,0:T(8,128)S(1)} %nearly.1.nearly_ref, bf16[256,768]{1,0:T(8,128)(2,1)S(1)} %get-tuple-element.47.picks_ref, f32[32,11,128]{2,1,0:T(8,128)S(1)} %collective-permute-done.1.other_ref), custom_call_target="tpu_custom_call" | custom-call | tf_op jit(solution)/shard_map/final/pallas_call | solution.py:964
Async XLA Ops:
  3.1 15.7 %all-to-all-start = ((f32[8,53,128]{2,1,0:T(8,128)}), f32[8,53,128]{2,1,0:T(8,128)S(1)}, u32[]{:S(2)}, u32[]{:S(2)}) async-start(f32[8,53,128]{2,1,0:T(8,128)} %get-tuple-element.26), calls=%async_computation | async-start | bytes 458752 | tf_op jit(solution)/shard_map/all_to_all | solution.py:1012
  18.8 1.5 %collective-permute-start = (f32[8,53,128]{2,1,0:T(8,128)S(1)}, f32[8,53,128]{2,1,0:T(8,128)S(1)}, u32[]{:S(2)}, u32[]{:S(2)}) collective-permute-start(f32[8,53,128]{2,1,0:T(8,128)S(1)} %all-to-all-done.received_ref), channel_id=1, source_target_pairs={{0,8},{8,0},{16,24},{24,16},{1,9},{9,1},{17,25},{25,17},{2,10},{10... | collective-permute-start | bytes 651272 | tf_op jit(solution)/shard_map/ppermute | solution.py:1061
  24.7 13.8 %all-to-all-start.1 = ((f32[32,11,128]{2,1,0:T(8,128)}), f32[32,11,128]{2,1,0:T(8,128)S(1)}, u32[]{:S(2)}, u32[]{:S(2)}) async-start(f32[32,11,128]{2,1,0:T(8,128)} %bitcast.10), calls=%async_computation.1 | async-start | bytes 524288 | tf_op jit(solution)/shard_map/all_to_all | solution.py:1113
  38.5 1.5 %collective-permute-start.1 = (f32[32,11,128]{2,1,0:T(8,128)S(1)}, f32[32,11,128]{2,1,0:T(8,128)S(1)}, u32[]{:S(2)}, u32[]{:S(2)}) collective-permute-start(f32[32,11,128]{2,1,0:T(8,128)S(1)} %all-to-all-done.1.mine_ref), channel_id=1, source_target_pairs={{0,8},{8,0},{16,24},{24,16},{1,9},{9,1},{17,25},{25,17},{2,10},{10... | collective-permute-start | bytes 540680 | tf_op jit(solution)/shard_map/ppermute | solution.py:1163

commit v9 on v8

--- a/solution.py
+++ b/solution.py
@@ -19,6 +19,7 @@
 F32 = jnp.float32
 BF16 = jnp.bfloat16
 STEP = 10
+QUAD = 4
 SHRINK = 1.0 / LATENT
 I32 = jnp.int32
 
@@ -741,11 +742,12 @@
     spread = select(places_ref[...], change_ref[...], NT)
     load.wait()
     back = product(spread, unfold_ref[...], NN)
-    half = back_ref.shape[2]
+    quads = back_ref.shape[2]
     for h in range(2):
         for j in range(hosts):
-            first = j * padded + h * half
-            back_ref[h, j] = back[first : first + half]
+            for q in range(quads):
+                first = j * padded + (h * quads + q) * QUAD
+                back_ref[h, j, q] = back[first : first + QUAD]
     for i in range(back_far.shape[0]):
         copies.append(pltpu.make_async_copy(back_ref.at[i % 2], back_far.at[i], back_sems.at[i]))
         copies[-1].start()
@@ -928,13 +930,15 @@
 
 
 def gather_half(picks_ref, half_ref, table_ref, idle, part):
-    sources, half, _ = half_ref.shape
+    sources, quads, _, _ = half_ref.shape
     height = table_ref.shape[0]
     held = height // (sources - idle)
-    if half != held:
+    if quads * QUAD != held:
         table_ref[...] = jnp.zeros_like(table_ref)
     for j in range(sources - idle):
-        table_ref[j * held : j * held + half, :] = half_ref[idle + j]
+        for q in range(quads):
+            first = j * held + q * QUAD
+            table_ref[first : first + QUAD, :] = half_ref[idle + j, q]
     picks = picks_ref[:, part * height : (part + 1) * height]
     return select(picks, table_ref[...], NN)
 
@@ -982,9 +986,9 @@
     _, fields, _, columns, slots = cloud_state.shape
     elements = count // 4
     capacity = slots // col_count
-    padded = -(-capacity // 8) * 8
-    half = -(-capacity // 2)
+    half = -(-capacity // (2 * QUAD)) * QUAD
     held = -(-half // 8) * 8
+    padded = -(-max(capacity, 2 * half) // 8) * 8
     block = col_count * padded
     clouds = (sec_count - 1) * col_count
     segments, used, rows = segments_of(slots, cloud_levels)
@@ -1087,7 +1091,7 @@
             ("far", (rows, columns, LANES), F32),
             ("far", (MAX_SUB - 1, rows, columns, LANES), F32),
             ("far", (MAX_SUB + 3, rows, LANES), F32),
-            ("far", (sec_count, col_count, half, width), F32),
+            ("far", (sec_count, col_count, half // QUAD, QUAD, width), F32),
         ],
         scratch=[
             pltpu.VMEM((width, width), F32),
@@ -1101,7 +1105,7 @@
             pltpu.VMEM((rows, LANES), F32),
             pltpu.VMEM((rows * 8, LANES), F32),
             pltpu.VMEM((width, mapped), F32),
-            pltpu.VMEM((2, col_count, half, width), F32),
+            pltpu.VMEM((2, col_count, half // QUAD, QUAD, width), F32),
             dma(()),
             dma((MAX_SUB - 1,)),
             dma(()),
@@ -1111,7 +1115,7 @@
         limit=24,
     )
     returned = lax.all_to_all(
-        back.reshape(sec_count * col_count, half, width),
+        back.reshape(sec_count * col_count, half // QUAD, QUAD, width),
         ("sec", "col"),
         split_axis=0,
         concat_axis=0,

time: 41.4 us -> 39.1 us (0.944)
  waiting for transfers between devices: 10.6 us -> 7.91 us
    all_to_all x1, waiting for transfers between devices: 3.96 us -> 1.76 us  [body(): lax.all_to_all(back.reshape(sec_count * col_count, half // QUAD, QUAD, wi...]
    ppermute x1, waiting for transfers between devices: 1.2 us -> 0.73 us  [body(): partner = lax.ppermute(returned, 'sec', pairs)]
    ppermute x1, starting transfers between devices: 0.01 us -> 0.45 us  [body(): partner = lax.ppermute(returned, 'sec', pairs)]
  transfers between devices with their start and end apart: 4 -> 4, of which waited for: 4 -> 4; matrix products, arithmetic and copies ran while one was open for 0% -> 0% of each run, Pallas kernels for 27% -> 29%
where the time goes in v9:
time: 39.1 us; the launch traced here: 38.8 us
  Pallas kernels  19.1 us (49%)
  starting transfers between devices  11.1 us (28%)
  waiting for transfers between devices  7.91 us (20%)
  between operations  0.68 us (2%)
    pallas_call x7, Pallas kernels, call(): pl.pallas_call(kernel, out_shape=shapes, in_specs=[SPACES[space] for spac...  19.1 us
    all_to_all x1, starting transfers between devices, body(): lax.all_to_all(outgoing, 'col', split_axis=0, concat_axis=0, tiled=True)  7.31 us
    all_to_all x1, waiting for transfers between devices, body(): lax.all_to_all(outgoing, 'col', split_axis=0, concat_axis=0, tiled=True)  4.59 us
    all_to_all x1, starting transfers between devices, body(): lax.all_to_all(back.reshape(sec_count * col_count, half // QUAD, QUAD, wi...  3.39 us
    all_to_all x1, waiting for transfers between devices, body(): lax.all_to_all(back.reshape(sec_count * col_count, half // QUAD, QUAD, wi...  1.76 us
    ppermute x1, waiting for transfers between devices, body(): other = lax.ppermute(received, 'sec', pairs)  0.84 us
  transfers between devices with their start and end apart: 4, of which 4 were waited for; matrix products, arithmetic and copies ran while one was open for 0% of the time, Pallas kernels for 29%

profile of v9, /device:TPU:0, one launch (start us, length us, event | category | flops | bytes accessed | tf_op | source)
XLA Modules:
  0.0 38.8 jit_solution(12057808899247733176)
XLA Ops:
  0.6 2.4 %host.1 = (f32[8,53,128]{2,1,0:T(8,128)}, f32[128,128]{1,0:T(8,128)}) custom-call(f32[256,128]{1,0:T(8,128)} %columns_far.1, f32[1,128]{1,0:T(1,128)} %bitcast.13, s32[4,64]{1,0:T(4,128)} %bitcast.11, s32[1,256]{1,0:T(1,128)} %bitcast.16, s32[1,256]{1,0:T(1,128)} %bitcast.18, f32[58,64]{1,0:T(8,128)} %map_far.1), custom_call_target="tpu_custom_call" | custom-call | tf_op jit(solution)/shard_map/host/pallas_call | solution.py:968
  3.1 7.3 %all-to-all-start = ((f32[8,53,128]{2,1,0:T(8,128)}), f32[8,53,128]{2,1,0:T(8,128)S(1)}, u32[]{:S(2)}, u32[]{:S(2)}) async-start(f32[8,53,128]{2,1,0:T(8,128)} %get-tuple-element.26), calls=%async_computation | async-start | bytes 458752 | tf_op jit(solution)/shard_map/all_to_all | solution.py:1016
  10.4 3.8 %prepare.1 = (f32[82,32,128]{2,1,0:T(8,128)S(1)}, f32[2,88,128]{2,1,0:T(8,128)S(1)}, f32[88,128]{1,0:T(8,128)S(1)}, f32[82,32,128]{2,1,0:T(8,128)}, f32[256,128]...) custom-call(bf16[2,58,32,168]{3,2,1,0:T(8,128)(2,1)} %bitcast.8, ...), custom_call_target="tpu_custom_call" | custom-call | tf_op jit(solution)/shard_map/prepare/pallas_call | solution.py:968
  14.2 4.6 %all-to-all-done.received_ref = f32[8,53,128]{2,1,0:T(8,128)S(1)} async-done(((f32[8,53,128]{2,1,0:T(8,128)}), f32[8,53,128]{2,1,0:T(8,128)S(1)}, u32[]{:S(2)}, u32[]{:S(2)}) %all-to-all-start) | async-done | bytes 217120 | tf_op jit(solution)/shard_map/all_to_all | solution.py:1016
  18.8 0.0 collective-permute-start
  18.8 0.6 %arrive.1 = (f32[128,256]{1,0:T(8,128)S(1)}, bf16[192,256]{1,0:T(8,128)(2,1)S(1)}) custom-call(f32[8,53,128]{2,1,0:T(8,128)S(1)} %all-to-all-done.received_ref, f32[128,128]{1,0:T(8,128)S(1)} %get-tuple-element.30.fold_ref), custom_call_target="tpu_custom_call" | custom-call | tf_op jit(solution)/shard_map/arrive/pallas_call | solution.py:968
  19.5 0.8 %collective-permute-done.other_ref = f32[8,53,128]{2,1,0:T(8,128)S(1)} collective-permute-done((f32[8,53,128]{2,1,0:T(8,128)S(1)}, f32[8,53,128]{2,1,0:T(8,128)S(1)}, u32[]{:S(2)}, u32[]{:S(2)}) %collective-permute-start) | collective-permute-done | bytes 217120 | tf_op jit(solution)/shard_map/ppermute | solution.py:1065
  20.3 4.4 %water.1 = (f32[88,32,128]{2,1,0:T(8,128)}, f32[3,88,32,128]{3,2,1,0:T(8,128)}, f32[7,88,128]{2,1,0:T(8,128)}, f32[4,8,3,4,128]{4,3,2,1,0:T(4,128)}) custom-call(f32[128,256]{1,0:T(8,128)S(1)} %get-tuple-element.31.arrived_ref, bf16[192,256]{1,0:T(8,128)(2,1)S(1)} %get-tuple-element.32.places_ref, f32[8,53,128]{2,1,0:T(8,128)S(1)} %collective-permute-done.other_ref, ...), custom_call_target="tpu_custom_call" | custom-call | tf_op jit(solution)/shard_map/water/pallas_call | solution.py:968
  24.7 3.4 %all-to-all-start.1 = ((f32[32,3,4,128]{3,2,1,0:T(4,128)}), f32[32,3,4,128]{3,2,1,0:T(4,128)S(1)}, u32[]{:S(2)}, u32[]{:S(2)}) async-start(f32[32,3,4,128]{3,2,1,0:T(4,128)} %bitcast.10), calls=%async_computation.1 | async-start | bytes 393216 | tf_op jit(solution)/shard_map/all_to_all | solution.py:1117
  28.1 6.5 %energy.1 = (bf16[2,58,32,168]{3,2,1,0:T(8,128)(2,1)}, f32[256,128]{1,0:T(8,128)S(1)}, bf16[256,768]{1,0:T(8,128)(2,1)S(1)}) custom-call(bf16[2,58,32,168]{3,2,1,0:T(8,128)(2,1)} %bitcast.9, f32[82,32,128]{2,1,0:T(8,128)} %get-tuple-element.38.energy_far, f32[88,32,128]{2,1,0:T(8,128)} %get-tuple-element.39.water_far, ...), custom_call_target="tpu_custom_call" | custom-call | tf_op jit(solution)/shard_map/energy/pallas_call | solution.py:968
  34.6 1.8 %all-to-all-done.1.mine_ref = f32[32,3,4,128]{3,2,1,0:T(4,128)S(1)} async-done(((f32[32,3,4,128]{3,2,1,0:T(4,128)}), f32[32,3,4,128]{3,2,1,0:T(4,128)S(1)}, u32[]{:S(2)}, u32[]{:S(2)}) %all-to-all-start.1) | async-done | bytes 196640 | tf_op jit(solution)/shard_map/all_to_all | solution.py:1117
  36.3 0.4 %collective-permute-start.1 = (f32[32,3,4,128]{3,2,1,0:T(4,128)S(1)}, f32[32,3,4,128]{3,2,1,0:T(4,128)S(1)}, u32[]{:S(2)}, u32[]{:S(2)}) collective-permute-start(f32[32,3,4,128]{3,2,1,0:T(4,128)S(1)} %all-to-all-done.1.mine_ref), channel_id=1, source_target_pairs={{0,8},{8,0},{16,24},{24,16},{1,9},{9,1},{17,25},{25,17},{2,10},{10... | collective-permute-start | bytes 589832 | tf_op jit(solution)/shard_map/ppermute | solution.py:1167
  36.8 0.3 nearly.1.nearly_ref
  37.1 0.7 %collective-permute-done.1.other_ref = f32[32,3,4,128]{3,2,1,0:T(4,128)S(1)} collective-permute-done((f32[32,3,4,128]{3,2,1,0:T(4,128)S(1)}, f32[32,3,4,128]{3,2,1,0:T(4,128)S(1)}, u32[]{:S(2)}, u32[]{:S(2)}) %collective-permute-start.1) | collective-permute-done | bytes 196640 | tf_op jit(solution)/shard_map/ppermute | solution.py:1167
  37.8 1.0 %final.1 = f32[256,128]{1,0:T(8,128)} custom-call(f32[256,128]{1,0:T(8,128)S(1)} %nearly.1.nearly_ref, bf16[256,768]{1,0:T(8,128)(2,1)S(1)} %get-tuple-element.47.picks_ref, f32[32,3,4,128]{3,2,1,0:T(4,128)S(1)} %collective-permute-done.1.other_ref), custom_call_target="tpu_custom_call" | custom-call | tf_op jit(solution)/shard_map/final/pallas_call | solution.py:968
Async XLA Ops:
  3.1 15.7 %all-to-all-start = ((f32[8,53,128]{2,1,0:T(8,128)}), f32[8,53,128]{2,1,0:T(8,128)S(1)}, u32[]{:S(2)}, u32[]{:S(2)}) async-start(f32[8,53,128]{2,1,0:T(8,128)} %get-tuple-element.26), calls=%async_computation | async-start | bytes 458752 | tf_op jit(solution)/shard_map/all_to_all | solution.py:1016
  18.8 1.5 %collective-permute-start = (f32[8,53,128]{2,1,0:T(8,128)S(1)}, f32[8,53,128]{2,1,0:T(8,128)S(1)}, u32[]{:S(2)}, u32[]{:S(2)}) collective-permute-start(f32[8,53,128]{2,1,0:T(8,128)S(1)} %all-to-all-done.received_ref), channel_id=1, source_target_pairs={{0,8},{8,0},{16,24},{24,16},{1,9},{9,1},{17,25},{25,17},{2,10},{10... | collective-permute-start | bytes 651272 | tf_op jit(solution)/shard_map/ppermute | solution.py:1065
  24.7 11.6 %all-to-all-start.1 = ((f32[32,3,4,128]{3,2,1,0:T(4,128)}), f32[32,3,4,128]{3,2,1,0:T(4,128)S(1)}, u32[]{:S(2)}, u32[]{:S(2)}) async-start(f32[32,3,4,128]{3,2,1,0:T(4,128)} %bitcast.10), calls=%async_computation.1 | async-start | bytes 393216 | tf_op jit(solution)/shard_map/all_to_all | solution.py:1117
  36.3 1.5 %collective-permute-start.1 = (f32[32,3,4,128]{3,2,1,0:T(4,128)S(1)}, f32[32,3,4,128]{3,2,1,0:T(4,128)S(1)}, u32[]{:S(2)}, u32[]{:S(2)}) collective-permute-start(f32[32,3,4,128]{3,2,1,0:T(4,128)S(1)} %all-to-all-done.1.mine_ref), channel_id=1, source_target_pairs={{0,8},{8,0},{16,24},{24,16},{1,9},{9,1},{17,25},{25,17},{2,10},{10... | collective-permute-start | bytes 589832 | tf_op jit(solution)/shard_map/ppermute | solution.py:1167

commit v10 on v9

--- a/solution.py
+++ b/solution.py
@@ -43,12 +43,12 @@
     return jnp.floor((value.astype(F32) + 0.5) * (1.0 / by)).astype(I32)
 
 
-def split(values):
-    high = values.astype(BF16)
-    rest = values - high.astype(F32)
-    middle = rest.astype(BF16)
-    low = (rest - middle.astype(F32)).astype(BF16)
-    return low, middle, high
+def split(values, count=3):
+    parts, rest = [], values
+    for _ in range(count - 1):
+        parts.append(rest.astype(BF16))
+        rest = rest - parts[-1].astype(F32)
+    return [rest.astype(BF16)] + parts[::-1]
 
 
 def select(picks, values, contract, swap=False):
@@ -61,9 +61,9 @@
 
 
 def product(a, b, contract):
-    (al, am, ah), (bl, bm, bh) = split(a), split(b)
+    (am, ah), (bm, bh) = split(a, 2), split(b, 2)
     total = None
-    for x, y in ((al, bh), (ah, bl), (am, bm), (am, bh), (ah, bm), (ah, bh)):
+    for x, y in ((am, bh), (ah, bm), (ah, bh)):
         term = lax.dot_general(x, y, (contract, ((), ())), preferred_element_type=F32)
         total = term if total is None else total + term
     return total
@@ -208,8 +208,9 @@
     rank = slot - place * padded
     upper = jnp.where(rank >= half, 1, 0)
     parity = lax.axis_index("sec") % 2
-    cloud = owner * col_count + place + jnp.where(upper == parity, 0, clouds)
-    everywhere = (cloud * held + rank - half * upper).astype(F32)
+    cloud = owner * col_count + place
+    row = jnp.where(upper == parity, cloud * held + rank - half * upper, -1)
+    everywhere = row.astype(F32)
     identity = jnp.where(iota((rows, rows), 0) == iota((rows, rows), 1), 1.0, 0.0)
     homes_ref[...] = select(
         identity.astype(BF16), jnp.broadcast_to(everywhere, (LANES, rows)), NT
@@ -929,26 +930,20 @@
             leave(f, part).wait()
 
 
-def gather_half(picks_ref, half_ref, table_ref, idle, part):
-    sources, quads, _, _ = half_ref.shape
-    height = table_ref.shape[0]
-    held = height // (sources - idle)
+def nearly_kernel(picks_ref, mine_ref, out_ref, table_ref, *, idle):
+    sources, quads, _, _ = mine_ref.shape
+    held = table_ref.shape[0] // (sources - idle)
     if quads * QUAD != held:
         table_ref[...] = jnp.zeros_like(table_ref)
     for j in range(sources - idle):
         for q in range(quads):
             first = j * held + q * QUAD
-            table_ref[first : first + QUAD, :] = half_ref[idle + j, q]
-    picks = picks_ref[:, part * height : (part + 1) * height]
-    return select(picks, table_ref[...], NN)
-
-
-def nearly_kernel(advanced_ref, picks_ref, mine_ref, out_ref, table_ref, *, idle):
-    out_ref[...] = advanced_ref[...] + gather_half(picks_ref, mine_ref, table_ref, idle, 0)
-
-
-def final_kernel(nearly_ref, picks_ref, other_ref, out_ref, table_ref, *, levels, idle):
-    summed = nearly_ref[...] + gather_half(picks_ref, other_ref, table_ref, idle, 1)
+            table_ref[first : first + QUAD, :] = mine_ref[idle + j, q]
+    out_ref[...] = select(picks_ref[...], table_ref[...], NN)
+
+
+def final_kernel(advanced_ref, mine_ref, other_ref, out_ref, *, levels):
+    summed = advanced_ref[...] + (mine_ref[...] + other_ref[...])
     water = divided(iota(summed.shape, 1), levels) == 1
     out_ref[...] = jnp.where(water, jnp.maximum(summed, 0.0), summed)
 
@@ -1140,7 +1135,7 @@
         [
             ("far", state.shape, BF16),
             ("near", (count, width), F32),
-            ("near", (count, 2 * clouds * held), BF16),
+            ("near", (count, clouds * held), BF16),
         ],
         scratch=[
             pltpu.VMEM(state.shape, BF16),
@@ -1164,21 +1159,19 @@
         limit=32,
     )
     returned, advanced = lax.optimization_barrier((returned, advanced))
-    partner = lax.ppermute(returned, "sec", pairs)
-    table = pltpu.VMEM((clouds * held, width), F32)
-    (nearly,) = call(
+    (mine,) = call(
         functools.partial(nearly_kernel, idle=col_count),
         "nearly",
-        [("near", advanced), ("near", picks), ("near", returned)],
+        [("near", picks), ("near", returned)],
         [("near", (count, width), F32)],
-        scratch=[table],
-    )
+        scratch=[pltpu.VMEM((clouds * held, width), F32)],
+    )
+    partner = lax.ppermute(mine, "sec", pairs)
     (new_columns,) = call(
-        functools.partial(final_kernel, levels=levels, idle=col_count),
+        functools.partial(final_kernel, levels=levels),
         "final",
-        [("near", nearly), ("near", picks), ("near", partner)],
+        [("near", advanced), ("near", mine), ("near", partner)],
         [("auto", (count, width), F32)],
-        scratch=[table],
     )
     return new_columns, new_block[None]
 

time: 39.1 us -> 38.9 us (level)
  Pallas kernels: 19.1 us -> 18.4 us
    pallas_call x7, Pallas kernels: 19.1 us -> 18.4 us  [call(): pl.pallas_call(kernel, out_shape=shapes, in_specs=[SPACES[space] for spac...]
  transfers between devices with their start and end apart: 4 -> 4, of which waited for: 4 -> 4; matrix products, arithmetic and copies ran while one was open for 0% -> 0% of each run, Pallas kernels for 29% -> 28%
where the time goes in v10:
time: 38.9 us; the launch traced here: 38.5 us
  Pallas kernels  18.4 us (47%)
  starting transfers between devices  11.2 us (29%)
  waiting for transfers between devices  8.23 us (21%)
  between operations  0.68 us (2%)
    pallas_call x7, Pallas kernels, call(): pl.pallas_call(kernel, out_shape=shapes, in_specs=[SPACES[space] for spac...  18.4 us
    all_to_all x1, starting transfers between devices, body(): lax.all_to_all(outgoing, 'col', split_axis=0, concat_axis=0, tiled=True)  7.31 us
    all_to_all x1, waiting for transfers between devices, body(): lax.all_to_all(outgoing, 'col', split_axis=0, concat_axis=0, tiled=True)  4.59 us
    all_to_all x1, starting transfers between devices, body(): lax.all_to_all(back.reshape(sec_count * col_count, half // QUAD, QUAD, wi...  3.39 us
    all_to_all x1, waiting for transfers between devices, body(): lax.all_to_all(back.reshape(sec_count * col_count, half // QUAD, QUAD, wi...  1.76 us
    ppermute x1, waiting for transfers between devices, body(): partner = lax.ppermute(mine, 'sec', pairs)  0.99 us
    ppermute x1, waiting for transfers between devices, body(): other = lax.ppermute(received, 'sec', pairs)  0.9 us
  transfers between devices with their start and end apart: 4, of which 4 were waited for; matrix products, arithmetic and copies ran while one was open for 0% of the time, Pallas kernels for 28%

profile of v10, /device:TPU:0, one launch (start us, length us, event | category | flops | bytes accessed | tf_op | source)
XLA Modules:
  0.0 38.5 jit_solution(17187120936444098638)
XLA Ops:
  0.6 2.3 %host.1 = (f32[8,53,128]{2,1,0:T(8,128)}, f32[128,128]{1,0:T(8,128)}) custom-call(f32[256,128]{1,0:T(8,128)} %columns_far.1, f32[1,128]{1,0:T(1,128)} %bitcast.13, s32[4,64]{1,0:T(4,128)} %bitcast.11, s32[1,256]{1,0:T(1,128)} %bitcast.16, s32[1,256]{1,0:T(1,128)} %bitcast.18, f32[58,64]{1,0:T(8,128)} %map_far.1), custom_call_target="tpu_custom_call" | custom-call | tf_op jit(solution)/shard_map/host/pallas_call | solution.py:963
  2.9 7.3 %all-to-all-start = ((f32[8,53,128]{2,1,0:T(8,128)}), f32[8,53,128]{2,1,0:T(8,128)S(1)}, u32[]{:S(2)}, u32[]{:S(2)}) async-start(f32[8,53,128]{2,1,0:T(8,128)} %get-tuple-element.26), calls=%async_computation | async-start | bytes 458752 | tf_op jit(solution)/shard_map/all_to_all | solution.py:1011
  10.2 3.8 %prepare.1 = (f32[82,32,128]{2,1,0:T(8,128)S(1)}, f32[2,88,128]{2,1,0:T(8,128)S(1)}, f32[88,128]{1,0:T(8,128)S(1)}, f32[82,32,128]{2,1,0:T(8,128)}, f32[256,128]...) custom-call(bf16[2,58,32,168]{3,2,1,0:T(8,128)(2,1)} %bitcast.8, ...), custom_call_target="tpu_custom_call" | custom-call | tf_op jit(solution)/shard_map/prepare/pallas_call | solution.py:963
  14.1 4.6 %all-to-all-done.received_ref = f32[8,53,128]{2,1,0:T(8,128)S(1)} async-done(((f32[8,53,128]{2,1,0:T(8,128)}), f32[8,53,128]{2,1,0:T(8,128)S(1)}, u32[]{:S(2)}, u32[]{:S(2)}) %all-to-all-start) | async-done | bytes 217120 | tf_op jit(solution)/shard_map/all_to_all | solution.py:1011
  18.7 0.0 collective-permute-start
  18.7 0.6 %arrive.1 = (f32[128,256]{1,0:T(8,128)S(1)}, bf16[192,256]{1,0:T(8,128)(2,1)S(1)}) custom-call(f32[8,53,128]{2,1,0:T(8,128)S(1)} %all-to-all-done.received_ref, f32[128,128]{1,0:T(8,128)S(1)} %get-tuple-element.30.fold_ref), custom_call_target="tpu_custom_call" | custom-call | tf_op jit(solution)/shard_map/arrive/pallas_call | solution.py:963
  19.3 0.9 %collective-permute-done.other_ref = f32[8,53,128]{2,1,0:T(8,128)S(1)} collective-permute-done((f32[8,53,128]{2,1,0:T(8,128)S(1)}, f32[8,53,128]{2,1,0:T(8,128)S(1)}, u32[]{:S(2)}, u32[]{:S(2)}) %collective-permute-start) | collective-permute-done | bytes 217120 | tf_op jit(solution)/shard_map/ppermute | solution.py:1060
  20.2 4.2 %water.1 = (f32[88,32,128]{2,1,0:T(8,128)}, f32[3,88,32,128]{3,2,1,0:T(8,128)}, f32[7,88,128]{2,1,0:T(8,128)}, f32[4,8,3,4,128]{4,3,2,1,0:T(4,128)}) custom-call(f32[128,256]{1,0:T(8,128)S(1)} %get-tuple-element.31.arrived_ref, bf16[192,256]{1,0:T(8,128)(2,1)S(1)} %get-tuple-element.32.places_ref, f32[8,53,128]{2,1,0:T(8,128)S(1)} %collective-permute-done.other_ref, ...), custom_call_target="tpu_custom_call" | custom-call | tf_op jit(solution)/shard_map/water/pallas_call | solution.py:963
  24.4 3.4 %all-to-all-start.1 = ((f32[32,3,4,128]{3,2,1,0:T(4,128)}), f32[32,3,4,128]{3,2,1,0:T(4,128)S(1)}, u32[]{:S(2)}, u32[]{:S(2)}) async-start(f32[32,3,4,128]{3,2,1,0:T(4,128)} %bitcast.10), calls=%async_computation.1 | async-start | bytes 393216 | tf_op jit(solution)/shard_map/all_to_all | solution.py:1112
  27.8 6.5 %energy.1 = (bf16[2,58,32,168]{3,2,1,0:T(8,128)(2,1)}, f32[256,128]{1,0:T(8,128)S(1)}, bf16[256,384]{1,0:T(8,128)(2,1)S(1)}) custom-call(bf16[2,58,32,168]{3,2,1,0:T(8,128)(2,1)} %bitcast.9, f32[82,32,128]{2,1,0:T(8,128)} %get-tuple-element.38.energy_far, f32[88,32,128]{2,1,0:T(8,128)} %get-tuple-element.39.water_far, ...), custom_call_target="tpu_custom_call" | custom-call | tf_op jit(solution)/shard_map/energy/pallas_call | solution.py:963
  34.3 1.8 %all-to-all-done.1.mine_ref = f32[32,3,4,128]{3,2,1,0:T(4,128)S(1)} async-done(((f32[32,3,4,128]{3,2,1,0:T(4,128)}), f32[32,3,4,128]{3,2,1,0:T(4,128)S(1)}, u32[]{:S(2)}, u32[]{:S(2)}) %all-to-all-start.1) | async-done | bytes 196640 | tf_op jit(solution)/shard_map/all_to_all | solution.py:1112
  36.0 0.3 nearly.1.mine_ref
  36.4 0.5 %collective-permute-start.1 = (f32[256,128]{1,0:T(8,128)S(1)}, f32[256,128]{1,0:T(8,128)S(1)}, u32[]{:S(2)}, u32[]{:S(2)}) collective-permute-start(f32[256,128]{1,0:T(8,128)S(1)} %nearly.1.mine_ref), channel_id=1, source_target_pairs={{0,8},{8,0},{16,24},{24,16},{1,9},{9,1},{17,25},{25,17},{2,10},{10... | collective-permute-start | bytes 393224 | tf_op jit(solution)/shard_map/ppermute | solution.py:1169
  36.9 1.0 %collective-permute-done.1.other_ref = f32[256,128]{1,0:T(8,128)S(1)} collective-permute-done((f32[256,128]{1,0:T(8,128)S(1)}, f32[256,128]{1,0:T(8,128)S(1)}, u32[]{:S(2)}, u32[]{:S(2)}) %collective-permute-start.1) | collective-permute-done | bytes 131104 | tf_op jit(solution)/shard_map/ppermute | solution.py:1169
  37.9 0.7 %final.1 = f32[256,128]{1,0:T(8,128)} custom-call(f32[256,128]{1,0:T(8,128)S(1)} %get-tuple-element.46.advanced_ref, f32[256,128]{1,0:T(8,128)S(1)} %nearly.1.mine_ref, f32[256,128]{1,0:T(8,128)S(1)} %collective-permute-done.1.other_ref), custom_call_target="tpu_custom_call" | custom-call | tf_op jit(solution)/shard_map/final/pallas_call | solution.py:963
Async XLA Ops:
  2.9 15.7 %all-to-all-start = ((f32[8,53,128]{2,1,0:T(8,128)}), f32[8,53,128]{2,1,0:T(8,128)S(1)}, u32[]{:S(2)}, u32[]{:S(2)}) async-start(f32[8,53,128]{2,1,0:T(8,128)} %get-tuple-element.26), calls=%async_computation | async-start | bytes 458752 | tf_op jit(solution)/shard_map/all_to_all | solution.py:1011
  18.7 1.5 %collective-permute-start = (f32[8,53,128]{2,1,0:T(8,128)S(1)}, f32[8,53,128]{2,1,0:T(8,128)S(1)}, u32[]{:S(2)}, u32[]{:S(2)}) collective-permute-start(f32[8,53,128]{2,1,0:T(8,128)S(1)} %all-to-all-done.received_ref), channel_id=1, source_target_pairs={{0,8},{8,0},{16,24},{24,16},{1,9},{9,1},{17,25},{25,17},{2,10},{10... | collective-permute-start | bytes 651272 | tf_op jit(solution)/shard_map/ppermute | solution.py:1060
  24.4 11.6 %all-to-all-start.1 = ((f32[32,3,4,128]{3,2,1,0:T(4,128)}), f32[32,3,4,128]{3,2,1,0:T(4,128)S(1)}, u32[]{:S(2)}, u32[]{:S(2)}) async-start(f32[32,3,4,128]{3,2,1,0:T(4,128)} %bitcast.10), calls=%async_computation.1 | async-start | bytes 393216 | tf_op jit(solution)/shard_map/all_to_all | solution.py:1112
  36.4 1.5 %collective-permute-start.1 = (f32[256,128]{1,0:T(8,128)S(1)}, f32[256,128]{1,0:T(8,128)S(1)}, u32[]{:S(2)}, u32[]{:S(2)}) collective-permute-start(f32[256,128]{1,0:T(8,128)S(1)} %nearly.1.mine_ref), channel_id=1, source_target_pairs={{0,8},{8,0},{16,24},{24,16},{1,9},{9,1},{17,25},{25,17},{2,10},{10... | collective-permute-start | bytes 393224 | tf_op jit(solution)/shard_map/ppermute | solution.py:1169

commit v11 on v10

--- a/solution.py
+++ b/solution.py
@@ -18,7 +18,7 @@
 LANES = 128
 F32 = jnp.float32
 BF16 = jnp.bfloat16
-STEP = 10
+STEP = 20
 QUAD = 4
 SHRINK = 1.0 / LATENT
 I32 = jnp.int32

time: 38.9 us -> 38.7 us (level)
  Pallas kernels: 18.4 us -> 17.6 us
  waiting for transfers between devices: 8.23 us -> 8.89 us
    pallas_call x7, Pallas kernels: 18.4 us -> 17.6 us  [call(): pl.pallas_call(kernel, out_shape=shapes, in_specs=[SPACES[space] for spac...]
    all_to_all x1, waiting for transfers between devices: 1.76 us -> 2.22 us  [body(): lax.all_to_all(back.reshape(sec_count * col_count, half // QUAD, QUAD, wi...]
  transfers between devices with their start and end apart: 4 -> 4, of which waited for: 4 -> 4; matrix products, arithmetic and copies ran while one was open for 0% -> 0% of each run, Pallas kernels for 28% -> 27%
where the time goes in v11:
time: 38.7 us; the launch traced here: 38.4 us
  Pallas kernels  17.6 us (45%)
  starting transfers between devices  11.2 us (29%)
  waiting for transfers between devices  8.89 us (23%)
  between operations  0.68 us (2%)
    pallas_call x7, Pallas kernels, call(): pl.pallas_call(kernel, out_shape=shapes, in_specs=[SPACES[space] for spac...  17.6 us
    all_to_all x1, starting transfers between devices, body(): lax.all_to_all(outgoing, 'col', split_axis=0, concat_axis=0, tiled=True)  7.31 us
    all_to_all x1, waiting for transfers between devices, body(): lax.all_to_all(outgoing, 'col', split_axis=0, concat_axis=0, tiled=True)  4.79 us
    all_to_all x1, starting transfers between devices, body(): lax.all_to_all(back.reshape(sec_count * col_count, half // QUAD, QUAD, wi...  3.39 us
    all_to_all x1, waiting for transfers between devices, body(): lax.all_to_all(back.reshape(sec_count * col_count, half // QUAD, QUAD, wi...  2.22 us
    ppermute x1, waiting for transfers between devices, body(): partner = lax.ppermute(mine, 'sec', pairs)  0.99 us
    ppermute x1, waiting for transfers between devices, body(): other = lax.ppermute(received, 'sec', pairs)  0.9 us
  transfers between devices with their start and end apart: 4, of which 4 were waited for; matrix products, arithmetic and copies ran while one was open for 0% of the time, Pallas kernels for 27%

profile of v11, /device:TPU:0, one launch (start us, length us, event | category | flops | bytes accessed | tf_op | source)
XLA Modules:
  0.0 38.4 jit_solution(4269215427289892197)
XLA Ops:
  0.6 2.3 %host.1 = (f32[8,53,128]{2,1,0:T(8,128)}, f32[128,128]{1,0:T(8,128)}) custom-call(f32[256,128]{1,0:T(8,128)} %columns_far.1, f32[1,128]{1,0:T(1,128)} %bitcast.13, s32[4,64]{1,0:T(4,128)} %bitcast.11, s32[1,256]{1,0:T(1,128)} %bitcast.16, s32[1,256]{1,0:T(1,128)} %bitcast.18, f32[58,64]{1,0:T(8,128)} %map_far.1), custom_call_target="tpu_custom_call" | custom-call | tf_op jit(solution)/shard_map/host/pallas_call | solution.py:963
  2.9 7.3 %all-to-all-start = ((f32[8,53,128]{2,1,0:T(8,128)}), f32[8,53,128]{2,1,0:T(8,128)S(1)}, u32[]{:S(2)}, u32[]{:S(2)}) async-start(f32[8,53,128]{2,1,0:T(8,128)} %get-tuple-element.26), calls=%async_computation | async-start | bytes 458752 | tf_op jit(solution)/shard_map/all_to_all | solution.py:1011
  10.2 3.6 %prepare.1 = (f32[82,32,128]{2,1,0:T(8,128)S(1)}, f32[2,88,128]{2,1,0:T(8,128)S(1)}, f32[88,128]{1,0:T(8,128)S(1)}, f32[82,32,128]{2,1,0:T(8,128)}, f32[256,128]...) custom-call(bf16[2,58,32,168]{3,2,1,0:T(8,128)(2,1)} %bitcast.8, ...), custom_call_target="tpu_custom_call" | custom-call | tf_op jit(solution)/shard_map/prepare/pallas_call | solution.py:963
  13.9 4.8 %all-to-all-done.received_ref = f32[8,53,128]{2,1,0:T(8,128)S(1)} async-done(((f32[8,53,128]{2,1,0:T(8,128)}), f32[8,53,128]{2,1,0:T(8,128)S(1)}, u32[]{:S(2)}, u32[]{:S(2)}) %all-to-all-start) | async-done | bytes 217120 | tf_op jit(solution)/shard_map/all_to_all | solution.py:1011
  18.7 0.0 collective-permute-start
  18.7 0.6 %arrive.1 = (f32[128,256]{1,0:T(8,128)S(1)}, bf16[192,256]{1,0:T(8,128)(2,1)S(1)}) custom-call(f32[8,53,128]{2,1,0:T(8,128)S(1)} %all-to-all-done.received_ref, f32[128,128]{1,0:T(8,128)S(1)} %get-tuple-element.30.fold_ref), custom_call_target="tpu_custom_call" | custom-call | tf_op jit(solution)/shard_map/arrive/pallas_call | solution.py:963
  19.3 0.9 %collective-permute-done.other_ref = f32[8,53,128]{2,1,0:T(8,128)S(1)} collective-permute-done((f32[8,53,128]{2,1,0:T(8,128)S(1)}, f32[8,53,128]{2,1,0:T(8,128)S(1)}, u32[]{:S(2)}, u32[]{:S(2)}) %collective-permute-start) | collective-permute-done | bytes 217120 | tf_op jit(solution)/shard_map/ppermute | solution.py:1060
  20.2 4.1 %water.1 = (f32[88,32,128]{2,1,0:T(8,128)}, f32[3,88,32,128]{3,2,1,0:T(8,128)}, f32[7,88,128]{2,1,0:T(8,128)}, f32[4,8,3,4,128]{4,3,2,1,0:T(4,128)}) custom-call(f32[128,256]{1,0:T(8,128)S(1)} %get-tuple-element.31.arrived_ref, bf16[192,256]{1,0:T(8,128)(2,1)S(1)} %get-tuple-element.32.places_ref, f32[8,53,128]{2,1,0:T(8,128)S(1)} %collective-permute-done.other_ref, ...), custom_call_target="tpu_custom_call" | custom-call | tf_op jit(solution)/shard_map/water/pallas_call | solution.py:963
  24.3 3.4 %all-to-all-start.1 = ((f32[32,3,4,128]{3,2,1,0:T(4,128)}), f32[32,3,4,128]{3,2,1,0:T(4,128)S(1)}, u32[]{:S(2)}, u32[]{:S(2)}) async-start(f32[32,3,4,128]{3,2,1,0:T(4,128)} %bitcast.10), calls=%async_computation.1 | async-start | bytes 393216 | tf_op jit(solution)/shard_map/all_to_all | solution.py:1112
  27.6 6.0 %energy.1 = (bf16[2,58,32,168]{3,2,1,0:T(8,128)(2,1)}, f32[256,128]{1,0:T(8,128)S(1)}, bf16[256,384]{1,0:T(8,128)(2,1)S(1)}) custom-call(bf16[2,58,32,168]{3,2,1,0:T(8,128)(2,1)} %bitcast.9, f32[82,32,128]{2,1,0:T(8,128)} %get-tuple-element.38.energy_far, f32[88,32,128]{2,1,0:T(8,128)} %get-tuple-element.39.water_far, ...), custom_call_target="tpu_custom_call" | custom-call | tf_op jit(solution)/shard_map/energy/pallas_call | solution.py:963
  33.7 2.2 %all-to-all-done.1.mine_ref = f32[32,3,4,128]{3,2,1,0:T(4,128)S(1)} async-done(((f32[32,3,4,128]{3,2,1,0:T(4,128)}), f32[32,3,4,128]{3,2,1,0:T(4,128)S(1)}, u32[]{:S(2)}, u32[]{:S(2)}) %all-to-all-start.1) | async-done | bytes 196640 | tf_op jit(solution)/shard_map/all_to_all | solution.py:1112
  35.9 0.3 nearly.1.mine_ref
  36.2 0.5 %collective-permute-start.1 = (f32[256,128]{1,0:T(8,128)S(1)}, f32[256,128]{1,0:T(8,128)S(1)}, u32[]{:S(2)}, u32[]{:S(2)}) collective-permute-start(f32[256,128]{1,0:T(8,128)S(1)} %nearly.1.mine_ref), channel_id=1, source_target_pairs={{0,8},{8,0},{16,24},{24,16},{1,9},{9,1},{17,25},{25,17},{2,10},{10... | collective-permute-start | bytes 393224 | tf_op jit(solution)/shard_map/ppermute | solution.py:1169
  36.7 1.0 %collective-permute-done.1.other_ref = f32[256,128]{1,0:T(8,128)S(1)} collective-permute-done((f32[256,128]{1,0:T(8,128)S(1)}, f32[256,128]{1,0:T(8,128)S(1)}, u32[]{:S(2)}, u32[]{:S(2)}) %collective-permute-start.1) | collective-permute-done | bytes 131104 | tf_op jit(solution)/shard_map/ppermute | solution.py:1169
  37.7 0.7 %final.1 = f32[256,128]{1,0:T(8,128)} custom-call(f32[256,128]{1,0:T(8,128)S(1)} %get-tuple-element.46.advanced_ref, f32[256,128]{1,0:T(8,128)S(1)} %nearly.1.mine_ref, f32[256,128]{1,0:T(8,128)S(1)} %collective-permute-done.1.other_ref), custom_call_target="tpu_custom_call" | custom-call | tf_op jit(solution)/shard_map/final/pallas_call | solution.py:963
Async XLA Ops:
  2.9 15.7 %all-to-all-start = ((f32[8,53,128]{2,1,0:T(8,128)}), f32[8,53,128]{2,1,0:T(8,128)S(1)}, u32[]{:S(2)}, u32[]{:S(2)}) async-start(f32[8,53,128]{2,1,0:T(8,128)} %get-tuple-element.26), calls=%async_computation | async-start | bytes 458752 | tf_op jit(solution)/shard_map/all_to_all | solution.py:1011
  18.7 1.5 %collective-permute-start = (f32[8,53,128]{2,1,0:T(8,128)S(1)}, f32[8,53,128]{2,1,0:T(8,128)S(1)}, u32[]{:S(2)}, u32[]{:S(2)}) collective-permute-start(f32[8,53,128]{2,1,0:T(8,128)S(1)} %all-to-all-done.received_ref), channel_id=1, source_target_pairs={{0,8},{8,0},{16,24},{24,16},{1,9},{9,1},{17,25},{25,17},{2,10},{10... | collective-permute-start | bytes 651272 | tf_op jit(solution)/shard_map/ppermute | solution.py:1060
  24.3 11.6 %all-to-all-start.1 = ((f32[32,3,4,128]{3,2,1,0:T(4,128)}), f32[32,3,4,128]{3,2,1,0:T(4,128)S(1)}, u32[]{:S(2)}, u32[]{:S(2)}) async-start(f32[32,3,4,128]{3,2,1,0:T(4,128)} %bitcast.10), calls=%async_computation.1 | async-start | bytes 393216 | tf_op jit(solution)/shard_map/all_to_all | solution.py:1112
  36.2 1.5 %collective-permute-start.1 = (f32[256,128]{1,0:T(8,128)S(1)}, f32[256,128]{1,0:T(8,128)S(1)}, u32[]{:S(2)}, u32[]{:S(2)}) collective-permute-start(f32[256,128]{1,0:T(8,128)S(1)} %nearly.1.mine_ref), channel_id=1, source_target_pairs={{0,8},{8,0},{16,24},{24,16},{1,9},{9,1},{17,25},{25,17},{2,10},{10... | collective-permute-start | bytes 393224 | tf_op jit(solution)/shard_map/ppermute | solution.py:1169

commit v12 on v11

--- a/solution.py
+++ b/solution.py
@@ -51,9 +51,9 @@
     return [rest.astype(BF16)] + parts[::-1]
 
 
-def select(picks, values, contract, swap=False):
+def select(picks, values, contract, swap=False, count=3):
     total = None
-    for part in split(values):
+    for part in split(values, count):
         a, b = (part, picks) if swap else (picks, part)
         term = lax.dot_general(a, b, (contract, ((), ())), preferred_element_type=F32)
         total = term if total is None else total + term
@@ -154,7 +154,7 @@
     pack = jnp.where(iota((block, rows), 0) == mine, 1.0, 0.0).astype(BF16)
     base = own_part(columns_ref[...], means, mixing_ref[...], levels)
     count = neighbours_ref.shape[0]
-    ids = select(element_of_row(rows), neighbours_ref[...].astype(F32), NT, swap=True)
+    ids = select(element_of_row(rows), neighbours_ref[...].astype(F32), NT, swap=True, count=2)
     extras = jnp.concatenate(
         [
             jnp.zeros((cloud_levels, rows), F32),
@@ -165,7 +165,7 @@
         ],
         axis=0,
     )
-    sent = product(select(pack, base, NN), fold_ref[...], NT) + select(pack, extras, NT)
+    sent = product(select(pack, base, NN, count=2), fold_ref[...], NT) + select(pack, extras, NT, count=2)
     capacity = out_ref.shape[1] - share
     for c in range(col_count):
         out_ref[c, share:, :] = sent[c * padded : c * padded + capacity]
@@ -556,7 +556,7 @@
         for k in range(1, neighbours):
             wanted = wanted + jnp.where(element == ids[k], 1.0, 0.0)
         part = folded[:, first : first + chunk]
-        term = select(wanted.astype(BF16), part, NN, swap=True)
+        term = select(wanted.astype(BF16), part, NN, swap=True, count=2)
         total = term if total is None else total + term
     return total
 
@@ -740,7 +740,7 @@
                 first, number = f * stride + g * s.steps, s.group_steps(g)
                 part = turn(change[s.rows[0] : s.rows[0] + number], -g * s.width)
                 change_ref[first : first + number, t * LANES : (t + 1) * LANES] = part
-    spread = select(places_ref[...], change_ref[...], NT)
+    spread = select(places_ref[...], change_ref[...], NT, count=2)
     load.wait()
     back = product(spread, unfold_ref[...], NN)
     quads = back_ref.shape[2]

time: 38.7 us -> 38.6 us (level)
  no operation moved by 1% of the time
where the time goes in v12:
time: 38.6 us; the launch traced here: 38.3 us
  Pallas kernels  17.5 us (45%)
  starting transfers between devices  11.2 us (29%)
  waiting for transfers between devices  8.92 us (23%)
  between operations  0.68 us (2%)
    pallas_call x7, Pallas kernels, call(): pl.pallas_call(kernel, out_shape=shapes, in_specs=[SPACES[space] for spac...  17.5 us
    all_to_all x1, starting transfers between devices, body(): lax.all_to_all(outgoing, 'col', split_axis=0, concat_axis=0, tiled=True)  7.31 us
    all_to_all x1, waiting for transfers between devices, body(): lax.all_to_all(outgoing, 'col', split_axis=0, concat_axis=0, tiled=True)  4.79 us
    all_to_all x1, starting transfers between devices, body(): lax.all_to_all(back.reshape(sec_count * col_count, half // QUAD, QUAD, wi...  3.39 us
    all_to_all x1, waiting for transfers between devices, body(): lax.all_to_all(back.reshape(sec_count * col_count, half // QUAD, QUAD, wi...  2.22 us
    ppermute x1, waiting for transfers between devices, body(): partner = lax.ppermute(mine, 'sec', pairs)  0.99 us
    ppermute x1, waiting for transfers between devices, body(): other = lax.ppermute(received, 'sec', pairs)  0.93 us
  transfers between devices with their start and end apart: 4, of which 4 were waited for; matrix products, arithmetic and copies ran while one was open for 0% of the time, Pallas kernels for 27%

profile of v12, /device:TPU:0, one launch (start us, length us, event | category | flops | bytes accessed | tf_op | source)
XLA Modules:
  0.0 38.3 jit_solution(9169163695630137499)
XLA Ops:
  0.6 2.3 %host.1 = (f32[8,53,128]{2,1,0:T(8,128)}, f32[128,128]{1,0:T(8,128)}) custom-call(f32[256,128]{1,0:T(8,128)} %columns_far.1, f32[1,128]{1,0:T(1,128)} %bitcast.13, s32[4,64]{1,0:T(4,128)} %bitcast.11, s32[1,256]{1,0:T(1,128)} %bitcast.16, s32[1,256]{1,0:T(1,128)} %bitcast.18, f32[58,64]{1,0:T(8,128)} %map_far.1), custom_call_target="tpu_custom_call" | custom-call | tf_op jit(solution)/shard_map/host/pallas_call | solution.py:963
  2.9 7.3 %all-to-all-start = ((f32[8,53,128]{2,1,0:T(8,128)}), f32[8,53,128]{2,1,0:T(8,128)S(1)}, u32[]{:S(2)}, u32[]{:S(2)}) async-start(f32[8,53,128]{2,1,0:T(8,128)} %get-tuple-element.26), calls=%async_computation | async-start | bytes 458752 | tf_op jit(solution)/shard_map/all_to_all | solution.py:1011
  10.2 3.6 %prepare.1 = (f32[82,32,128]{2,1,0:T(8,128)S(1)}, f32[2,88,128]{2,1,0:T(8,128)S(1)}, f32[88,128]{1,0:T(8,128)S(1)}, f32[82,32,128]{2,1,0:T(8,128)}, f32[256,128]...) custom-call(bf16[2,58,32,168]{3,2,1,0:T(8,128)(2,1)} %bitcast.8, ...), custom_call_target="tpu_custom_call" | custom-call | tf_op jit(solution)/shard_map/prepare/pallas_call | solution.py:963
  13.8 4.8 %all-to-all-done.received_ref = f32[8,53,128]{2,1,0:T(8,128)S(1)} async-done(((f32[8,53,128]{2,1,0:T(8,128)}), f32[8,53,128]{2,1,0:T(8,128)S(1)}, u32[]{:S(2)}, u32[]{:S(2)}) %all-to-all-start) | async-done | bytes 217120 | tf_op jit(solution)/shard_map/all_to_all | solution.py:1011
  18.6 0.0 collective-permute-start
  18.6 0.6 %arrive.1 = (f32[128,256]{1,0:T(8,128)S(1)}, bf16[192,256]{1,0:T(8,128)(2,1)S(1)}) custom-call(f32[8,53,128]{2,1,0:T(8,128)S(1)} %all-to-all-done.received_ref, f32[128,128]{1,0:T(8,128)S(1)} %get-tuple-element.30.fold_ref), custom_call_target="tpu_custom_call" | custom-call | tf_op jit(solution)/shard_map/arrive/pallas_call | solution.py:963
  19.2 0.9 %collective-permute-done.other_ref = f32[8,53,128]{2,1,0:T(8,128)S(1)} collective-permute-done((f32[8,53,128]{2,1,0:T(8,128)S(1)}, f32[8,53,128]{2,1,0:T(8,128)S(1)}, u32[]{:S(2)}, u32[]{:S(2)}) %collective-permute-start) | collective-permute-done | bytes 217120 | tf_op jit(solution)/shard_map/ppermute | solution.py:1060
  20.1 4.0 %water.1 = (f32[88,32,128]{2,1,0:T(8,128)}, f32[3,88,32,128]{3,2,1,0:T(8,128)}, f32[7,88,128]{2,1,0:T(8,128)}, f32[4,8,3,4,128]{4,3,2,1,0:T(4,128)}) custom-call(f32[128,256]{1,0:T(8,128)S(1)} %get-tuple-element.31.arrived_ref, bf16[192,256]{1,0:T(8,128)(2,1)S(1)} %get-tuple-element.32.places_ref, f32[8,53,128]{2,1,0:T(8,128)S(1)} %collective-permute-done.other_ref, ...), custom_call_target="tpu_custom_call" | custom-call | tf_op jit(solution)/shard_map/water/pallas_call | solution.py:963
  24.1 3.4 %all-to-all-start.1 = ((f32[32,3,4,128]{3,2,1,0:T(4,128)}), f32[32,3,4,128]{3,2,1,0:T(4,128)S(1)}, u32[]{:S(2)}, u32[]{:S(2)}) async-start(f32[32,3,4,128]{3,2,1,0:T(4,128)} %bitcast.10), calls=%async_computation.1 | async-start | bytes 393216 | tf_op jit(solution)/shard_map/all_to_all | solution.py:1112
  27.5 6.0 %energy.1 = (bf16[2,58,32,168]{3,2,1,0:T(8,128)(2,1)}, f32[256,128]{1,0:T(8,128)S(1)}, bf16[256,384]{1,0:T(8,128)(2,1)S(1)}) custom-call(bf16[2,58,32,168]{3,2,1,0:T(8,128)(2,1)} %bitcast.9, f32[82,32,128]{2,1,0:T(8,128)} %get-tuple-element.38.energy_far, f32[88,32,128]{2,1,0:T(8,128)} %get-tuple-element.39.water_far, ...), custom_call_target="tpu_custom_call" | custom-call | tf_op jit(solution)/shard_map/energy/pallas_call | solution.py:963
  33.6 2.2 %all-to-all-done.1.mine_ref = f32[32,3,4,128]{3,2,1,0:T(4,128)S(1)} async-done(((f32[32,3,4,128]{3,2,1,0:T(4,128)}), f32[32,3,4,128]{3,2,1,0:T(4,128)S(1)}, u32[]{:S(2)}, u32[]{:S(2)}) %all-to-all-start.1) | async-done | bytes 196640 | tf_op jit(solution)/shard_map/all_to_all | solution.py:1112
  35.8 0.3 nearly.1.mine_ref
  36.1 0.5 %collective-permute-start.1 = (f32[256,128]{1,0:T(8,128)S(1)}, f32[256,128]{1,0:T(8,128)S(1)}, u32[]{:S(2)}, u32[]{:S(2)}) collective-permute-start(f32[256,128]{1,0:T(8,128)S(1)} %nearly.1.mine_ref), channel_id=1, source_target_pairs={{0,8},{8,0},{16,24},{24,16},{1,9},{9,1},{17,25},{25,17},{2,10},{10... | collective-permute-start | bytes 393224 | tf_op jit(solution)/shard_map/ppermute | solution.py:1169
  36.6 1.0 %collective-permute-done.1.other_ref = f32[256,128]{1,0:T(8,128)S(1)} collective-permute-done((f32[256,128]{1,0:T(8,128)S(1)}, f32[256,128]{1,0:T(8,128)S(1)}, u32[]{:S(2)}, u32[]{:S(2)}) %collective-permute-start.1) | collective-permute-done | bytes 131104 | tf_op jit(solution)/shard_map/ppermute | solution.py:1169
  37.6 0.7 %final.1 = f32[256,128]{1,0:T(8,128)} custom-call(f32[256,128]{1,0:T(8,128)S(1)} %get-tuple-element.46.advanced_ref, f32[256,128]{1,0:T(8,128)S(1)} %nearly.1.mine_ref, f32[256,128]{1,0:T(8,128)S(1)} %collective-permute-done.1.other_ref), custom_call_target="tpu_custom_call" | custom-call | tf_op jit(solution)/shard_map/final/pallas_call | solution.py:963
Async XLA Ops:
  2.9 15.7 %all-to-all-start = ((f32[8,53,128]{2,1,0:T(8,128)}), f32[8,53,128]{2,1,0:T(8,128)S(1)}, u32[]{:S(2)}, u32[]{:S(2)}) async-start(f32[8,53,128]{2,1,0:T(8,128)} %get-tuple-element.26), calls=%async_computation | async-start | bytes 458752 | tf_op jit(solution)/shard_map/all_to_all | solution.py:1011
  18.6 1.5 %collective-permute-start = (f32[8,53,128]{2,1,0:T(8,128)S(1)}, f32[8,53,128]{2,1,0:T(8,128)S(1)}, u32[]{:S(2)}, u32[]{:S(2)}) collective-permute-start(f32[8,53,128]{2,1,0:T(8,128)S(1)} %all-to-all-done.received_ref), channel_id=1, source_target_pairs={{0,8},{8,0},{16,24},{24,16},{1,9},{9,1},{17,25},{25,17},{2,10},{10... | collective-permute-start | bytes 651272 | tf_op jit(solution)/shard_map/ppermute | solution.py:1060
  24.1 11.6 %all-to-all-start.1 = ((f32[32,3,4,128]{3,2,1,0:T(4,128)}), f32[32,3,4,128]{3,2,1,0:T(4,128)S(1)}, u32[]{:S(2)}, u32[]{:S(2)}) async-start(f32[32,3,4,128]{3,2,1,0:T(4,128)} %bitcast.10), calls=%async_computation.1 | async-start | bytes 393216 | tf_op jit(solution)/shard_map/all_to_all | solution.py:1112
  36.1 1.5 %collective-permute-start.1 = (f32[256,128]{1,0:T(8,128)S(1)}, f32[256,128]{1,0:T(8,128)S(1)}, u32[]{:S(2)}, u32[]{:S(2)}) collective-permute-start(f32[256,128]{1,0:T(8,128)S(1)} %nearly.1.mine_ref), channel_id=1, source_target_pairs={{0,8},{8,0},{16,24},{24,16},{1,9},{9,1},{17,25},{25,17},{2,10},{10... | collective-permute-start | bytes 393224 | tf_op jit(solution)/shard_map/ppermute | solution.py:1169
